TPU v7x, 32 devices: a whole 2x2x4 slice. The times are simulated.
32 devices in a mesh: groups: 2 (over y), ctx: 4 (over z), role: 2 (over x), seq: 2 (over core).
Axes of the slice: x: 2, y: 2, z: 4, core: 2. Of those that a mesh axis runs over, the one named last changes fastest.
Arguments:
- queries: bfloat16 [32, 128, 576], P(('groups', 'role', 'seq'), 'ctx'), parts along dimension 0, may hold values from -24 to 24
- cache: bfloat16 [16, 4096, 576], P(('groups', 'role', 'seq'), 'ctx'), parts along dimension 0, may hold values from -4 to 4
- lengths: int32 [16], P(('groups', 'role', 'seq')), parts along dimension 0, may hold values from 4 to 4096, as said below
- positions: int32 [32], P(('groups', 'role', 'seq')), parts along dimension 0, may hold values from 0 to 4098, as said below
- value_up_weight: bfloat16 [128, 512, 128], P('ctx', ('role', 'seq')), may hold values from -0.25 to 0.25
- out_proj: bfloat16 [16384, 7168], P('ctx', ('role', 'seq')), may hold values from -0.046875 to 0.046875
- residual: bfloat16 [32, 7168], P('groups', ('role', 'seq')), parts along dimension 0, may hold values from -4 to 4
- norm_gain: float32 [7168], P(('role', 'seq')), may hold values from 0.5 to 1.5
- gate_weight: bfloat16 [7168, 9216], P(('role', 'seq'), 'ctx'), may hold values from -0.0625 to 0.0625
- up_weight: bfloat16 [7168, 9216], P(('role', 'seq'), 'ctx'), may hold values from -0.0625 to 0.0625
- down_weight: bfloat16 [9216, 7168], P('ctx', ('role', 'seq')), may hold values from -0.0625 to 0.0625
Outputs:
- layer_out: bfloat16 [32, 7168], P(('groups', 'ctx'), ('role', 'seq')), parts along dimension 0
There are 2 independent parts, one for each index of `groups`. A program takes and returns all parts, laid end to end along the dimension named above; an argument that names none is the same for every part. Nothing has to cross between parts.
Inputs may be any that keep to these rules, and one draw needn't show every extreme that they name: `lengths`: every sequence has at least 4 cached positions, and in every draw some sequence has all 4096. positions[r] lies between lengths[r // 2] - 4 and lengths[r // 2] + 2.
All inputs are finite; a program needn't handle non-finite values.
Results may differ from a plain program's by a relative error of at most 0.013.
Values may be sent and summed in bfloat16 or wider, within the bound.
No kernel may reach another device: no remote copies, remote signals or barrier semaphores. Data moves between devices by JAX's collectives and lax.ppermute only.
A program may use at most 128 MiB of HBM per device.

v0:
```python
import functools

import jax
import jax.numpy as jnp
from jax import lax
from jax.experimental import pallas as pl
from jax.experimental.pallas import tpu as pltpu
from jax.sharding import PartitionSpec as P


LATENT = 512
MTP = 2
SCALE = 0.07216878364870323
EPSILON = 1e-06
DEAD = -1e30
STAT_ROWS = 16
LANES = 128
ATTEND_LIMIT = 8 << 20
KERNEL_LIMIT = 3 << 20


f32, bf16 = jnp.float32, jnp.bfloat16
IN_VMEM = pl.BlockSpec(memory_space=pltpu.VMEM)
IN_SMEM = pl.BlockSpec(memory_space=pltpu.SMEM)
IN_HBM = pl.BlockSpec(memory_space=pltpu.HBM)


def xor_permute(x, axis, mask):
    size = lax.axis_size(axis)
    return lax.ppermute(x, axis, [(i, i ^ mask) for i in range(size)])


def exchange(pieces, axis):
    got = {0: pieces[0]}
    for mask in reversed(range(1, len(pieces))):
        got[mask] = xor_permute(pieces[mask], axis, mask)
    return [got[mask] for mask in range(len(pieces))]


def call(body, outs, args, specs, scratch=(), limit=KERNEL_LIMIT, cost=None):
    flops, moved = cost or (0, 0)
    return pl.pallas_call(
        body,
        out_shape=outs,
        in_specs=specs,
        out_specs=jax.tree.map(lambda _: IN_VMEM, outs),
        scratch_shapes=list(scratch),
        compiler_params=pltpu.CompilerParams(vmem_limit_bytes=limit),
        cost_estimate=pl.CostEstimate(flops=flops, bytes_accessed=moved, transcendentals=0),
    )(*args)


def in_vmem(x):
    return pltpu.with_memory_space_constraint(x, pltpu.VMEM)


def three_parts(x):
    high = x.astype(bf16)
    rest = x - high.astype(f32)
    middle = rest.astype(bf16)
    return high, middle, (rest - middle.astype(f32)).astype(bf16)


def fetch(arrays, lengths=None, positions=None):
    count = len(arrays)
    tables = 0 if positions is None else 1
    rows = positions.shape[0] if tables else 0

    def body(*refs):
        sources, refs = refs[:count], refs[count:]
        scalars, refs = refs[: 2 * tables], refs[2 * tables :]
        targets, refs = refs[:count], refs[count:]
        done = refs[-1]
        copies = [
            pltpu.make_async_copy(source, target, done.at[i])
            for i, (source, target) in enumerate(zip(sources, targets))
        ]
        for copy in copies:
            copy.start()
        if tables:
            length_ref, position_ref = scalars
            row = lax.broadcasted_iota(jnp.int32, (rows, LANES), 0)
            seen = jnp.zeros((rows, LANES), jnp.int32)
            for r in range(rows):
                bound = jnp.minimum(length_ref[r // MTP], position_ref[r] + 1)
                seen = jnp.where(row == r, bound, seen)
            refs[0][...] = seen
        for copy in copies:
            copy.wait()

    moved = sum(2 * x.size * x.dtype.itemsize for x in arrays)
    return call(
        body,
        [pltpu.VMEM(x.shape, x.dtype) for x in arrays]
        + [pltpu.VMEM((rows, LANES), jnp.int32)] * tables,
        [pltpu.with_memory_space_constraint(x, pltpu.HBM) for x in arrays]
        + [lengths, positions] * tables,
        [IN_HBM] * count + [IN_SMEM] * (2 * tables),
        [pltpu.SemaphoreType.DMA((count,))],
        limit=1 << 20,
        cost=(0, moved),
    )


def attend(groups, cache, seen):
    count = len(groups)
    rows, heads, width = groups[0].shape
    seqs, _, context = cache.shape
    per_seq = MTP * heads
    per_group = rows * heads

    def body(*refs):
        query_refs = refs[:count]
        cache_ref, seen_ref = refs[count : count + 2]
        out_refs = refs[count + 2 :]
        offset = lax.axis_index("ctx") * context
        total = count * per_seq
        tops, sums = [[] for _ in range(count)], [[] for _ in range(count)]
        for n in range(seqs):
            queries = jnp.concatenate(
                [q[MTP * n : MTP * (n + 1)].reshape(per_seq, width) for q in query_refs], axis=0
            )
            scores = jnp.dot(queries, cache_ref[n], preferred_element_type=f32) * SCALE
            row = lax.broadcasted_iota(jnp.int32, (total, 1), 0)
            which = (row // heads) % MTP
            limit = jnp.full((total, 1), 0, jnp.int32)
            for t in range(MTP):
                r = MTP * n + t
                limit = jnp.where(which == t, seen_ref[r : r + 1, 0:1], limit)
            place = offset + lax.broadcasted_iota(jnp.int32, (total, context), 1)
            live = place < limit
            top = jnp.max(jnp.where(live, scores, DEAD), axis=1, keepdims=True)
            probs = jnp.exp(jnp.where(live, scores - top, DEAD)).astype(bf16)
            weight = jnp.sum(probs.astype(f32), axis=1, keepdims=True)
            out = lax.dot_general(
                probs, cache_ref[n, :LATENT, :], (((1,), (1,)), ((), ())), preferred_element_type=f32
            )
            for g in range(count):
                part = slice(g * per_seq, (g + 1) * per_seq)
                out_refs[g][n * per_seq : (n + 1) * per_seq, :] = out[part].astype(bf16)
                tops[g].append(top[part])
                sums[g].append(weight[part])
        lane = lax.broadcasted_iota(jnp.int32, (LANES, LANES), 1)
        for g in range(count):
            fill = [jnp.zeros((LANES - per_group, 1), f32)] if per_group < LANES else []
            top = jnp.concatenate(tops[g] + fill, axis=0)
            weight = jnp.concatenate(sums[g] + fill, axis=0)
            table = jnp.where(lane == 0, top, jnp.where(lane == 1, weight, 0.0)).T
            for i, part in enumerate(three_parts(table[:STAT_ROWS])):
                out_refs[g][per_group:, i * LANES : (i + 1) * LANES] = part
            out_refs[g][per_group:, 3 * LANES :] = jnp.zeros((STAT_ROWS, LATENT - 3 * LANES), bf16)

    shape = jax.ShapeDtypeStruct((per_group + STAT_ROWS, LATENT), bf16)
    flops = 2 * count * rows * heads * context * (width + LATENT)
    return call(
        body,
        [shape] * count,
        [*groups, in_vmem(cache), seen],
        [IN_VMEM] * (count + 2),
        limit=ATTEND_LIMIT,
        cost=(flops, 4 << 20),
    )


def join_and_project(parts, pieces, rows, heads, after):
    count, slices = len(parts), len(pieces)
    per_group = rows * heads
    _, depth, vdim = pieces[0].shape

    def body(*refs):
        part_refs, piece_refs = refs[:count], refs[count : count + slices]
        value_ref, attended = refs[count + slices + 1 :]
        me = lax.axis_index(("role", "seq"))
        tops, sums = [], []
        for ref in part_refs:
            table = sum(
                ref[per_group:, i * LANES : (i + 1) * LANES].astype(f32) for i in reversed(range(3))
            )
            table = jnp.concatenate([table, jnp.zeros((LANES - STAT_ROWS, LANES), f32)], axis=0).T
            tops.append(table[:per_group, 0:1])
            sums.append(table[:per_group, 1:2])
        highest = functools.reduce(jnp.maximum, tops)
        factors = [jnp.exp(top - highest) for top in tops]
        denom = sum(f * s for f, s in zip(factors, sums))
        numer = sum(f * ref[:per_group, :].astype(f32) for f, ref in zip(factors, part_refs))
        joined = (numer / denom).astype(bf16).astype(f32)
        for k in range(slices):
            attended[k] = joined[:, k * depth : (k + 1) * depth]
        for h in range(heads):
            total = None
            for m in range(slices):
                left = attended[me ^ m, pl.ds(h, rows, stride=heads), :].astype(bf16)
                term = jnp.dot(left, piece_refs[m][h], preferred_element_type=f32)
                total = term if total is None else total + term
            value_ref[:, h * vdim : (h + 1) * vdim] = total.astype(bf16)

    return call(
        body,
        jax.ShapeDtypeStruct((rows, heads * vdim), bf16),
        [*parts, *[in_vmem(piece) for piece in pieces], after],
        [IN_VMEM] * (count + slices + 1),
        [pltpu.VMEM((slices, per_group, depth), f32)],
        cost=(2 * rows * heads * LATENT * vdim, 4 << 20),
    )


def project_out(pieces, weight):
    count = len(pieces)
    rows, depth = pieces[0].shape
    width = weight.shape[1]

    def body(*refs):
        weight_ref, out_ref, placed = refs[count:]
        me = lax.axis_index(("role", "seq"))
        for m in range(count):
            placed[me ^ m] = refs[m][...].astype(f32)
        values = jnp.concatenate([placed[k] for k in range(count)], axis=0).astype(bf16)
        out_ref[...] = jnp.dot(values, weight_ref[...], preferred_element_type=f32).astype(bf16)

    return call(
        body,
        jax.ShapeDtypeStruct((count * rows, width), bf16),
        [*pieces, in_vmem(weight)],
        [IN_VMEM] * (count + 1),
        [pltpu.VMEM((count, rows, depth), f32)],
        cost=(2 * count * rows * depth * width, 4 << 20),
    )


def gate_and_up(pieces, residual, gain, gate_weight, up_weight):
    count = len(pieces)
    rows, width = residual.shape
    hidden = gate_weight.shape[1]
    cores = lax.axis_size("seq")
    half = hidden // cores
    own_rows = rows // count

    def body(*refs):
        residual_ref, gain_ref, gate_ref, up_ref, keep_ref, send_ref, base_ref, split, placed = refs[count:]
        resid = residual_ref[...].astype(f32) + sum(ref[...].astype(f32) for ref in refs[:count])
        for k in range(count):
            placed[k] = resid[k * own_rows : (k + 1) * own_rows]
        base_ref[...] = placed[lax.axis_index("ctx")]
        squares = jnp.sum(resid * resid, axis=1, keepdims=True)
        scaled = (resid * gain_ref[...]).astype(bf16)
        gate = jnp.dot(scaled, gate_ref[...], preferred_element_type=f32)
        up = jnp.dot(scaled, up_ref[...], preferred_element_type=f32)
        for k in range(cores):
            split[k, :, :half] = gate[:, k * half : (k + 1) * half]
            split[k, :, half:] = up[:, k * half : (k + 1) * half]
        me = lax.axis_index("seq")
        keep_ref[:, : 2 * half] = split[me]
        send_ref[:, : 2 * half] = split[me ^ 1].astype(bf16)
        keep_ref[:, 2 * half :] = jnp.broadcast_to(squares, (rows, LANES))
        lane = lax.broadcasted_iota(jnp.int32, (rows, LANES), 1)
        send_ref[:, 2 * half :] = spread(squares, lane)

    shape = (rows, 2 * half + LANES)
    return call(
        body,
        [
            jax.ShapeDtypeStruct(shape, f32),
            jax.ShapeDtypeStruct(shape, bf16),
            jax.ShapeDtypeStruct((own_rows, width), f32),
        ],
        [*pieces, residual, gain, in_vmem(gate_weight), in_vmem(up_weight)],
        [IN_VMEM] * (count + 4),
        [pltpu.VMEM((cores, rows, 2 * half), f32), pltpu.VMEM((count, own_rows, width), f32)],
        cost=(4 * rows * width * hidden, 4 << 20),
    )


def spread(column, lane):
    high, middle, low = three_parts(column)
    return jnp.where(
        lane == 0,
        high.astype(f32),
        jnp.where(lane == 1, middle.astype(f32), jnp.where(lane == 2, low.astype(f32), 0.0)),
    ).astype(bf16)


def add_core(keep, got):
    rows, width = keep.shape
    body_width = width - LANES

    def body(keep_ref, got_ref, sum_ref, send_ref):
        total = keep_ref[:, :body_width] + got_ref[:, :body_width].astype(f32)
        squares = keep_ref[:, body_width : body_width + 1] + jnp.sum(
            got_ref[:, body_width:].astype(f32), axis=1, keepdims=True
        )
        sum_ref[:, :body_width] = total
        sum_ref[:, body_width:] = jnp.broadcast_to(squares, (rows, LANES))
        send_ref[:, :body_width] = total.astype(bf16)
        lane = lax.broadcasted_iota(jnp.int32, (rows, LANES), 1)
        send_ref[:, body_width:] = spread(squares, lane)

    return call(
        body,
        [jax.ShapeDtypeStruct((rows, width), f32), jax.ShapeDtypeStruct((rows, width), bf16)],
        [keep, got],
        [IN_VMEM] * 2,
        cost=(rows * width, rows * width * 8),
    )


def activate(keep, pieces, features):
    rows, width = keep.shape
    body_width = width - LANES
    half = body_width // 2

    def body(*refs):
        keep_ref, out_ref = refs[0], refs[-1]
        total = keep_ref[:, :body_width] + sum(r[:, :body_width].astype(f32) for r in refs[1:-1])
        squares = keep_ref[:, body_width : body_width + 1] + sum(
            jnp.sum(r[:, body_width:].astype(f32), axis=1, keepdims=True) for r in refs[1:-1]
        )
        scale = lax.rsqrt(squares / features + EPSILON)
        gate = total[:, :half] * scale
        up = total[:, half:] * scale
        out_ref[...] = (gate / (1.0 + jnp.exp(-gate)) * up).astype(bf16)

    return call(
        body,
        jax.ShapeDtypeStruct((rows, half), bf16),
        [keep, *pieces],
        [IN_VMEM] * (1 + len(pieces)),
        cost=(rows * width, rows * width * 8),
    )


def project_down(own, other, weight):
    rows, half = own.shape
    width = weight.shape[1]
    count = lax.axis_size("ctx")
    own_rows = rows // count

    def body(own_ref, other_ref, weight_ref, *refs):
        out_refs, (joined, placed) = refs[:count], refs[count:]
        core = lax.axis_index("seq")
        joined[core] = own_ref[...]
        joined[core ^ 1] = other_ref[...]
        hidden = jnp.concatenate([joined[0], joined[1]], axis=1)
        out = jnp.dot(hidden, weight_ref[...], preferred_element_type=f32)
        for k in range(count):
            placed[k] = out[k * own_rows : (k + 1) * own_rows]
        me = lax.axis_index("ctx")
        for m in range(count):
            out_refs[m][...] = placed[me ^ m].astype(bf16)

    return call(
        body,
        [jax.ShapeDtypeStruct((own_rows, width), bf16)] * count,
        [own, other, in_vmem(weight)],
        [IN_VMEM] * 3,
        [pltpu.VMEM((2, rows, half), bf16), pltpu.VMEM((count, own_rows, width), f32)],
        cost=(4 * rows * half * width, 4 << 20),
    )


def finish(base, pieces):
    def body(*refs):
        refs[-1][...] = (refs[0][...] + sum(r[...].astype(f32) for r in refs[1:-1])).astype(bf16)

    return call(
        body,
        jax.ShapeDtypeStruct(base.shape, bf16),
        [base, *pieces],
        [IN_VMEM] * (1 + len(pieces)),
        cost=(base.size, base.size * 8),
    )


def per_device(
    queries,
    cache,
    lengths,
    positions,
    value_up_weight,
    out_proj,
    residual,
    norm_gain,
    gate_weight,
    up_weight,
    down_weight,
):
    rows, heads, _ = queries.shape
    blocks = lax.axis_size("ctx")
    roles = lax.axis_size("role")
    members = lax.axis_size(("role", "seq"))

    groups = exchange([queries] * blocks, "ctx")
    along = exchange([value_up_weight] * roles, "role")

    own_queries, cache_fast, up_own, out_fast, seen = fetch(
        [queries, jnp.swapaxes(cache, 1, 2), value_up_weight, out_proj], lengths, positions
    )
    partial = list(attend([own_queries, *groups[1:]], cache_fast, seen))

    gate_weight, up_weight, down_weight, partial[0] = lax.optimization_barrier(
        (gate_weight, up_weight, down_weight, partial[0])
    )
    parts = exchange(partial, "ctx")
    gate_fast, up_fast, down_fast, residual, gain = fetch(
        [gate_weight, up_weight, down_weight, residual, norm_gain.reshape(1, -1)]
    )
    *along, gain = lax.optimization_barrier((*along, gain))
    across = [xor_permute(piece, "seq", 1) for piece in along]
    up_pieces = [up_own, *[piece for pair in zip(along, across) for piece in pair][1:]]
    values = join_and_project(parts, up_pieces, rows, heads, gain)
    shared = exchange([values] * members, ("role", "seq"))
    terms = exchange([project_out(shared, out_fast)] * blocks, "ctx")
    keep, send, base = gate_and_up(terms, residual, gain, gate_fast, up_fast)
    keep, send = add_core(keep, xor_permute(send, "seq", 1))
    pieces = exchange([send] * roles, "role")[1:]
    features = norm_gain.shape[0] * members
    hidden = activate(keep, pieces, features)
    last = project_down(hidden, xor_permute(hidden, "seq", 1), down_fast)
    last = exchange(last, "ctx")
    return finish(base, last)


def solution(mesh):
    placed = (
        P(("groups", "role", "seq"), "ctx", None),
        P(("groups", "role", "seq"), "ctx", None),
        P(("groups", "role", "seq")),
        P(("groups", "role", "seq")),
        P("ctx", ("role", "seq"), None),
        P("ctx", ("role", "seq")),
        P("groups", ("role", "seq")),
        P(("role", "seq")),
        P(("role", "seq"), "ctx"),
        P(("role", "seq"), "ctx"),
        P("ctx", ("role", "seq")),
    )

    return jax.shard_map(
        per_device,
        mesh=mesh,
        in_specs=placed,
        out_specs=P(("groups", "ctx"), ("role", "seq")),
        check_vma=False,
    )
```

profile of v0, /device:TPU:0, one launch (start us, length us, event | category | flops | bytes accessed | tf_op | source)
XLA Modules:
  0.0 84.1 jit_solution(3146621897239750619)
XLA Ops:
  0.0 3.0 %collective-permute-start.6 = (bf16[32,128,128]{2,1,0:T(8,128)(2,1)}, bf16[32,128,128]{2,1,0:T(8,128)(2,1)S(1)}, u32[]{:S(2)}, u32[]{:S(2)}) collective-permute-start(bf16[32,128,128]{2,1,0:T(8,128)(2,1)} %refs_2_.1), channel_id=1, source_target_pairs={{0,2},{2,0},{1,3},{3,1},{4,6},{6,4},{5,7},{7,5},{8,10},{10,8},{9,1... | collective-permute-start | bytes 3145736 | tf_op jit(solution)/shard_map/ppermute | solution.py:30
  3.0 1.6 %collective-permute-start = (bf16[4,32,576]{2,1,0:T(8,128)(2,1)}, bf16[4,32,576]{2,1,0:T(8,128)(2,1)S(1)}, u32[]{:S(2)}, u32[]{:S(2)}) collective-permute-start(bf16[4,32,576]{2,1,0:T(8,128)(2,1)} %refs_0_.1), channel_id=1, source_target_pairs={{0,4},{4,0},{8,12},{12,8},{1,5},{5,1},{9,13},{13,9},{2,6},{6,2},{1... | collective-permute-start | bytes 442376 | tf_op jit(solution)/shard_map/ppermute | solution.py:30
  4.5 2.5 %collective-permute-start.2 = (bf16[4,32,576]{2,1,0:T(8,128)(2,1)}, bf16[4,32,576]{2,1,0:T(8,128)(2,1)S(1)}, u32[]{:S(2)}, u32[]{:S(2)}) collective-permute-start(bf16[4,32,576]{2,1,0:T(8,128)(2,1)} %refs_0_.1), channel_id=1, source_target_pairs={{0,12},{4,8},{8,4},{12,0},{1,13},{5,9},{9,5},{13,1},{2,14},{6,10},... | collective-permute-start | bytes 442376 | tf_op jit(solution)/shard_map/ppermute | solution.py:30
  7.0 0.1 collective-permute-start.1
  7.1 1.3 %reshape.3.refs_4_ = f32[1,1792]{1,0:T(1,128)} reshape(f32[1792]{0:T(1024)} %param.18) | data formatting | bytes 14336 | tf_op jit(solution)/shard_map/reshape | solution.py:404
  8.4 0.0 copy-start
  8.4 0.7 copy-done
  9.1 0.0 copy-start.1
  9.1 0.7 copy-done.1
  9.7 6.9 %shard_map.109 = (bf16[4,32,576]{2,1,0:T(8,128)(2,1)S(1)}, bf16[2,576,1024]{2,1,0:T(8,128)(2,1)S(1)}, bf16[32,128,128]{2,1,0:T(8,128)(2,1)S(1)}, bf16[4096,1792]{1,0:T(8,128)(2,1)S(1)}, s32[4,128]{1,0:T(4,128)S(1)}) custom-call(bf16[4,32,576]{2,1,0:T(8,128)(2,1)} %refs_0_.1, bf16[2,576,1024]{2,1,0:T(8,128)(2,1)} %bitcast.1, bf16[32,128,128]{2,1,0:T(8,128)(2,1)} %refs_2_.1, ...), custom_call_target="tpu_custom_call" | custom-call | bytes 36470784 | tf_op jit(solution)/shard_map/pallas_call | solution.py:42
  16.6 0.0 collective-permute-done.refs_1_
  16.6 0.0 collective-permute-done.2.refs_3_
  16.6 4.9 %collective-permute-done.1.refs_2_ = bf16[4,32,576]{2,1,0:T(8,128)(2,1)S(1)} collective-permute-done((bf16[4,32,576]{2,1,0:T(8,128)(2,1)}, bf16[4,32,576]{2,1,0:T(8,128)(2,1)S(1)}, u32[]{:S(2)}, u32[]{:S(2)}) %collective-permute-start.1) | collective-permute-done | bytes 147488 | tf_op jit(solution)/shard_map/ppermute | solution.py:30
  21.5 2.3 %shard_map.110 = (bf16[144,512]{1,0:T(8,128)(2,1)S(1)}, bf16[144,512]{1,0:T(8,128)(2,1)S(1)}, bf16[144,512]{1,0:T(8,128)(2,1)S(1)}, bf16[144,512]{1,0:T(8,128)(2,1)S(1)}) custom-call(bf16[4,32,576]{2,1,0:T(8,128)(2,1)S(1)} %get-tuple-element.35.refs_0_, bf16[4,32,576]{2,1,0:T(8,128)(2,1)S(1)} %collective-permute-done.refs_1_, ...), custom_call_target="tpu_custom_call" | custom-call | flops 1140850688 | bytes 4194304 | tf_op jit(solution)/shard_map/pallas_call | solution.py:42
  23.9 0.0 copy-start.2
  23.9 8.3 %shard_map.111 = (bf16[1792,2304]{1,0:T(8,128)(2,1)S(1)}, bf16[1792,2304]{1,0:T(8,128)(2,1)S(1)}, bf16[2304,1792]{1,0:T(8,128)(2,1)S(1)}, bf16[16,1792]{1,0:T(8,128)(2,1)S(1)}, f32[1,1792]{1,0:T(1,128)S(1)}) custom-call(bf16[1792,2304]{1,0:T(8,128)(2,1)} %refs_0_.2, bf16[1792,2304]{1,0:T(8,128)(2,1)} %refs_1_, bf16[2304,1792]{1,0:T(8,128)(2,1)} %refs_2_.2, ...), custom_call_target="tpu_custom_call" | custom-call | bytes 49674240 | tf_op jit(solution)/shard_map/pallas_call | solution.py:42
  32.2 0.0 collective-permute-done.6.refs_6_
  32.2 0.0 copy-done.2
  32.2 0.1 collective-permute-start.7
  32.3 0.5 collective-permute-start.8
  32.8 0.0 collective-permute-start.3
  32.8 3.2 %collective-permute-start.4 = (bf16[144,512]{1,0:T(8,128)(2,1)S(1)}, bf16[144,512]{1,0:T(8,128)(2,1)S(1)}, u32[]{:S(2)}, u32[]{:S(2)}) collective-permute-start(bf16[144,512]{1,0:T(8,128)(2,1)S(1)} %get-tuple-element.41), channel_id=1, source_target_pairs={{0,8},{4,12},{8,0},{12,4},{1,9},{5,13},{9,1},{13,5},{2,10},{6,14},... | collective-permute-start | bytes 442376 | tf_op jit(solution)/shard_map/ppermute | solution.py:30
  35.9 1.2 %collective-permute-start.5 = (bf16[144,512]{1,0:T(8,128)(2,1)S(1)}, bf16[144,512]{1,0:T(8,128)(2,1)S(1)}, u32[]{:S(2)}, u32[]{:S(2)}) collective-permute-start(bf16[144,512]{1,0:T(8,128)(2,1)S(1)} %get-tuple-element.42), channel_id=1, source_target_pairs={{0,12},{4,8},{8,4},{12,0},{1,13},{5,9},{9,5},{13,1},{2,14},{6,10},... | collective-permute-start | bytes 442376 | tf_op jit(solution)/shard_map/ppermute | solution.py:30
  37.2 4.0 %collective-permute-done.3.refs_1_ = bf16[144,512]{1,0:T(8,128)(2,1)S(1)} collective-permute-done((bf16[144,512]{1,0:T(8,128)(2,1)S(1)}, bf16[144,512]{1,0:T(8,128)(2,1)S(1)}, u32[]{:S(2)}, u32[]{:S(2)}) %collective-permute-start.3) | collective-permute-done | bytes 147488 | tf_op jit(solution)/shard_map/ppermute | solution.py:30
  41.2 5.8 %collective-permute-done.4.refs_2_ = bf16[144,512]{1,0:T(8,128)(2,1)S(1)} collective-permute-done((bf16[144,512]{1,0:T(8,128)(2,1)S(1)}, bf16[144,512]{1,0:T(8,128)(2,1)S(1)}, u32[]{:S(2)}, u32[]{:S(2)}) %collective-permute-start.4) | collective-permute-done | bytes 147488 | tf_op jit(solution)/shard_map/ppermute | solution.py:30
  47.0 0.0 collective-permute-done.5.refs_3_
  47.0 0.0 collective-permute-done.7.refs_5_
  47.0 0.0 collective-permute-done.8.refs_7_
  47.0 1.6 %shard_map.112.refs_0_ = bf16[4,4096]{1,0:T(4,128)(2,1)S(1)} custom-call(bf16[144,512]{1,0:T(8,128)(2,1)S(1)} %get-tuple-element.39.refs_0_, bf16[144,512]{1,0:T(8,128)(2,1)S(1)} %collective-permute-done.3.refs_1_, bf16[144,512]{1,0:T(8,128)(2,1)S(1)} %collective-permute-done.4.refs_2_, bf16[144,512]{1,0:T(8,128)(2,1)S(1)} %collective-permute-done.5.refs_3_, ...), custom_call_target="tpu_custom_call" | custom-call | flops 16777216 | bytes 4194304 | tf_op jit(solution)/shard_map/pallas_call | solution.py:42
  48.7 0.0 collective-permute-start.11
  48.7 0.6 collective-permute-start.10
  49.2 1.3 %collective-permute-start.9 = (bf16[4,4096]{1,0:T(4,128)(2,1)S(1)}, bf16[4,4096]{1,0:T(4,128)(2,1)S(1)}, u32[]{:S(2)}, u32[]{:S(2)}) collective-permute-start(bf16[4,4096]{1,0:T(4,128)(2,1)S(1)} %shard_map.112.refs_0_), channel_id=1, source_target_pairs={{0,1},{1,0},{2,3},{3,2},{4,5},{5,4},{6,7},{7,6},{8,9},{9,8},{10,11... | collective-permute-start | bytes 98312 | tf_op jit(solution)/shard_map/ppermute | solution.py:30
  50.5 1.5 %collective-permute-done.11.refs_3_ = bf16[4,4096]{1,0:T(4,128)(2,1)S(1)} collective-permute-done((bf16[4,4096]{1,0:T(4,128)(2,1)S(1)}, bf16[4,4096]{1,0:T(4,128)(2,1)S(1)}, u32[]{:S(2)}, u32[]{:S(2)}) %collective-permute-start.11) | collective-permute-done | bytes 32800 | tf_op jit(solution)/shard_map/ppermute | solution.py:30
  52.0 0.7 collective-permute-done.10.refs_2_
  52.7 0.0 collective-permute-done.9.refs_1_
  52.7 2.0 %shard_map.113.refs_0_ = bf16[16,1792]{1,0:T(8,128)(2,1)S(1)} custom-call(bf16[4,4096]{1,0:T(4,128)(2,1)S(1)} %shard_map.112.refs_0_, bf16[4,4096]{1,0:T(4,128)(2,1)S(1)} %collective-permute-done.9.refs_1_, bf16[4,4096]{1,0:T(4,128)(2,1)S(1)} %collective-permute-done.10.refs_2_, bf16[4,4096]{1,0:T(4,128)(2,1)S(1)} %collective-permute-done.11.refs_3_, ...), custom_call_target="tpu_custom_call" | custom-call | flops 234881024 | bytes 4194304 | tf_op jit(solution)/shard_map/pallas_call | solution.py:42
  54.7 2.4 %collective-permute-start.14 = (bf16[16,1792]{1,0:T(8,128)(2,1)S(1)}, bf16[16,1792]{1,0:T(8,128)(2,1)S(1)}, u32[]{:S(2)}, u32[]{:S(2)}) collective-permute-start(bf16[16,1792]{1,0:T(8,128)(2,1)S(1)} %shard_map.113.refs_0_), channel_id=1, source_target_pairs={{0,12},{4,8},{8,4},{12,0},{1,13},{5,9},{9,5},{13,1},{2,14},{6,10},... | collective-permute-start | bytes 172040 | tf_op jit(solution)/shard_map/ppermute | solution.py:30
  57.1 1.9 %collective-permute-start.13 = (bf16[16,1792]{1,0:T(8,128)(2,1)S(1)}, bf16[16,1792]{1,0:T(8,128)(2,1)S(1)}, u32[]{:S(2)}, u32[]{:S(2)}) collective-permute-start(bf16[16,1792]{1,0:T(8,128)(2,1)S(1)} %shard_map.113.refs_0_), channel_id=1, source_target_pairs={{0,8},{4,12},{8,0},{12,4},{1,9},{5,13},{9,1},{13,5},{2,10},{6,14},... | collective-permute-start | bytes 172040 | tf_op jit(solution)/shard_map/ppermute | solution.py:30
  59.0 0.1 collective-permute-start.12
  59.1 1.7 %collective-permute-done.14.refs_3_ = bf16[16,1792]{1,0:T(8,128)(2,1)S(1)} collective-permute-done((bf16[16,1792]{1,0:T(8,128)(2,1)S(1)}, bf16[16,1792]{1,0:T(8,128)(2,1)S(1)}, u32[]{:S(2)}, u32[]{:S(2)}) %collective-permute-start.14) | collective-permute-done | bytes 57376 | tf_op jit(solution)/shard_map/ppermute | solution.py:30
  60.8 3.1 %collective-permute-done.13.refs_2_ = bf16[16,1792]{1,0:T(8,128)(2,1)S(1)} collective-permute-done((bf16[16,1792]{1,0:T(8,128)(2,1)S(1)}, bf16[16,1792]{1,0:T(8,128)(2,1)S(1)}, u32[]{:S(2)}, u32[]{:S(2)}) %collective-permute-start.13) | collective-permute-done | bytes 57376 | tf_op jit(solution)/shard_map/ppermute | solution.py:30
  63.9 0.0 collective-permute-done.12.refs_1_
  63.9 2.3 %shard_map.114 = (f32[16,2432]{1,0:T(8,128)S(1)}, bf16[16,2432]{1,0:T(8,128)(2,1)S(1)}, f32[4,1792]{1,0:T(4,128)S(1)}) custom-call(bf16[16,1792]{1,0:T(8,128)(2,1)S(1)} %shard_map.113.refs_0_, bf16[16,1792]{1,0:T(8,128)(2,1)S(1)} %collective-permute-done.12.refs_1_, bf16[16,1792]{1,0:T(8,128)(2,1)S(1)} %collective-permute-done.13.refs_2_, ...), custom_call_target="tpu_custom_call" | custom-call | flops 264241152 | bytes 4194304 | tf_op jit(solution)/shard_map/pallas_call | solution.py:42
  66.2 0.1 collective-permute-start.15
  66.3 1.3 %collective-permute-done.15.got_ref = bf16[16,2432]{1,0:T(8,128)(2,1)S(1)} collective-permute-done((bf16[16,2432]{1,0:T(8,128)(2,1)S(1)}, bf16[16,2432]{1,0:T(8,128)(2,1)S(1)}, u32[]{:S(2)}, u32[]{:S(2)}) %collective-permute-start.15) | collective-permute-done | bytes 77856 | tf_op jit(solution)/shard_map/ppermute | solution.py:30
  67.5 0.2 shard_map.115
  67.7 1.0 %collective-permute-start.16 = (bf16[16,2432]{1,0:T(8,128)(2,1)S(1)}, bf16[16,2432]{1,0:T(8,128)(2,1)S(1)}, u32[]{:S(2)}, u32[]{:S(2)}) collective-permute-start(bf16[16,2432]{1,0:T(8,128)(2,1)S(1)} %get-tuple-element.59), channel_id=1, source_target_pairs={{0,2},{2,0},{1,3},{3,1},{4,6},{6,4},{5,7},{7,5},{8,10},{10,8},{9,1... | collective-permute-start | bytes 233480 | tf_op jit(solution)/shard_map/ppermute | solution.py:30
  68.7 3.4 %collective-permute-done.16.refs_1_ = bf16[16,2432]{1,0:T(8,128)(2,1)S(1)} collective-permute-done((bf16[16,2432]{1,0:T(8,128)(2,1)S(1)}, bf16[16,2432]{1,0:T(8,128)(2,1)S(1)}, u32[]{:S(2)}, u32[]{:S(2)}) %collective-permute-start.16) | collective-permute-done | bytes 77856 | tf_op jit(solution)/shard_map/ppermute | solution.py:30
  72.1 0.2 shard_map.116.own_ref
  72.3 0.1 collective-permute-start.17
  72.4 1.2 %collective-permute-done.17.other_ref = bf16[16,1152]{1,0:T(8,128)(2,1)S(1)} collective-permute-done((bf16[16,1152]{1,0:T(8,128)(2,1)S(1)}, bf16[16,1152]{1,0:T(8,128)(2,1)S(1)}, u32[]{:S(2)}, u32[]{:S(2)}) %collective-permute-start.17) | collective-permute-done | bytes 36896 | tf_op jit(solution)/shard_map/ppermute | solution.py:30
  73.6 1.2 %shard_map.117 = (bf16[4,1792]{1,0:T(4,128)(2,1)S(1)}, bf16[4,1792]{1,0:T(4,128)(2,1)S(1)}, bf16[4,1792]{1,0:T(4,128)(2,1)S(1)}, bf16[4,1792]{1,0:T(4,128)(2,1)S(1)}) custom-call(bf16[16,1152]{1,0:T(8,128)(2,1)S(1)} %shard_map.116.own_ref, bf16[16,1152]{1,0:T(8,128)(2,1)S(1)} %collective-permute-done.17.other_ref, ...), custom_call_target="tpu_custom_call" | custom-call | flops 132120576 | bytes 4194304 | tf_op jit(solution)/shard_map/pallas_call | solution.py:42
  74.8 0.4 collective-permute-start.18
  75.2 2.8 %collective-permute-start.19 = (bf16[4,1792]{1,0:T(4,128)(2,1)S(1)}, bf16[4,1792]{1,0:T(4,128)(2,1)S(1)}, u32[]{:S(2)}, u32[]{:S(2)}) collective-permute-start(bf16[4,1792]{1,0:T(4,128)(2,1)S(1)} %get-tuple-element.63), channel_id=1, source_target_pairs={{0,8},{4,12},{8,0},{12,4},{1,9},{5,13},{9,1},{13,5},{2,10},{6,14},... | collective-permute-start | bytes 43016 | tf_op jit(solution)/shard_map/ppermute | solution.py:30
  78.0 1.3 %collective-permute-start.20 = (bf16[4,1792]{1,0:T(4,128)(2,1)S(1)}, bf16[4,1792]{1,0:T(4,128)(2,1)S(1)}, u32[]{:S(2)}, u32[]{:S(2)}) collective-permute-start(bf16[4,1792]{1,0:T(4,128)(2,1)S(1)} %get-tuple-element.64), channel_id=1, source_target_pairs={{0,12},{4,8},{8,4},{12,0},{1,13},{5,9},{9,5},{13,1},{2,14},{6,10},... | collective-permute-start | bytes 43016 | tf_op jit(solution)/shard_map/ppermute | solution.py:30
  79.3 0.0 collective-permute-done.18.refs_2_
  79.3 0.5 collective-permute-done.19.refs_3_
  79.8 3.7 %collective-permute-done.20.refs_4_ = bf16[4,1792]{1,0:T(4,128)(2,1)S(1)} collective-permute-done((bf16[4,1792]{1,0:T(4,128)(2,1)S(1)}, bf16[4,1792]{1,0:T(4,128)(2,1)S(1)}, u32[]{:S(2)}, u32[]{:S(2)}) %collective-permute-start.20) | collective-permute-done | bytes 14368 | tf_op jit(solution)/shard_map/ppermute | solution.py:30
  83.5 0.6 shard_map.118
Async XLA Ops:
  0.0 32.2 %collective-permute-start.6 = (bf16[32,128,128]{2,1,0:T(8,128)(2,1)}, bf16[32,128,128]{2,1,0:T(8,128)(2,1)S(1)}, u32[]{:S(2)}, u32[]{:S(2)}) collective-permute-start(bf16[32,128,128]{2,1,0:T(8,128)(2,1)} %refs_2_.1), channel_id=1, source_target_pairs={{0,2},{2,0},{1,3},{3,1},{4,6},{6,4},{5,7},{7,5},{8,10},{10,8},{9,1... | collective-permute-start | bytes 3145736 | tf_op jit(solution)/shard_map/ppermute | solution.py:30
  3.0 13.7 %collective-permute-start = (bf16[4,32,576]{2,1,0:T(8,128)(2,1)}, bf16[4,32,576]{2,1,0:T(8,128)(2,1)S(1)}, u32[]{:S(2)}, u32[]{:S(2)}) collective-permute-start(bf16[4,32,576]{2,1,0:T(8,128)(2,1)} %refs_0_.1), channel_id=1, source_target_pairs={{0,4},{4,0},{8,12},{12,8},{1,5},{5,1},{9,13},{13,9},{2,6},{6,2},{1... | collective-permute-start | bytes 442376 | tf_op jit(solution)/shard_map/ppermute | solution.py:30
  4.5 12.1 %collective-permute-start.2 = (bf16[4,32,576]{2,1,0:T(8,128)(2,1)}, bf16[4,32,576]{2,1,0:T(8,128)(2,1)S(1)}, u32[]{:S(2)}, u32[]{:S(2)}) collective-permute-start(bf16[4,32,576]{2,1,0:T(8,128)(2,1)} %refs_0_.1), channel_id=1, source_target_pairs={{0,12},{4,8},{8,4},{12,0},{1,13},{5,9},{9,5},{13,1},{2,14},{6,10},... | collective-permute-start | bytes 442376 | tf_op jit(solution)/shard_map/ppermute | solution.py:30
  7.0 14.5 %collective-permute-start.1 = (bf16[4,32,576]{2,1,0:T(8,128)(2,1)}, bf16[4,32,576]{2,1,0:T(8,128)(2,1)S(1)}, u32[]{:S(2)}, u32[]{:S(2)}) collective-permute-start(bf16[4,32,576]{2,1,0:T(8,128)(2,1)} %refs_0_.1), channel_id=1, source_target_pairs={{0,8},{4,12},{8,0},{12,4},{1,9},{5,13},{9,1},{13,5},{2,10},{6,14},... | collective-permute-start | bytes 442376 | tf_op jit(solution)/shard_map/ppermute | solution.py:30
  8.4 0.7 copy-start
  9.1 0.7 copy-start.1
  23.9 8.3 %copy-start.2 = (bf16[32,128,128]{2,1,0:T(8,128)(2,1)S(1)}, bf16[32,128,128]{2,1,0:T(8,128)(2,1)}, u32[]{:S(2)}) copy-start(bf16[32,128,128]{2,1,0:T(8,128)(2,1)} %refs_2_.1) | copy-start | bytes 3145732
  32.2 14.8 %collective-permute-start.7 = (bf16[32,128,128]{2,1,0:T(8,128)(2,1)S(1)}, bf16[32,128,128]{2,1,0:T(8,128)(2,1)S(1)}, u32[]{:S(2)}, u32[]{:S(2)}) collective-permute-start(bf16[32,128,128]{2,1,0:T(8,128)(2,1)S(1)} %copy-done.2), channel_id=1, source_target_pairs={{0,1},{1,0},{2,3},{3,2},{4,5},{5,4},{6,7},{7,6},{8,9},{9,8},{10,11... | collective-permute-start | bytes 3145736 | tf_op jit(solution)/shard_map/ppermute | solution.py:30
  32.3 14.7 %collective-permute-start.8 = (bf16[32,128,128]{2,1,0:T(8,128)(2,1)S(1)}, bf16[32,128,128]{2,1,0:T(8,128)(2,1)S(1)}, u32[]{:S(2)}, u32[]{:S(2)}) collective-permute-start(bf16[32,128,128]{2,1,0:T(8,128)(2,1)S(1)} %collective-permute-done.6.refs_6_), channel_id=1, source_target_pairs={{0,1},{1,0},{2,3},{3,2},{4,5},{5,4},{6,7},{7,6},{8,9},{9,8},{10,11... | collective-permute-start | bytes 3145736 | tf_op jit(solution)/shard_map/ppermute | solution.py:30
  32.8 8.4 %collective-permute-start.3 = (bf16[144,512]{1,0:T(8,128)(2,1)S(1)}, bf16[144,512]{1,0:T(8,128)(2,1)S(1)}, u32[]{:S(2)}, u32[]{:S(2)}) collective-permute-start(bf16[144,512]{1,0:T(8,128)(2,1)S(1)} %get-tuple-element.40), channel_id=1, source_target_pairs={{0,4},{4,0},{8,12},{12,8},{1,5},{5,1},{9,13},{13,9},{2,6},{6,2},{1... | collective-permute-start | bytes 442376 | tf_op jit(solution)/shard_map/ppermute | solution.py:30
  32.8 14.2 %collective-permute-start.4 = (bf16[144,512]{1,0:T(8,128)(2,1)S(1)}, bf16[144,512]{1,0:T(8,128)(2,1)S(1)}, u32[]{:S(2)}, u32[]{:S(2)}) collective-permute-start(bf16[144,512]{1,0:T(8,128)(2,1)S(1)} %get-tuple-element.41), channel_id=1, source_target_pairs={{0,8},{4,12},{8,0},{12,4},{1,9},{5,13},{9,1},{13,5},{2,10},{6,14},... | collective-permute-start | bytes 442376 | tf_op jit(solution)/shard_map/ppermute | solution.py:30
  35.9 11.1 %collective-permute-start.5 = (bf16[144,512]{1,0:T(8,128)(2,1)S(1)}, bf16[144,512]{1,0:T(8,128)(2,1)S(1)}, u32[]{:S(2)}, u32[]{:S(2)}) collective-permute-start(bf16[144,512]{1,0:T(8,128)(2,1)S(1)} %get-tuple-element.42), channel_id=1, source_target_pairs={{0,12},{4,8},{8,4},{12,0},{1,13},{5,9},{9,5},{13,1},{2,14},{6,10},... | collective-permute-start | bytes 442376 | tf_op jit(solution)/shard_map/ppermute | solution.py:30
  48.7 3.3 %collective-permute-start.11 = (bf16[4,4096]{1,0:T(4,128)(2,1)S(1)}, bf16[4,4096]{1,0:T(4,128)(2,1)S(1)}, u32[]{:S(2)}, u32[]{:S(2)}) collective-permute-start(bf16[4,4096]{1,0:T(4,128)(2,1)S(1)} %shard_map.112.refs_0_), channel_id=1, source_target_pairs={{0,3},{1,2},{2,1},{3,0},{4,7},{5,6},{6,5},{7,4},{8,11},{9,10},{10,... | collective-permute-start | bytes 98312 | tf_op jit(solution)/shard_map/ppermute | solution.py:30
  48.7 4.0 %collective-permute-start.10 = (bf16[4,4096]{1,0:T(4,128)(2,1)S(1)}, bf16[4,4096]{1,0:T(4,128)(2,1)S(1)}, u32[]{:S(2)}, u32[]{:S(2)}) collective-permute-start(bf16[4,4096]{1,0:T(4,128)(2,1)S(1)} %shard_map.112.refs_0_), channel_id=1, source_target_pairs={{0,2},{1,3},{2,0},{3,1},{4,6},{5,7},{6,4},{7,5},{8,10},{9,11},{10,... | collective-permute-start | bytes 98312 | tf_op jit(solution)/shard_map/ppermute | solution.py:30
  49.2 3.5 %collective-permute-start.9 = (bf16[4,4096]{1,0:T(4,128)(2,1)S(1)}, bf16[4,4096]{1,0:T(4,128)(2,1)S(1)}, u32[]{:S(2)}, u32[]{:S(2)}) collective-permute-start(bf16[4,4096]{1,0:T(4,128)(2,1)S(1)} %shard_map.112.refs_0_), channel_id=1, source_target_pairs={{0,1},{1,0},{2,3},{3,2},{4,5},{5,4},{6,7},{7,6},{8,9},{9,8},{10,11... | collective-permute-start | bytes 98312 | tf_op jit(solution)/shard_map/ppermute | solution.py:30
  54.7 6.1 %collective-permute-start.14 = (bf16[16,1792]{1,0:T(8,128)(2,1)S(1)}, bf16[16,1792]{1,0:T(8,128)(2,1)S(1)}, u32[]{:S(2)}, u32[]{:S(2)}) collective-permute-start(bf16[16,1792]{1,0:T(8,128)(2,1)S(1)} %shard_map.113.refs_0_), channel_id=1, source_target_pairs={{0,12},{4,8},{8,4},{12,0},{1,13},{5,9},{9,5},{13,1},{2,14},{6,10},... | collective-permute-start | bytes 172040 | tf_op jit(solution)/shard_map/ppermute | solution.py:30
  57.1 6.8 %collective-permute-start.13 = (bf16[16,1792]{1,0:T(8,128)(2,1)S(1)}, bf16[16,1792]{1,0:T(8,128)(2,1)S(1)}, u32[]{:S(2)}, u32[]{:S(2)}) collective-permute-start(bf16[16,1792]{1,0:T(8,128)(2,1)S(1)} %shard_map.113.refs_0_), channel_id=1, source_target_pairs={{0,8},{4,12},{8,0},{12,4},{1,9},{5,13},{9,1},{13,5},{2,10},{6,14},... | collective-permute-start | bytes 172040 | tf_op jit(solution)/shard_map/ppermute | solution.py:30
  59.0 4.9 %collective-permute-start.12 = (bf16[16,1792]{1,0:T(8,128)(2,1)S(1)}, bf16[16,1792]{1,0:T(8,128)(2,1)S(1)}, u32[]{:S(2)}, u32[]{:S(2)}) collective-permute-start(bf16[16,1792]{1,0:T(8,128)(2,1)S(1)} %shard_map.113.refs_0_), channel_id=1, source_target_pairs={{0,4},{4,0},{8,12},{12,8},{1,5},{5,1},{9,13},{13,9},{2,6},{6,2},{1... | collective-permute-start | bytes 172040 | tf_op jit(solution)/shard_map/ppermute | solution.py:30
  66.2 1.3 %collective-permute-start.15 = (bf16[16,2432]{1,0:T(8,128)(2,1)S(1)}, bf16[16,2432]{1,0:T(8,128)(2,1)S(1)}, u32[]{:S(2)}, u32[]{:S(2)}) collective-permute-start(bf16[16,2432]{1,0:T(8,128)(2,1)S(1)} %get-tuple-element.57), channel_id=1, source_target_pairs={{0,1},{1,0},{2,3},{3,2},{4,5},{5,4},{6,7},{7,6},{8,9},{9,8},{10,11... | collective-permute-start | bytes 233480 | tf_op jit(solution)/shard_map/ppermute | solution.py:30
  67.7 4.4 %collective-permute-start.16 = (bf16[16,2432]{1,0:T(8,128)(2,1)S(1)}, bf16[16,2432]{1,0:T(8,128)(2,1)S(1)}, u32[]{:S(2)}, u32[]{:S(2)}) collective-permute-start(bf16[16,2432]{1,0:T(8,128)(2,1)S(1)} %get-tuple-element.59), channel_id=1, source_target_pairs={{0,2},{2,0},{1,3},{3,1},{4,6},{6,4},{5,7},{7,5},{8,10},{10,8},{9,1... | collective-permute-start | bytes 233480 | tf_op jit(solution)/shard_map/ppermute | solution.py:30
  72.3 1.3 %collective-permute-start.17 = (bf16[16,1152]{1,0:T(8,128)(2,1)S(1)}, bf16[16,1152]{1,0:T(8,128)(2,1)S(1)}, u32[]{:S(2)}, u32[]{:S(2)}) collective-permute-start(bf16[16,1152]{1,0:T(8,128)(2,1)S(1)} %shard_map.116.own_ref), channel_id=1, source_target_pairs={{0,1},{1,0},{2,3},{3,2},{4,5},{5,4},{6,7},{7,6},{8,9},{9,8},{10,11... | collective-permute-start | bytes 110600 | tf_op jit(solution)/shard_map/ppermute | solution.py:30
  74.8 4.5 %collective-permute-start.18 = (bf16[4,1792]{1,0:T(4,128)(2,1)S(1)}, bf16[4,1792]{1,0:T(4,128)(2,1)S(1)}, u32[]{:S(2)}, u32[]{:S(2)}) collective-permute-start(bf16[4,1792]{1,0:T(4,128)(2,1)S(1)} %get-tuple-element.62), channel_id=1, source_target_pairs={{0,4},{4,0},{8,12},{12,8},{1,5},{5,1},{9,13},{13,9},{2,6},{6,2},{1... | collective-permute-start | bytes 43016 | tf_op jit(solution)/shard_map/ppermute | solution.py:30
  75.2 4.6 %collective-permute-start.19 = (bf16[4,1792]{1,0:T(4,128)(2,1)S(1)}, bf16[4,1792]{1,0:T(4,128)(2,1)S(1)}, u32[]{:S(2)}, u32[]{:S(2)}) collective-permute-start(bf16[4,1792]{1,0:T(4,128)(2,1)S(1)} %get-tuple-element.63), channel_id=1, source_target_pairs={{0,8},{4,12},{8,0},{12,4},{1,9},{5,13},{9,1},{13,5},{2,10},{6,14},... | collective-permute-start | bytes 43016 | tf_op jit(solution)/shard_map/ppermute | solution.py:30
  78.0 5.5 %collective-permute-start.20 = (bf16[4,1792]{1,0:T(4,128)(2,1)S(1)}, bf16[4,1792]{1,0:T(4,128)(2,1)S(1)}, u32[]{:S(2)}, u32[]{:S(2)}) collective-permute-start(bf16[4,1792]{1,0:T(4,128)(2,1)S(1)} %get-tuple-element.64), channel_id=1, source_target_pairs={{0,12},{4,8},{8,4},{12,0},{1,13},{5,9},{9,5},{13,1},{2,14},{6,10},... | collective-permute-start | bytes 43016 | tf_op jit(solution)/shard_map/ppermute | solution.py:30
where the time goes:
time: 84.4 us; the launch traced here: 84.1 us
  waiting for transfers between devices  31.8 us (38%)
  Pallas kernels  25.6 us (30%)
  starting transfers between devices  24 us (28%)
  local copies, waits for them, and re-layouts  2.62 us (3%)
    ppermute x21, waiting for transfers between devices, xor_permute(): return lax.ppermute(x, axis, [(i, i ^ mask) for i in range(size)])  31.8 us
    pallas_call x10, Pallas kernels, call(): pl.pallas_call(body, out_shape=outs, in_specs=specs, out_specs=jax.tree.m...  25.6 us
    ppermute x21, starting transfers between devices, xor_permute(): return lax.ppermute(x, axis, [(i, i ^ mask) for i in range(size)])  24 us
  transfers between devices with their start and end apart: 21, of which 12 were waited for; matrix products, arithmetic and copies ran while one was open for 2% of the time, Pallas kernels for 21%

commit v1 on v0

--- a/solution.py
+++ b/solution.py
@@ -13,10 +13,10 @@
 SCALE = 0.07216878364870323
 EPSILON = 1e-06
 DEAD = -1e30
-STAT_ROWS = 16
+STAT_ROWS = 8
 LANES = 128
 ATTEND_LIMIT = 8 << 20
-KERNEL_LIMIT = 3 << 20
+KERNEL_LIMIT = 6 << 20
 
 
 f32, bf16 = jnp.float32, jnp.bfloat16
@@ -30,11 +30,15 @@
     return lax.ppermute(x, axis, [(i, i ^ mask) for i in range(size)])
 
 
-def exchange(pieces, axis):
+def exchange(pieces, axis, masks=None):
     got = {0: pieces[0]}
-    for mask in reversed(range(1, len(pieces))):
+    for mask in masks or reversed(range(1, len(pieces))):
         got[mask] = xor_permute(pieces[mask], axis, mask)
-    return [got[mask] for mask in range(len(pieces))]
+    return got
+
+
+def listed(got):
+    return [got[mask] for mask in sorted(got)]
 
 
 def call(body, outs, args, specs, scratch=(), limit=KERNEL_LIMIT, cost=None):
@@ -227,7 +231,7 @@
     )
 
 
-def gate_and_up(pieces, residual, gain, gate_weight, up_weight):
+def gate_and_up_away(pieces, residual, gain, gate_weight, up_weight):
     count = len(pieces)
     rows, width = residual.shape
     hidden = gate_weight.shape[1]
@@ -236,37 +240,67 @@
     own_rows = rows // count
 
     def body(*refs):
-        residual_ref, gain_ref, gate_ref, up_ref, keep_ref, send_ref, base_ref, split, placed = refs[count:]
+        residual_ref, gain_ref, gate_ref, up_ref = refs[count : count + 4]
+        send_ref, scaled_ref, squares_ref, base_ref, placed = refs[count + 4 :]
         resid = residual_ref[...].astype(f32) + sum(ref[...].astype(f32) for ref in refs[:count])
+        scaled = (resid * gain_ref[...]).astype(bf16)
+        scaled_ref[...] = scaled
+        other = lax.axis_index("seq") ^ 1
+        for k in range(cores):
+
+            @pl.when(other == k)
+            def _(k=k):
+                part = slice(k * half, (k + 1) * half)
+                gate = jnp.dot(scaled, gate_ref[:, part], preferred_element_type=f32)
+                up = jnp.dot(scaled, up_ref[:, part], preferred_element_type=f32)
+                send_ref[:, :half] = gate.astype(bf16)
+                send_ref[:, half : 2 * half] = up.astype(bf16)
+
         for k in range(count):
             placed[k] = resid[k * own_rows : (k + 1) * own_rows]
         base_ref[...] = placed[lax.axis_index("ctx")]
         squares = jnp.sum(resid * resid, axis=1, keepdims=True)
-        scaled = (resid * gain_ref[...]).astype(bf16)
-        gate = jnp.dot(scaled, gate_ref[...], preferred_element_type=f32)
-        up = jnp.dot(scaled, up_ref[...], preferred_element_type=f32)
-        for k in range(cores):
-            split[k, :, :half] = gate[:, k * half : (k + 1) * half]
-            split[k, :, half:] = up[:, k * half : (k + 1) * half]
-        me = lax.axis_index("seq")
-        keep_ref[:, : 2 * half] = split[me]
-        send_ref[:, : 2 * half] = split[me ^ 1].astype(bf16)
-        keep_ref[:, 2 * half :] = jnp.broadcast_to(squares, (rows, LANES))
         lane = lax.broadcasted_iota(jnp.int32, (rows, LANES), 1)
+        squares_ref[...] = jnp.broadcast_to(squares, (rows, LANES))
         send_ref[:, 2 * half :] = spread(squares, lane)
 
-    shape = (rows, 2 * half + LANES)
     return call(
         body,
         [
-            jax.ShapeDtypeStruct(shape, f32),
-            jax.ShapeDtypeStruct(shape, bf16),
+            jax.ShapeDtypeStruct((rows, 2 * half + LANES), bf16),
+            jax.ShapeDtypeStruct((rows, width), bf16),
+            jax.ShapeDtypeStruct((rows, LANES), f32),
             jax.ShapeDtypeStruct((own_rows, width), f32),
         ],
         [*pieces, residual, gain, in_vmem(gate_weight), in_vmem(up_weight)],
         [IN_VMEM] * (count + 4),
-        [pltpu.VMEM((cores, rows, 2 * half), f32), pltpu.VMEM((count, own_rows, width), f32)],
-        cost=(4 * rows * width * hidden, 4 << 20),
+        [pltpu.VMEM((count, own_rows, width), f32)],
+        cost=(2 * rows * width * hidden, 4 << 20),
+    )
+
+
+def gate_and_up_here(scaled, gate_weight, up_weight):
+    rows, width = scaled.shape
+    hidden = gate_weight.shape[1]
+    cores = lax.axis_size("seq")
+    half = hidden // cores
+
+    def body(scaled_ref, gate_ref, up_ref, keep_ref):
+        me = lax.axis_index("seq")
+        for k in range(cores):
+
+            @pl.when(me == k)
+            def _(k=k):
+                part = slice(k * half, (k + 1) * half)
+                keep_ref[:, :half] = jnp.dot(scaled_ref[...], gate_ref[:, part], preferred_element_type=f32)
+                keep_ref[:, half:] = jnp.dot(scaled_ref[...], up_ref[:, part], preferred_element_type=f32)
+
+    return call(
+        body,
+        jax.ShapeDtypeStruct((rows, 2 * half), f32),
+        [scaled, in_vmem(gate_weight), in_vmem(up_weight)],
+        [IN_VMEM] * 3,
+        cost=(2 * rows * width * hidden, 4 << 20),
     )
 
 
@@ -279,26 +313,24 @@
     ).astype(bf16)
 
 
-def add_core(keep, got):
-    rows, width = keep.shape
+def add_core(keep, squares, got):
+    rows, width = got.shape
     body_width = width - LANES
 
-    def body(keep_ref, got_ref, sum_ref, send_ref):
-        total = keep_ref[:, :body_width] + got_ref[:, :body_width].astype(f32)
-        squares = keep_ref[:, body_width : body_width + 1] + jnp.sum(
-            got_ref[:, body_width:].astype(f32), axis=1, keepdims=True
-        )
+    def body(keep_ref, squares_ref, got_ref, sum_ref, send_ref):
+        total = keep_ref[...] + got_ref[:, :body_width].astype(f32)
+        both = squares_ref[:, 0:1] + jnp.sum(got_ref[:, body_width:].astype(f32), axis=1, keepdims=True)
         sum_ref[:, :body_width] = total
-        sum_ref[:, body_width:] = jnp.broadcast_to(squares, (rows, LANES))
+        sum_ref[:, body_width:] = jnp.broadcast_to(both, (rows, LANES))
         send_ref[:, :body_width] = total.astype(bf16)
         lane = lax.broadcasted_iota(jnp.int32, (rows, LANES), 1)
-        send_ref[:, body_width:] = spread(squares, lane)
+        send_ref[:, body_width:] = spread(both, lane)
 
     return call(
         body,
         [jax.ShapeDtypeStruct((rows, width), f32), jax.ShapeDtypeStruct((rows, width), bf16)],
-        [keep, got],
-        [IN_VMEM] * 2,
+        [keep, squares, got],
+        [IN_VMEM] * 3,
         cost=(rows * width, rows * width * 8),
     )
 
@@ -328,19 +360,35 @@
     )
 
 
-def project_down(own, other, weight):
+def project_down_own(own, weight):
     rows, half = own.shape
+    width = weight.shape[1]
+
+    def body(own_ref, weight_ref, out_ref):
+        start = pl.multiple_of(lax.axis_index("seq") * half, 16)
+        out_ref[...] = jnp.dot(own_ref[...], weight_ref[pl.ds(start, half), :], preferred_element_type=f32)
+
+    return call(
+        body,
+        jax.ShapeDtypeStruct((rows, width), f32),
+        [own, in_vmem(weight)],
+        [IN_VMEM] * 2,
+        cost=(2 * rows * half * width, 4 << 20),
+    )
+
+
+def project_down_other(other, weight, partial):
+    rows, half = other.shape
     width = weight.shape[1]
     count = lax.axis_size("ctx")
     own_rows = rows // count
 
-    def body(own_ref, other_ref, weight_ref, *refs):
-        out_refs, (joined, placed) = refs[:count], refs[count:]
-        core = lax.axis_index("seq")
-        joined[core] = own_ref[...]
-        joined[core ^ 1] = other_ref[...]
-        hidden = jnp.concatenate([joined[0], joined[1]], axis=1)
-        out = jnp.dot(hidden, weight_ref[...], preferred_element_type=f32)
+    def body(other_ref, weight_ref, partial_ref, *refs):
+        out_refs, placed = refs[:count], refs[count]
+        start = pl.multiple_of((lax.axis_index("seq") ^ 1) * half, 16)
+        out = partial_ref[...] + jnp.dot(
+            other_ref[...], weight_ref[pl.ds(start, half), :], preferred_element_type=f32
+        )
         for k in range(count):
             placed[k] = out[k * own_rows : (k + 1) * own_rows]
         me = lax.axis_index("ctx")
@@ -350,10 +398,10 @@
     return call(
         body,
         [jax.ShapeDtypeStruct((own_rows, width), bf16)] * count,
-        [own, other, in_vmem(weight)],
+        [other, in_vmem(weight), partial],
         [IN_VMEM] * 3,
-        [pltpu.VMEM((2, rows, half), bf16), pltpu.VMEM((count, own_rows, width), f32)],
-        cost=(4 * rows * half * width, 4 << 20),
+        [pltpu.VMEM((count, own_rows, width), f32)],
+        cost=(2 * rows * half * width, 4 << 20),
     )
 
 
@@ -388,35 +436,54 @@
     roles = lax.axis_size("role")
     members = lax.axis_size(("role", "seq"))
 
-    groups = exchange([queries] * blocks, "ctx")
-    along = exchange([value_up_weight] * roles, "role")
-
-    own_queries, cache_fast, up_own, out_fast, seen = fetch(
+    evens, odds = range(2, blocks, 2), range(3, blocks, 2)
+
+    groups = exchange([queries] * blocks, "ctx", [*evens, 1])
+    along = listed(exchange([value_up_weight] * roles, "role"))
+    groups[0], cache_fast, up_own, out_fast, seen = fetch(
         [queries, jnp.swapaxes(cache, 1, 2), value_up_weight, out_proj], lengths, positions
     )
-    partial = list(attend([own_queries, *groups[1:]], cache_fast, seen))
-
-    gate_weight, up_weight, down_weight, partial[0] = lax.optimization_barrier(
-        (gate_weight, up_weight, down_weight, partial[0])
-    )
-    parts = exchange(partial, "ctx")
-    gate_fast, up_fast, down_fast, residual, gain = fetch(
-        [gate_weight, up_weight, down_weight, residual, norm_gain.reshape(1, -1)]
+    relayed = {}
+    for mask in evens:
+        relayed[mask + 1] = xor_permute(groups[mask], "ctx", 1)
+
+    def attend_and_answer(source, masks):
+        outs = attend([source[mask] for mask in masks], cache_fast, seen)
+        return dict(zip(masks, outs))
+
+    partial = attend_and_answer(groups, evens)
+    answers = exchange({0: None, **partial}, "ctx", evens)
+    near = attend_and_answer(groups, [0, 1])
+    answers |= exchange(near, "ctx", [1])
+    far = attend_and_answer(relayed, odds)
+
+    gate_weight, up_weight, far[odds[0]] = lax.optimization_barrier((gate_weight, up_weight, far[odds[0]]))
+    answers |= exchange({0: near[0], **far}, "ctx", odds)
+    gate_fast, up_fast, residual, gain = fetch(
+        [gate_weight, up_weight, residual, norm_gain.reshape(1, -1)]
     )
     *along, gain = lax.optimization_barrier((*along, gain))
     across = [xor_permute(piece, "seq", 1) for piece in along]
     up_pieces = [up_own, *[piece for pair in zip(along, across) for piece in pair][1:]]
-    values = join_and_project(parts, up_pieces, rows, heads, gain)
-    shared = exchange([values] * members, ("role", "seq"))
-    terms = exchange([project_out(shared, out_fast)] * blocks, "ctx")
-    keep, send, base = gate_and_up(terms, residual, gain, gate_fast, up_fast)
-    keep, send = add_core(keep, xor_permute(send, "seq", 1))
-    pieces = exchange([send] * roles, "role")[1:]
+
+    values = join_and_project(listed(answers), up_pieces, rows, heads, gain)
+    shared = listed(exchange([values] * members, ("role", "seq")))
+    product = project_out(shared, out_fast)
+    down_weight, product = lax.optimization_barrier((down_weight, product))
+    terms = listed(exchange([product] * blocks, "ctx"))
+    (down_fast,) = fetch([down_weight])
+
+    send, scaled, squares, base = gate_and_up_away(terms, residual, gain, gate_fast, up_fast)
+    got = xor_permute(send, "seq", 1)
+    keep = gate_and_up_here(scaled, gate_fast, up_fast)
+    keep, send = add_core(keep, squares, got)
+    pieces = listed(exchange([send] * roles, "role"))[1:]
     features = norm_gain.shape[0] * members
     hidden = activate(keep, pieces, features)
-    last = project_down(hidden, xor_permute(hidden, "seq", 1), down_fast)
-    last = exchange(last, "ctx")
-    return finish(base, last)
+    other = xor_permute(hidden, "seq", 1)
+    own = project_down_own(hidden, down_fast)
+    last = exchange(project_down_other(other, down_fast, own), "ctx")
+    return finish(base, listed(last))
 
 
 def solution(mesh):

time: 84.4 us -> 95.1 us (1.13)
  waiting for transfers between devices: 31.8 us -> 37.2 us
  Pallas kernels: 25.6 us -> 29.5 us
  starting transfers between devices: 24 us -> 25.4 us
    ppermute x21, waiting for transfers between devices: 31.8 us -> 37.2 us  [xor_permute(): return lax.ppermute(x, axis, [(i, i ^ mask) for i in range(size)])]
    pallas_call x10 -> x15, Pallas kernels: 25.6 us -> 29.5 us  [call(): pl.pallas_call(body, out_shape=outs, in_specs=specs, out_specs=jax.tree.m...]
    ppermute x21, starting transfers between devices: 24 us -> 25.4 us  [xor_permute(): return lax.ppermute(x, axis, [(i, i ^ mask) for i in range(size)])]
  transfers between devices with their start and end apart: 21 -> 21, of which waited for: 12 -> 12; matrix products, arithmetic and copies ran while one was open for 2% -> 1% of each run, Pallas kernels for 21% -> 24%
where the time goes in v1:
time: 95.1 us; the launch traced here: 94.9 us
  waiting for transfers between devices  37.2 us (39%)
  Pallas kernels  29.5 us (31%)
  starting transfers between devices  25.4 us (27%)
  local copies, waits for them, and re-layouts  2.62 us (3%)
    ppermute x21, waiting for transfers between devices, xor_permute(): return lax.ppermute(x, axis, [(i, i ^ mask) for i in range(size)])  37.2 us
    pallas_call x15, Pallas kernels, call(): pl.pallas_call(body, out_shape=outs, in_specs=specs, out_specs=jax.tree.m...  29.5 us
    ppermute x21, starting transfers between devices, xor_permute(): return lax.ppermute(x, axis, [(i, i ^ mask) for i in range(size)])  25.4 us
  transfers between devices with their start and end apart: 21, of which 12 were waited for; matrix products, arithmetic and copies ran while one was open for 1% of the time, Pallas kernels for 24%

profile of v1, /device:TPU:0, one launch (start us, length us, event | category | flops | bytes accessed | tf_op | source)
XLA Modules:
  0.0 94.9 jit_solution(147050706628146845)
XLA Ops:
  0.0 3.0 %collective-permute-start.6 = (bf16[32,128,128]{2,1,0:T(8,128)(2,1)}, bf16[32,128,128]{2,1,0:T(8,128)(2,1)S(1)}, u32[]{:S(2)}, u32[]{:S(2)}) collective-permute-start(bf16[32,128,128]{2,1,0:T(8,128)(2,1)} %refs_2_.2), channel_id=1, source_target_pairs={{0,2},{2,0},{1,3},{3,1},{4,6},{6,4},{5,7},{7,5},{8,10},{10,8},{9,1... | collective-permute-start | bytes 3145736 | tf_op jit(solution)/shard_map/ppermute | solution.py:30
  3.0 2.6 %collective-permute-start.2 = (bf16[4,32,576]{2,1,0:T(8,128)(2,1)}, bf16[4,32,576]{2,1,0:T(8,128)(2,1)S(1)}, u32[]{:S(2)}, u32[]{:S(2)}) collective-permute-start(bf16[4,32,576]{2,1,0:T(8,128)(2,1)} %refs_0_.1), channel_id=1, source_target_pairs={{0,8},{4,12},{8,0},{12,4},{1,9},{5,13},{9,1},{13,5},{2,10},{6,14},... | collective-permute-start | bytes 442376 | tf_op jit(solution)/shard_map/ppermute | solution.py:30
  5.6 7.7 %collective-permute-done.2.refs_0_ = bf16[4,32,576]{2,1,0:T(8,128)(2,1)S(1)} collective-permute-done((bf16[4,32,576]{2,1,0:T(8,128)(2,1)}, bf16[4,32,576]{2,1,0:T(8,128)(2,1)S(1)}, u32[]{:S(2)}, u32[]{:S(2)}) %collective-permute-start.2) | collective-permute-done | bytes 147488 | tf_op jit(solution)/shard_map/ppermute | solution.py:30
  13.2 0.8 collective-permute-start.4
  14.0 1.3 %reshape.3.refs_3_ = f32[1,1792]{1,0:T(1,128)} reshape(f32[1792]{0:T(1024)} %param.18) | data formatting | bytes 14336 | tf_op jit(solution)/shard_map/reshape | solution.py:463
  15.3 0.7 copy-done
  16.0 0.7 copy-done.1
  16.6 6.9 %shard_map.109 = (bf16[4,32,576]{2,1,0:T(8,128)(2,1)S(1)}, bf16[2,576,1024]{2,1,0:T(8,128)(2,1)S(1)}, bf16[32,128,128]{2,1,0:T(8,128)(2,1)S(1)}, bf16[4096,1792]{1,0:T(8,128)(2,1)S(1)}, s32[4,128]{1,0:T(4,128)S(1)}) custom-call(bf16[4,32,576]{2,1,0:T(8,128)(2,1)} %refs_0_.1, bf16[2,576,1024]{2,1,0:T(8,128)(2,1)} %bitcast.1, bf16[32,128,128]{2,1,0:T(8,128)(2,1)} %refs_2_.2, ...), custom_call_target="tpu_custom_call" | custom-call | bytes 36470784 | tf_op jit(solution)/shard_map/pallas_call | solution.py:46
  23.5 0.0 collective-permute-done.4.refs_0_
  23.5 1.5 %shard_map.112 = bf16[136,512]{1,0:T(8,128)(2,1)S(1)} custom-call(bf16[4,32,576]{2,1,0:T(8,128)(2,1)S(1)} %collective-permute-done.4.refs_0_, bf16[2,576,1024]{2,1,0:T(8,128)(2,1)S(1)} %get-tuple-element.35.refs_2_.refs_1_, s32[4,128]{1,0:T(4,128)S(1)} %get-tuple-element.36.refs_3_.refs_2_), custom_call_target="tpu_custom_call" | custom-call | flops 285212672 | bytes 4194304 | tf_op jit(solution)/shard_map/pallas_call | solution.py:46
  25.1 0.0 copy-start.2
  25.1 0.0 copy-start.3
  25.1 5.9 %shard_map.113 = (bf16[1792,2304]{1,0:T(8,128)(2,1)S(1)}, bf16[1792,2304]{1,0:T(8,128)(2,1)S(1)}, bf16[16,1792]{1,0:T(8,128)(2,1)S(1)}, f32[1,1792]{1,0:T(1,128)S(1)}) custom-call(bf16[1792,2304]{1,0:T(8,128)(2,1)} %refs_0_.2, bf16[1792,2304]{1,0:T(8,128)(2,1)} %refs_1_, bf16[16,1792]{1,0:T(8,128)(2,1)} %refs_2_.3, f32[1,1792]{1,0:T(1,128)} %reshape.3.refs_3_), custom_call_target="tpu_custom_call" | custom-call | bytes 33159168 | tf_op jit(solution)/shard_map/pallas_call | solution.py:46
  31.0 0.0 collective-permute-done.6.refs_6_
  31.0 0.0 copy-done.2
  31.0 0.1 collective-permute-start.7
  31.1 0.5 collective-permute-start.8
  31.6 0.0 copy-done.3
  31.6 1.2 %collective-permute-start = (bf16[4,32,576]{2,1,0:T(8,128)(2,1)S(1)}, bf16[4,32,576]{2,1,0:T(8,128)(2,1)S(1)}, u32[]{:S(2)}, u32[]{:S(2)}) collective-permute-start(bf16[4,32,576]{2,1,0:T(8,128)(2,1)S(1)} %copy-done.3), channel_id=1, source_target_pairs={{0,4},{4,0},{8,12},{12,8},{1,5},{5,1},{9,13},{13,9},{2,6},{6,2},{1... | collective-permute-start | bytes 442376 | tf_op jit(solution)/shard_map/ppermute | solution.py:30
  32.9 4.9 %collective-permute-done.refs_1_ = bf16[4,32,576]{2,1,0:T(8,128)(2,1)S(1)} collective-permute-done((bf16[4,32,576]{2,1,0:T(8,128)(2,1)S(1)}, bf16[4,32,576]{2,1,0:T(8,128)(2,1)S(1)}, u32[]{:S(2)}, u32[]{:S(2)}) %collective-permute-start) | collective-permute-done | bytes 147488 | tf_op jit(solution)/shard_map/ppermute | solution.py:30
  37.8 1.7 %shard_map.110 = (bf16[136,512]{1,0:T(8,128)(2,1)S(1)}, bf16[136,512]{1,0:T(8,128)(2,1)S(1)}) custom-call(bf16[4,32,576]{2,1,0:T(8,128)(2,1)S(1)} %get-tuple-element.34.refs_0_, bf16[4,32,576]{2,1,0:T(8,128)(2,1)S(1)} %collective-permute-done.refs_1_, bf16[2,576,1024]{2,1,0:T(8,128)(2,1)S(1)} %get-tuple-element.35.refs_2_.refs_1_, ...), custom_call_target="tpu_custom_call" | custom-call | flops 570425344 | bytes 4194304 | tf_op jit(solution)/shard_map/pallas_call | solution.py:46
  39.5 1.3 %collective-permute-start.1 = (bf16[136,512]{1,0:T(8,128)(2,1)S(1)}, bf16[136,512]{1,0:T(8,128)(2,1)S(1)}, u32[]{:S(2)}, u32[]{:S(2)}) collective-permute-start(bf16[136,512]{1,0:T(8,128)(2,1)S(1)} %get-tuple-element.38), channel_id=1, source_target_pairs={{0,4},{4,0},{8,12},{12,8},{1,5},{5,1},{9,13},{13,9},{2,6},{6,2},{1... | collective-permute-start | bytes 417800 | tf_op jit(solution)/shard_map/ppermute | solution.py:30
  40.9 1.5 %shard_map.111 = bf16[136,512]{1,0:T(8,128)(2,1)S(1)} custom-call(bf16[4,32,576]{2,1,0:T(8,128)(2,1)S(1)} %collective-permute-done.2.refs_0_, bf16[2,576,1024]{2,1,0:T(8,128)(2,1)S(1)} %get-tuple-element.35.refs_2_.refs_1_, s32[4,128]{1,0:T(4,128)S(1)} %get-tuple-element.36.refs_3_.refs_2_), custom_call_target="tpu_custom_call" | custom-call | flops 285212672 | bytes 4194304 | tf_op jit(solution)/shard_map/pallas_call | solution.py:46
  42.4 2.4 %collective-permute-start.3 = (bf16[136,512]{1,0:T(8,128)(2,1)S(1)}, bf16[136,512]{1,0:T(8,128)(2,1)S(1)}, u32[]{:S(2)}, u32[]{:S(2)}) collective-permute-start(bf16[136,512]{1,0:T(8,128)(2,1)S(1)} %shard_map.111), channel_id=1, source_target_pairs={{0,8},{4,12},{8,0},{12,4},{1,9},{5,13},{9,1},{13,5},{2,10},{6,14},... | collective-permute-start | bytes 417800 | tf_op jit(solution)/shard_map/ppermute | solution.py:30
  44.8 1.3 %collective-permute-start.5 = (bf16[136,512]{1,0:T(8,128)(2,1)S(1)}, bf16[136,512]{1,0:T(8,128)(2,1)S(1)}, u32[]{:S(2)}, u32[]{:S(2)}) collective-permute-start(bf16[136,512]{1,0:T(8,128)(2,1)S(1)} %shard_map.112), channel_id=1, source_target_pairs={{0,12},{4,8},{8,4},{12,0},{1,13},{5,9},{9,5},{13,1},{2,14},{6,10},... | collective-permute-start | bytes 417800 | tf_op jit(solution)/shard_map/ppermute | solution.py:30
  46.0 0.0 collective-permute-done.1.refs_1_
  46.0 9.2 %collective-permute-done.3.refs_2_ = bf16[136,512]{1,0:T(8,128)(2,1)S(1)} collective-permute-done((bf16[136,512]{1,0:T(8,128)(2,1)S(1)}, bf16[136,512]{1,0:T(8,128)(2,1)S(1)}, u32[]{:S(2)}, u32[]{:S(2)}) %collective-permute-start.3) | collective-permute-done | bytes 139296 | tf_op jit(solution)/shard_map/ppermute | solution.py:30
  55.2 0.0 collective-permute-done.5.refs_3_
  55.2 0.0 collective-permute-done.7.refs_5_
  55.2 0.0 collective-permute-done.8.refs_7_
  55.2 1.7 %shard_map.114.refs_0_ = bf16[4,4096]{1,0:T(4,128)(2,1)S(1)} custom-call(bf16[136,512]{1,0:T(8,128)(2,1)S(1)} %get-tuple-element.37.refs_0_, bf16[136,512]{1,0:T(8,128)(2,1)S(1)} %collective-permute-done.1.refs_1_, bf16[136,512]{1,0:T(8,128)(2,1)S(1)} %collective-permute-done.3.refs_2_, bf16[136,512]{1,0:T(8,128)(2,1)S(1)} %collective-permute-done.5.refs_3_, ...), custom_call_target="tpu_custom_call" | custom-call | flops 16777216 | bytes 4194304 | tf_op jit(solution)/shard_map/pallas_call | solution.py:46
  56.9 0.0 collective-permute-start.11
  56.9 0.6 collective-permute-start.10
  57.4 1.3 %collective-permute-start.9 = (bf16[4,4096]{1,0:T(4,128)(2,1)S(1)}, bf16[4,4096]{1,0:T(4,128)(2,1)S(1)}, u32[]{:S(2)}, u32[]{:S(2)}) collective-permute-start(bf16[4,4096]{1,0:T(4,128)(2,1)S(1)} %shard_map.114.refs_0_), channel_id=1, source_target_pairs={{0,1},{1,0},{2,3},{3,2},{4,5},{5,4},{6,7},{7,6},{8,9},{9,8},{10,11... | collective-permute-start | bytes 98312 | tf_op jit(solution)/shard_map/ppermute | solution.py:30
  58.8 1.5 %collective-permute-done.11.refs_3_ = bf16[4,4096]{1,0:T(4,128)(2,1)S(1)} collective-permute-done((bf16[4,4096]{1,0:T(4,128)(2,1)S(1)}, bf16[4,4096]{1,0:T(4,128)(2,1)S(1)}, u32[]{:S(2)}, u32[]{:S(2)}) %collective-permute-start.11) | collective-permute-done | bytes 32800 | tf_op jit(solution)/shard_map/ppermute | solution.py:30
  60.2 0.7 collective-permute-done.10.refs_2_
  60.9 0.0 collective-permute-done.9.refs_1_
  60.9 2.0 %shard_map.115.refs_0_ = bf16[16,1792]{1,0:T(8,128)(2,1)S(1)} custom-call(bf16[4,4096]{1,0:T(4,128)(2,1)S(1)} %shard_map.114.refs_0_, bf16[4,4096]{1,0:T(4,128)(2,1)S(1)} %collective-permute-done.9.refs_1_, bf16[4,4096]{1,0:T(4,128)(2,1)S(1)} %collective-permute-done.10.refs_2_, bf16[4,4096]{1,0:T(4,128)(2,1)S(1)} %collective-permute-done.11.refs_3_, ...), custom_call_target="tpu_custom_call" | custom-call | flops 234881024 | bytes 4194304 | tf_op jit(solution)/shard_map/pallas_call | solution.py:46
  63.0 2.6 %collective-permute-start.14 = (bf16[16,1792]{1,0:T(8,128)(2,1)S(1)}, bf16[16,1792]{1,0:T(8,128)(2,1)S(1)}, u32[]{:S(2)}, u32[]{:S(2)}) collective-permute-start(bf16[16,1792]{1,0:T(8,128)(2,1)S(1)} %shard_map.115.refs_0_), channel_id=1, source_target_pairs={{0,12},{4,8},{8,4},{12,0},{1,13},{5,9},{9,5},{13,1},{2,14},{6,10},... | collective-permute-start | bytes 172040 | tf_op jit(solution)/shard_map/ppermute | solution.py:30
  65.5 2.0 %collective-permute-start.13 = (bf16[16,1792]{1,0:T(8,128)(2,1)S(1)}, bf16[16,1792]{1,0:T(8,128)(2,1)S(1)}, u32[]{:S(2)}, u32[]{:S(2)}) collective-permute-start(bf16[16,1792]{1,0:T(8,128)(2,1)S(1)} %shard_map.115.refs_0_), channel_id=1, source_target_pairs={{0,8},{4,12},{8,0},{12,4},{1,9},{5,13},{9,1},{13,5},{2,10},{6,14},... | collective-permute-start | bytes 172040 | tf_op jit(solution)/shard_map/ppermute | solution.py:30
  67.6 0.5 collective-permute-start.12
  68.1 1.0 %collective-permute-done.14.refs_3_ = bf16[16,1792]{1,0:T(8,128)(2,1)S(1)} collective-permute-done((bf16[16,1792]{1,0:T(8,128)(2,1)S(1)}, bf16[16,1792]{1,0:T(8,128)(2,1)S(1)}, u32[]{:S(2)}, u32[]{:S(2)}) %collective-permute-start.14) | collective-permute-done | bytes 57376 | tf_op jit(solution)/shard_map/ppermute | solution.py:30
  69.0 3.0 %collective-permute-done.13.refs_2_ = bf16[16,1792]{1,0:T(8,128)(2,1)S(1)} collective-permute-done((bf16[16,1792]{1,0:T(8,128)(2,1)S(1)}, bf16[16,1792]{1,0:T(8,128)(2,1)S(1)}, u32[]{:S(2)}, u32[]{:S(2)}) %collective-permute-start.13) | collective-permute-done | bytes 57376 | tf_op jit(solution)/shard_map/ppermute | solution.py:30
  72.1 0.3 collective-permute-done.12.refs_1_
  72.3 1.3 %shard_map.116 = (bf16[16,2432]{1,0:T(8,128)(2,1)S(1)}, bf16[16,1792]{1,0:T(8,128)(2,1)S(1)}, f32[16,128]{1,0:T(8,128)S(1)}, f32[4,1792]{1,0:T(4,128)S(1)}) custom-call(bf16[16,1792]{1,0:T(8,128)(2,1)S(1)} %shard_map.115.refs_0_, bf16[16,1792]{1,0:T(8,128)(2,1)S(1)} %collective-permute-done.12.refs_1_, bf16[16,1792]{1,0:T(8,128)(2,1)S(1)} %collective-permute-done.13.refs_2_, ...), custom_call_target="tpu_custom_call" | custom-call | flops 132120576 | bytes 4194304 | tf_op jit(solution)/shard_map/pallas_call | solution.py:46
  73.7 0.0 collective-permute-start.15
  73.7 1.2 %shard_map.117.keep_ref = f32[16,2304]{1,0:T(8,128)S(1)} custom-call(bf16[16,1792]{1,0:T(8,128)(2,1)S(1)} %get-tuple-element.53.scaled_ref, bf16[1792,2304]{1,0:T(8,128)(2,1)S(1)} %get-tuple-element.50.refs_6_.gate_ref, bf16[1792,2304]{1,0:T(8,128)(2,1)S(1)} %get-tuple-element.51.refs_7_.up_ref), custom_call_target="tpu_custom_call" | custom-call | flops 132120576 | bytes 4194304 | tf_op jit(solution)/shard_map/pallas_call | solution.py:46
  74.9 0.1 collective-permute-done.15.got_ref
  75.0 0.2 shard_map.118
  75.1 0.8 collective-permute-start.16
  75.9 3.9 %collective-permute-done.16.refs_1_ = bf16[16,2432]{1,0:T(8,128)(2,1)S(1)} collective-permute-done((bf16[16,2432]{1,0:T(8,128)(2,1)S(1)}, bf16[16,2432]{1,0:T(8,128)(2,1)S(1)}, u32[]{:S(2)}, u32[]{:S(2)}) %collective-permute-start.16) | collective-permute-done | bytes 77856 | tf_op jit(solution)/shard_map/ppermute | solution.py:30
  79.8 0.2 shard_map.119.own_ref
  80.0 0.1 collective-permute-start.17
  80.1 3.4 %shard_map.120.weight_ref = bf16[2304,1792]{1,0:T(8,128)(2,1)S(1)} custom-call(bf16[2304,1792]{1,0:T(8,128)(2,1)} %refs_0_.3), custom_call_target="tpu_custom_call" | custom-call | bytes 16515072 | tf_op jit(solution)/shard_map/pallas_call | solution.py:46
  83.5 0.7 shard_map.121.partial_ref
  84.1 0.0 collective-permute-done.17.other_ref
  84.1 0.7 shard_map.122
  84.8 0.9 collective-permute-start.18
  85.7 3.1 %collective-permute-start.19 = (bf16[4,1792]{1,0:T(4,128)(2,1)S(1)}, bf16[4,1792]{1,0:T(4,128)(2,1)S(1)}, u32[]{:S(2)}, u32[]{:S(2)}) collective-permute-start(bf16[4,1792]{1,0:T(4,128)(2,1)S(1)} %get-tuple-element.61), channel_id=1, source_target_pairs={{0,8},{4,12},{8,0},{12,4},{1,9},{5,13},{9,1},{13,5},{2,10},{6,14},... | collective-permute-start | bytes 43016 | tf_op jit(solution)/shard_map/ppermute | solution.py:30
  88.8 0.5 collective-permute-start.20
  89.3 0.0 collective-permute-done.18.refs_2_
  89.3 1.2 %collective-permute-done.19.refs_3_ = bf16[4,1792]{1,0:T(4,128)(2,1)S(1)} collective-permute-done((bf16[4,1792]{1,0:T(4,128)(2,1)S(1)}, bf16[4,1792]{1,0:T(4,128)(2,1)S(1)}, u32[]{:S(2)}, u32[]{:S(2)}) %collective-permute-start.19) | collective-permute-done | bytes 14368 | tf_op jit(solution)/shard_map/ppermute | solution.py:30
  90.5 3.8 %collective-permute-done.20.refs_4_ = bf16[4,1792]{1,0:T(4,128)(2,1)S(1)} collective-permute-done((bf16[4,1792]{1,0:T(4,128)(2,1)S(1)}, bf16[4,1792]{1,0:T(4,128)(2,1)S(1)}, u32[]{:S(2)}, u32[]{:S(2)}) %collective-permute-start.20) | collective-permute-done | bytes 14368 | tf_op jit(solution)/shard_map/ppermute | solution.py:30
  94.3 0.6 shard_map.123
  (2 shorter events, 0.0 us)
Async XLA Ops:
  0.0 31.0 %collective-permute-start.6 = (bf16[32,128,128]{2,1,0:T(8,128)(2,1)}, bf16[32,128,128]{2,1,0:T(8,128)(2,1)S(1)}, u32[]{:S(2)}, u32[]{:S(2)}) collective-permute-start(bf16[32,128,128]{2,1,0:T(8,128)(2,1)} %refs_2_.2), channel_id=1, source_target_pairs={{0,2},{2,0},{1,3},{3,1},{4,6},{6,4},{5,7},{7,5},{8,10},{10,8},{9,1... | collective-permute-start | bytes 3145736 | tf_op jit(solution)/shard_map/ppermute | solution.py:30
  3.0 10.3 %collective-permute-start.2 = (bf16[4,32,576]{2,1,0:T(8,128)(2,1)}, bf16[4,32,576]{2,1,0:T(8,128)(2,1)S(1)}, u32[]{:S(2)}, u32[]{:S(2)}) collective-permute-start(bf16[4,32,576]{2,1,0:T(8,128)(2,1)} %refs_0_.1), channel_id=1, source_target_pairs={{0,8},{4,12},{8,0},{12,4},{1,9},{5,13},{9,1},{13,5},{2,10},{6,14},... | collective-permute-start | bytes 442376 | tf_op jit(solution)/shard_map/ppermute | solution.py:30
  13.2 10.3 %collective-permute-start.4 = (bf16[4,32,576]{2,1,0:T(8,128)(2,1)S(1)}, bf16[4,32,576]{2,1,0:T(8,128)(2,1)S(1)}, u32[]{:S(2)}, u32[]{:S(2)}) collective-permute-start(bf16[4,32,576]{2,1,0:T(8,128)(2,1)S(1)} %collective-permute-done.2.refs_0_), channel_id=1, source_target_pairs={{0,4},{4,0},{8,12},{12,8},{1,5},{5,1},{9,13},{13,9},{2,6},{6,2},{1... | collective-permute-start | bytes 442376 | tf_op jit(solution)/shard_map/ppermute | solution.py:30
  15.3 0.7 copy-start
  16.0 0.7 copy-start.1
  25.1 6.0 %copy-start.2 = (bf16[32,128,128]{2,1,0:T(8,128)(2,1)S(1)}, bf16[32,128,128]{2,1,0:T(8,128)(2,1)}, u32[]{:S(2)}) copy-start(bf16[32,128,128]{2,1,0:T(8,128)(2,1)} %refs_2_.2) | copy-start | bytes 3145732
  25.1 6.5 %copy-start.3 = (bf16[4,32,576]{2,1,0:T(8,128)(2,1)S(1)}, bf16[4,32,576]{2,1,0:T(8,128)(2,1)}, u32[]{:S(2)}) copy-start(bf16[4,32,576]{2,1,0:T(8,128)(2,1)} %refs_0_.1) | copy-start | bytes 442372
  31.0 24.2 %collective-permute-start.7 = (bf16[32,128,128]{2,1,0:T(8,128)(2,1)S(1)}, bf16[32,128,128]{2,1,0:T(8,128)(2,1)S(1)}, u32[]{:S(2)}, u32[]{:S(2)}) collective-permute-start(bf16[32,128,128]{2,1,0:T(8,128)(2,1)S(1)} %copy-done.2), channel_id=1, source_target_pairs={{0,1},{1,0},{2,3},{3,2},{4,5},{5,4},{6,7},{7,6},{8,9},{9,8},{10,11... | collective-permute-start | bytes 3145736 | tf_op jit(solution)/shard_map/ppermute | solution.py:30
  31.1 24.1 %collective-permute-start.8 = (bf16[32,128,128]{2,1,0:T(8,128)(2,1)S(1)}, bf16[32,128,128]{2,1,0:T(8,128)(2,1)S(1)}, u32[]{:S(2)}, u32[]{:S(2)}) collective-permute-start(bf16[32,128,128]{2,1,0:T(8,128)(2,1)S(1)} %collective-permute-done.6.refs_6_), channel_id=1, source_target_pairs={{0,1},{1,0},{2,3},{3,2},{4,5},{5,4},{6,7},{7,6},{8,9},{9,8},{10,11... | collective-permute-start | bytes 3145736 | tf_op jit(solution)/shard_map/ppermute | solution.py:30
  31.6 6.2 %collective-permute-start = (bf16[4,32,576]{2,1,0:T(8,128)(2,1)S(1)}, bf16[4,32,576]{2,1,0:T(8,128)(2,1)S(1)}, u32[]{:S(2)}, u32[]{:S(2)}) collective-permute-start(bf16[4,32,576]{2,1,0:T(8,128)(2,1)S(1)} %copy-done.3), channel_id=1, source_target_pairs={{0,4},{4,0},{8,12},{12,8},{1,5},{5,1},{9,13},{13,9},{2,6},{6,2},{1... | collective-permute-start | bytes 442376 | tf_op jit(solution)/shard_map/ppermute | solution.py:30
  39.5 6.5 %collective-permute-start.1 = (bf16[136,512]{1,0:T(8,128)(2,1)S(1)}, bf16[136,512]{1,0:T(8,128)(2,1)S(1)}, u32[]{:S(2)}, u32[]{:S(2)}) collective-permute-start(bf16[136,512]{1,0:T(8,128)(2,1)S(1)} %get-tuple-element.38), channel_id=1, source_target_pairs={{0,4},{4,0},{8,12},{12,8},{1,5},{5,1},{9,13},{13,9},{2,6},{6,2},{1... | collective-permute-start | bytes 417800 | tf_op jit(solution)/shard_map/ppermute | solution.py:30
  42.4 12.8 %collective-permute-start.3 = (bf16[136,512]{1,0:T(8,128)(2,1)S(1)}, bf16[136,512]{1,0:T(8,128)(2,1)S(1)}, u32[]{:S(2)}, u32[]{:S(2)}) collective-permute-start(bf16[136,512]{1,0:T(8,128)(2,1)S(1)} %shard_map.111), channel_id=1, source_target_pairs={{0,8},{4,12},{8,0},{12,4},{1,9},{5,13},{9,1},{13,5},{2,10},{6,14},... | collective-permute-start | bytes 417800 | tf_op jit(solution)/shard_map/ppermute | solution.py:30
  44.8 10.4 %collective-permute-start.5 = (bf16[136,512]{1,0:T(8,128)(2,1)S(1)}, bf16[136,512]{1,0:T(8,128)(2,1)S(1)}, u32[]{:S(2)}, u32[]{:S(2)}) collective-permute-start(bf16[136,512]{1,0:T(8,128)(2,1)S(1)} %shard_map.112), channel_id=1, source_target_pairs={{0,12},{4,8},{8,4},{12,0},{1,13},{5,9},{9,5},{13,1},{2,14},{6,10},... | collective-permute-start | bytes 417800 | tf_op jit(solution)/shard_map/ppermute | solution.py:30
  56.9 3.3 %collective-permute-start.11 = (bf16[4,4096]{1,0:T(4,128)(2,1)S(1)}, bf16[4,4096]{1,0:T(4,128)(2,1)S(1)}, u32[]{:S(2)}, u32[]{:S(2)}) collective-permute-start(bf16[4,4096]{1,0:T(4,128)(2,1)S(1)} %shard_map.114.refs_0_), channel_id=1, source_target_pairs={{0,3},{1,2},{2,1},{3,0},{4,7},{5,6},{6,5},{7,4},{8,11},{9,10},{10,... | collective-permute-start | bytes 98312 | tf_op jit(solution)/shard_map/ppermute | solution.py:30
  56.9 4.0 %collective-permute-start.10 = (bf16[4,4096]{1,0:T(4,128)(2,1)S(1)}, bf16[4,4096]{1,0:T(4,128)(2,1)S(1)}, u32[]{:S(2)}, u32[]{:S(2)}) collective-permute-start(bf16[4,4096]{1,0:T(4,128)(2,1)S(1)} %shard_map.114.refs_0_), channel_id=1, source_target_pairs={{0,2},{1,3},{2,0},{3,1},{4,6},{5,7},{6,4},{7,5},{8,10},{9,11},{10,... | collective-permute-start | bytes 98312 | tf_op jit(solution)/shard_map/ppermute | solution.py:30
  57.4 3.5 %collective-permute-start.9 = (bf16[4,4096]{1,0:T(4,128)(2,1)S(1)}, bf16[4,4096]{1,0:T(4,128)(2,1)S(1)}, u32[]{:S(2)}, u32[]{:S(2)}) collective-permute-start(bf16[4,4096]{1,0:T(4,128)(2,1)S(1)} %shard_map.114.refs_0_), channel_id=1, source_target_pairs={{0,1},{1,0},{2,3},{3,2},{4,5},{5,4},{6,7},{7,6},{8,9},{9,8},{10,11... | collective-permute-start | bytes 98312 | tf_op jit(solution)/shard_map/ppermute | solution.py:30
  63.0 6.1 %collective-permute-start.14 = (bf16[16,1792]{1,0:T(8,128)(2,1)S(1)}, bf16[16,1792]{1,0:T(8,128)(2,1)S(1)}, u32[]{:S(2)}, u32[]{:S(2)}) collective-permute-start(bf16[16,1792]{1,0:T(8,128)(2,1)S(1)} %shard_map.115.refs_0_), channel_id=1, source_target_pairs={{0,12},{4,8},{8,4},{12,0},{1,13},{5,9},{9,5},{13,1},{2,14},{6,10},... | collective-permute-start | bytes 172040 | tf_op jit(solution)/shard_map/ppermute | solution.py:30
  65.5 6.5 %collective-permute-start.13 = (bf16[16,1792]{1,0:T(8,128)(2,1)S(1)}, bf16[16,1792]{1,0:T(8,128)(2,1)S(1)}, u32[]{:S(2)}, u32[]{:S(2)}) collective-permute-start(bf16[16,1792]{1,0:T(8,128)(2,1)S(1)} %shard_map.115.refs_0_), channel_id=1, source_target_pairs={{0,8},{4,12},{8,0},{12,4},{1,9},{5,13},{9,1},{13,5},{2,10},{6,14},... | collective-permute-start | bytes 172040 | tf_op jit(solution)/shard_map/ppermute | solution.py:30
  67.6 4.8 %collective-permute-start.12 = (bf16[16,1792]{1,0:T(8,128)(2,1)S(1)}, bf16[16,1792]{1,0:T(8,128)(2,1)S(1)}, u32[]{:S(2)}, u32[]{:S(2)}) collective-permute-start(bf16[16,1792]{1,0:T(8,128)(2,1)S(1)} %shard_map.115.refs_0_), channel_id=1, source_target_pairs={{0,4},{4,0},{8,12},{12,8},{1,5},{5,1},{9,13},{13,9},{2,6},{6,2},{1... | collective-permute-start | bytes 172040 | tf_op jit(solution)/shard_map/ppermute | solution.py:30
  73.7 1.3 %collective-permute-start.15 = (bf16[16,2432]{1,0:T(8,128)(2,1)S(1)}, bf16[16,2432]{1,0:T(8,128)(2,1)S(1)}, u32[]{:S(2)}, u32[]{:S(2)}) collective-permute-start(bf16[16,2432]{1,0:T(8,128)(2,1)S(1)} %get-tuple-element.55), channel_id=1, source_target_pairs={{0,1},{1,0},{2,3},{3,2},{4,5},{5,4},{6,7},{7,6},{8,9},{9,8},{10,11... | collective-permute-start | bytes 233480 | tf_op jit(solution)/shard_map/ppermute | solution.py:30
  75.1 4.7 %collective-permute-start.16 = (bf16[16,2432]{1,0:T(8,128)(2,1)S(1)}, bf16[16,2432]{1,0:T(8,128)(2,1)S(1)}, u32[]{:S(2)}, u32[]{:S(2)}) collective-permute-start(bf16[16,2432]{1,0:T(8,128)(2,1)S(1)} %get-tuple-element.57), channel_id=1, source_target_pairs={{0,2},{2,0},{1,3},{3,1},{4,6},{6,4},{5,7},{7,5},{8,10},{10,8},{9,1... | collective-permute-start | bytes 233480 | tf_op jit(solution)/shard_map/ppermute | solution.py:30
  80.0 4.1 %collective-permute-start.17 = (bf16[16,1152]{1,0:T(8,128)(2,1)S(1)}, bf16[16,1152]{1,0:T(8,128)(2,1)S(1)}, u32[]{:S(2)}, u32[]{:S(2)}) collective-permute-start(bf16[16,1152]{1,0:T(8,128)(2,1)S(1)} %shard_map.119.own_ref), channel_id=1, source_target_pairs={{0,1},{1,0},{2,3},{3,2},{4,5},{5,4},{6,7},{7,6},{8,9},{9,8},{10,11... | collective-permute-start | bytes 110600 | tf_op jit(solution)/shard_map/ppermute | solution.py:30
  84.8 4.5 %collective-permute-start.18 = (bf16[4,1792]{1,0:T(4,128)(2,1)S(1)}, bf16[4,1792]{1,0:T(4,128)(2,1)S(1)}, u32[]{:S(2)}, u32[]{:S(2)}) collective-permute-start(bf16[4,1792]{1,0:T(4,128)(2,1)S(1)} %get-tuple-element.60), channel_id=1, source_target_pairs={{0,4},{4,0},{8,12},{12,8},{1,5},{5,1},{9,13},{13,9},{2,6},{6,2},{1... | collective-permute-start | bytes 43016 | tf_op jit(solution)/shard_map/ppermute | solution.py:30
  85.7 4.7 %collective-permute-start.19 = (bf16[4,1792]{1,0:T(4,128)(2,1)S(1)}, bf16[4,1792]{1,0:T(4,128)(2,1)S(1)}, u32[]{:S(2)}, u32[]{:S(2)}) collective-permute-start(bf16[4,1792]{1,0:T(4,128)(2,1)S(1)} %get-tuple-element.61), channel_id=1, source_target_pairs={{0,8},{4,12},{8,0},{12,4},{1,9},{5,13},{9,1},{13,5},{2,10},{6,14},... | collective-permute-start | bytes 43016 | tf_op jit(solution)/shard_map/ppermute | solution.py:30
  88.8 5.5 %collective-permute-start.20 = (bf16[4,1792]{1,0:T(4,128)(2,1)S(1)}, bf16[4,1792]{1,0:T(4,128)(2,1)S(1)}, u32[]{:S(2)}, u32[]{:S(2)}) collective-permute-start(bf16[4,1792]{1,0:T(4,128)(2,1)S(1)} %get-tuple-element.62), channel_id=1, source_target_pairs={{0,12},{4,8},{8,4},{12,0},{1,13},{5,9},{9,5},{13,1},{2,14},{6,10},... | collective-permute-start | bytes 43016 | tf_op jit(solution)/shard_map/ppermute | solution.py:30

commit v2 on v1

--- a/solution.py
+++ b/solution.py
@@ -67,46 +67,47 @@
 
 def fetch(arrays, lengths=None, positions=None):
     count = len(arrays)
-    tables = 0 if positions is None else 1
-    rows = positions.shape[0] if tables else 0
-
-    def body(*refs):
-        sources, refs = refs[:count], refs[count:]
-        scalars, refs = refs[: 2 * tables], refs[2 * tables :]
+    scalars = [] if positions is None else [lengths, positions]
+    rows = positions.shape[0] if scalars else 0
+    copied = count + len(scalars)
+
+    def body(*refs):
+        sources, refs = refs[:copied], refs[copied:]
         targets, refs = refs[:count], refs[count:]
-        done = refs[-1]
+        done, in_smem = refs[-1], refs[-1 - len(scalars) : -1]
         copies = [
             pltpu.make_async_copy(source, target, done.at[i])
-            for i, (source, target) in enumerate(zip(sources, targets))
+            for i, (source, target) in enumerate(zip(sources, [*targets, *in_smem]))
         ]
-        for copy in copies:
+        for copy in reversed(copies):
             copy.start()
-        if tables:
-            length_ref, position_ref = scalars
+        for copy in copies[count:]:
+            copy.wait()
+        if scalars:
+            length_ref, position_ref = in_smem
             row = lax.broadcasted_iota(jnp.int32, (rows, LANES), 0)
             seen = jnp.zeros((rows, LANES), jnp.int32)
             for r in range(rows):
                 bound = jnp.minimum(length_ref[r // MTP], position_ref[r] + 1)
                 seen = jnp.where(row == r, bound, seen)
             refs[0][...] = seen
-        for copy in copies:
+        for copy in copies[:count]:
             copy.wait()
 
     moved = sum(2 * x.size * x.dtype.itemsize for x in arrays)
     return call(
         body,
         [pltpu.VMEM(x.shape, x.dtype) for x in arrays]
-        + [pltpu.VMEM((rows, LANES), jnp.int32)] * tables,
-        [pltpu.with_memory_space_constraint(x, pltpu.HBM) for x in arrays]
-        + [lengths, positions] * tables,
-        [IN_HBM] * count + [IN_SMEM] * (2 * tables),
-        [pltpu.SemaphoreType.DMA((count,))],
+        + ([pltpu.VMEM((rows, LANES), jnp.int32)] if scalars else []),
+        [pltpu.with_memory_space_constraint(x, pltpu.HBM) for x in [*arrays, *scalars]],
+        [IN_HBM] * copied,
+        [pltpu.SMEM(x.shape, x.dtype) for x in scalars] + [pltpu.SemaphoreType.DMA((copied,))],
         limit=1 << 20,
         cost=(0, moved),
     )
 
 
-def attend(groups, cache, seen):
+def attend(groups, cache, seen, weight, span):
     count = len(groups)
     rows, heads, width = groups[0].shape
     seqs, _, context = cache.shape
@@ -115,8 +116,11 @@
 
     def body(*refs):
         query_refs = refs[:count]
-        cache_ref, seen_ref = refs[count : count + 2]
-        out_refs = refs[count + 2 :]
+        cache_ref, seen_ref, weight_ref = refs[count : count + 3]
+        out_refs = refs[count + 3 : 2 * count + 3]
+        fetched, done = refs[2 * count + 3 :]
+        copy = pltpu.make_async_copy(weight_ref.at[pl.ds(span[0], span[1] - span[0])], fetched, done)
+        copy.start()
         offset = lax.axis_index("ctx") * context
         total = count * per_seq
         tops, sums = [[] for _ in range(count)], [[] for _ in range(count)]
@@ -153,14 +157,16 @@
             for i, part in enumerate(three_parts(table[:STAT_ROWS])):
                 out_refs[g][per_group:, i * LANES : (i + 1) * LANES] = part
             out_refs[g][per_group:, 3 * LANES :] = jnp.zeros((STAT_ROWS, LATENT - 3 * LANES), bf16)
+        copy.wait()
 
     shape = jax.ShapeDtypeStruct((per_group + STAT_ROWS, LATENT), bf16)
     flops = 2 * count * rows * heads * context * (width + LATENT)
     return call(
         body,
-        [shape] * count,
-        [*groups, in_vmem(cache), seen],
-        [IN_VMEM] * (count + 2),
+        [shape] * count + [pltpu.VMEM((span[1] - span[0], weight.shape[1]), weight.dtype)],
+        [*groups, in_vmem(cache), seen, pltpu.with_memory_space_constraint(weight, pltpu.HBM)],
+        [IN_VMEM] * (count + 2) + [IN_HBM],
+        [pltpu.SemaphoreType.DMA],
         limit=ATTEND_LIMIT,
         cost=(flops, 4 << 20),
     )
@@ -208,24 +214,29 @@
     )
 
 
-def project_out(pieces, weight):
-    count = len(pieces)
+def project_out(pieces, weights):
+    count, parts = len(pieces), len(weights)
     rows, depth = pieces[0].shape
-    width = weight.shape[1]
-
-    def body(*refs):
-        weight_ref, out_ref, placed = refs[count:]
+    width = weights[0].shape[1]
+
+    def body(*refs):
+        weight_refs, (out_ref, placed) = refs[count : count + parts], refs[count + parts :]
         me = lax.axis_index(("role", "seq"))
         for m in range(count):
             placed[me ^ m] = refs[m][...].astype(f32)
         values = jnp.concatenate([placed[k] for k in range(count)], axis=0).astype(bf16)
-        out_ref[...] = jnp.dot(values, weight_ref[...], preferred_element_type=f32).astype(bf16)
+        total, start = None, 0
+        for ref in weight_refs:
+            term = jnp.dot(values[:, start : start + ref.shape[0]], ref[...], preferred_element_type=f32)
+            total = term if total is None else total + term
+            start += ref.shape[0]
+        out_ref[...] = total.astype(bf16)
 
     return call(
         body,
         jax.ShapeDtypeStruct((count * rows, width), bf16),
-        [*pieces, in_vmem(weight)],
-        [IN_VMEM] * (count + 1),
+        [*pieces, *[in_vmem(weight) for weight in weights]],
+        [IN_VMEM] * (count + parts),
         [pltpu.VMEM((count, rows, depth), f32)],
         cost=(2 * count * rows * depth * width, 4 << 20),
     )
@@ -243,7 +254,7 @@
         residual_ref, gain_ref, gate_ref, up_ref = refs[count : count + 4]
         send_ref, scaled_ref, squares_ref, base_ref, placed = refs[count + 4 :]
         resid = residual_ref[...].astype(f32) + sum(ref[...].astype(f32) for ref in refs[:count])
-        scaled = (resid * gain_ref[...]).astype(bf16)
+        scaled = (resid * gain_ref[...][None, :]).astype(bf16)
         scaled_ref[...] = scaled
         other = lax.axis_index("seq") ^ 1
         for k in range(cores):
@@ -438,37 +449,45 @@
 
     evens, odds = range(2, blocks, 2), range(3, blocks, 2)
 
+    along = listed(exchange([value_up_weight] * roles, "role"))
     groups = exchange([queries] * blocks, "ctx", [*evens, 1])
-    along = listed(exchange([value_up_weight] * roles, "role"))
-    groups[0], cache_fast, up_own, out_fast, seen = fetch(
-        [queries, jnp.swapaxes(cache, 1, 2), value_up_weight, out_proj], lengths, positions
+    gate_fast, up_own, groups[0], cache_fast, seen = fetch(
+        [gate_weight, value_up_weight, queries, jnp.swapaxes(cache, 1, 2)], lengths, positions
     )
     relayed = {}
     for mask in evens:
         relayed[mask + 1] = xor_permute(groups[mask], "ctx", 1)
 
+    unit = out_proj.shape[0] // 16
+    cuts = [0, 5 * unit, 11 * unit, 16 * unit]
+    out_parts = []
+
     def attend_and_answer(source, masks):
-        outs = attend([source[mask] for mask in masks], cache_fast, seen)
+        k = len(out_parts)
+        *outs, part = attend(
+            [source[mask] for mask in masks], cache_fast, seen, out_proj, (cuts[k], cuts[k + 1])
+        )
+        out_parts.append(part)
         return dict(zip(masks, outs))
 
     partial = attend_and_answer(groups, evens)
     answers = exchange({0: None, **partial}, "ctx", evens)
     near = attend_and_answer(groups, [0, 1])
+    far = attend_and_answer(relayed, odds)
+    answers |= exchange({0: near[0], **far}, "ctx", odds)
     answers |= exchange(near, "ctx", [1])
-    far = attend_and_answer(relayed, odds)
-
-    gate_weight, up_weight, far[odds[0]] = lax.optimization_barrier((gate_weight, up_weight, far[odds[0]]))
-    answers |= exchange({0: near[0], **far}, "ctx", odds)
-    gate_fast, up_fast, residual, gain = fetch(
-        [gate_weight, up_weight, residual, norm_gain.reshape(1, -1)]
-    )
-    *along, gain = lax.optimization_barrier((*along, gain))
-    across = [xor_permute(piece, "seq", 1) for piece in along]
-    up_pieces = [up_own, *[piece for pair in zip(along, across) for piece in pair][1:]]
+
+    up_weight, part = lax.optimization_barrier((up_weight, out_parts[-1]))
+    out_parts[-1] = part
+    up_fast, residual, gain = fetch([up_weight, residual, norm_gain])
+    *far_rows, gain = lax.optimization_barrier((*along[1:], gain))
+    across = [xor_permute(along[0], "seq", 1)]
+    across += [xor_permute(piece, "seq", 1) for piece in far_rows]
+    up_pieces = [up_own, *[piece for pair in zip([None, *far_rows], across) for piece in pair][1:]]
 
     values = join_and_project(listed(answers), up_pieces, rows, heads, gain)
     shared = listed(exchange([values] * members, ("role", "seq")))
-    product = project_out(shared, out_fast)
+    product = project_out(shared, out_parts)
     down_weight, product = lax.optimization_barrier((down_weight, product))
     terms = listed(exchange([product] * blocks, "ctx"))
     (down_fast,) = fetch([down_weight])
@@ -501,6 +520,7 @@
         P("ctx", ("role", "seq")),
     )
 
+
     return jax.shard_map(
         per_device,
         mesh=mesh,

time: 95.1 us -> 84.5 us (0.89)
  waiting for transfers between devices: 37.2 us -> 29.8 us
  local copies, waits for them, and re-layouts: 2.62 us -> 0.01 us
  Pallas kernels: 29.5 us -> 27.1 us
  starting transfers between devices: 25.4 us -> 27.3 us
    ppermute x21, waiting for transfers between devices: 37.2 us -> 29.8 us  [xor_permute(): return lax.ppermute(x, axis, [(i, i ^ mask) for i in range(size)])]
    pallas_call x15, Pallas kernels: 29.5 us -> 27.1 us  [call(): pl.pallas_call(body, out_shape=outs, in_specs=specs, out_specs=jax.tree.m...]
    ppermute x21, starting transfers between devices: 25.4 us -> 27.3 us  [xor_permute(): return lax.ppermute(x, axis, [(i, i ^ mask) for i in range(size)])]
    unnamed x8 -> x2, local copies, waits for them, and re-layouts: 1.32 us -> 0.01 us
    reshape x1 -> x0, local copies, waits for them, and re-layouts: 1.29 us -> none  [per_device(): norm_gain.reshape(1, -1)]
  transfers between devices with their start and end apart: 21 -> 21, of which waited for: 12 -> 11; matrix products, arithmetic and copies ran while one was open for 1% -> 0% of each run, Pallas kernels for 24% -> 24%
where the time goes in v2:
time: 84.5 us; the launch traced here: 84.3 us
  waiting for transfers between devices  29.8 us (35%)
  starting transfers between devices  27.3 us (32%)
  Pallas kernels  27.1 us (32%)
    ppermute x21, waiting for transfers between devices, xor_permute(): return lax.ppermute(x, axis, [(i, i ^ mask) for i in range(size)])  29.8 us
    ppermute x21, starting transfers between devices, xor_permute(): return lax.ppermute(x, axis, [(i, i ^ mask) for i in range(size)])  27.3 us
    pallas_call x15, Pallas kernels, call(): pl.pallas_call(body, out_shape=outs, in_specs=specs, out_specs=jax.tree.m...  27.1 us
  transfers between devices with their start and end apart: 21, of which 11 were waited for; matrix products, arithmetic and copies ran while one was open for 0% of the time, Pallas kernels for 24%

profile of v2, /device:TPU:0, one launch (start us, length us, event | category | flops | bytes accessed | tf_op | source)
XLA Modules:
  0.0 84.3 jit_solution(16997550130243123918)
XLA Ops:
  0.0 3.0 %collective-permute-start.7 = (bf16[32,128,128]{2,1,0:T(8,128)(2,1)}, bf16[32,128,128]{2,1,0:T(8,128)(2,1)S(1)}, u32[]{:S(2)}, u32[]{:S(2)}) collective-permute-start(bf16[32,128,128]{2,1,0:T(8,128)(2,1)} %refs_1_.2), channel_id=1, source_target_pairs={{0,2},{2,0},{1,3},{3,1},{4,6},{6,4},{5,7},{7,5},{8,10},{10,8},{9,1... | collective-permute-start | bytes 3145736 | tf_op jit(solution)/shard_map/ppermute | solution.py:30
  3.0 2.6 %collective-permute-start.2 = (bf16[4,32,576]{2,1,0:T(8,128)(2,1)}, bf16[4,32,576]{2,1,0:T(8,128)(2,1)S(1)}, u32[]{:S(2)}, u32[]{:S(2)}) collective-permute-start(bf16[4,32,576]{2,1,0:T(8,128)(2,1)} %refs_2_.2), channel_id=1, source_target_pairs={{0,8},{4,12},{8,0},{12,4},{1,9},{5,13},{9,1},{13,5},{2,10},{6,14},... | collective-permute-start | bytes 442376 | tf_op jit(solution)/shard_map/ppermute | solution.py:30
  5.6 7.7 %collective-permute-done.2.refs_0_ = bf16[4,32,576]{2,1,0:T(8,128)(2,1)S(1)} collective-permute-done((bf16[4,32,576]{2,1,0:T(8,128)(2,1)}, bf16[4,32,576]{2,1,0:T(8,128)(2,1)S(1)}, u32[]{:S(2)}, u32[]{:S(2)}) %collective-permute-start.2) | collective-permute-done | bytes 147488 | tf_op jit(solution)/shard_map/ppermute | solution.py:30
  13.2 0.8 collective-permute-start.4
  14.0 0.0 collective-permute-start.6
  14.0 4.5 %shard_map.109 = (bf16[1792,2304]{1,0:T(8,128)(2,1)S(1)}, bf16[32,128,128]{2,1,0:T(8,128)(2,1)S(1)}, bf16[4,32,576]{2,1,0:T(8,128)(2,1)S(1)}, bf16[2,576,1024]{2,1,0:T(8,128)(2,1)S(1)}, s32[4,128]{1,0:T(4,128)S(1)}) custom-call(bf16[1792,2304]{1,0:T(8,128)(2,1)} %refs_0_.1, bf16[32,128,128]{2,1,0:T(8,128)(2,1)} %refs_1_.2, bf16[4,32,576]{2,1,0:T(8,128)(2,1)} %refs_2_.2, ...), custom_call_target="tpu_custom_call" | custom-call | bytes 23625728 | tf_op jit(solution)/shard_map/pallas_call | solution.py:46
  18.6 0.0 collective-permute-done.4.refs_0_
  18.6 2.3 %shard_map.112 = (bf16[136,512]{1,0:T(8,128)(2,1)S(1)}, bf16[1280,1792]{1,0:T(8,128)(2,1)S(1)}) custom-call(bf16[4,32,576]{2,1,0:T(8,128)(2,1)S(1)} %collective-permute-done.4.refs_0_, bf16[2,576,1024]{2,1,0:T(8,128)(2,1)S(1)} %get-tuple-element.37.refs_2_.refs_1_, s32[4,128]{1,0:T(4,128)S(1)} %get-tuple-element.38.refs_3_.refs_2_, bf16[4096,1792]{1,0:T(8,128)(2,1)} %refs_3_.3), custom_call_target="tpu_custom_call" | custom-call | flops 285212672 | bytes 4194304 | tf_op jit(solution)/shard_map/pallas_call | solution.py:46
  20.9 0.0 copy-start
  20.9 3.5 %shard_map.113 = (bf16[1792,2304]{1,0:T(8,128)(2,1)S(1)}, bf16[16,1792]{1,0:T(8,128)(2,1)S(1)}, f32[1792]{0:T(1024)S(1)}) custom-call(bf16[1792,2304]{1,0:T(8,128)(2,1)} %refs_0_.2, bf16[16,1792]{1,0:T(8,128)(2,1)} %refs_1_.3, f32[1792]{0:T(1024)} %refs_2_.3), custom_call_target="tpu_custom_call" | custom-call | bytes 16644096 | tf_op jit(solution)/shard_map/pallas_call | solution.py:46
  24.4 2.0 %collective-permute-done.7.refs_6_ = bf16[32,128,128]{2,1,0:T(8,128)(2,1)S(1)} collective-permute-done((bf16[32,128,128]{2,1,0:T(8,128)(2,1)}, bf16[32,128,128]{2,1,0:T(8,128)(2,1)S(1)}, u32[]{:S(2)}, u32[]{:S(2)}) %collective-permute-start.7) | collective-permute-done | bytes 1048608 | tf_op jit(solution)/shard_map/ppermute | solution.py:30
  26.3 0.0 collective-permute-start.8
  26.3 0.0 copy-done
  26.3 1.8 %collective-permute-start = (bf16[4,32,576]{2,1,0:T(8,128)(2,1)S(1)}, bf16[4,32,576]{2,1,0:T(8,128)(2,1)S(1)}, u32[]{:S(2)}, u32[]{:S(2)}) collective-permute-start(bf16[4,32,576]{2,1,0:T(8,128)(2,1)S(1)} %copy-done), channel_id=1, source_target_pairs={{0,4},{4,0},{8,12},{12,8},{1,5},{5,1},{9,13},{13,9},{2,6},{6,2},{1... | collective-permute-start | bytes 442376 | tf_op jit(solution)/shard_map/ppermute | solution.py:30
  28.2 2.3 %shard_map.111 = (bf16[136,512]{1,0:T(8,128)(2,1)S(1)}, bf16[1280,1792]{1,0:T(8,128)(2,1)S(1)}) custom-call(bf16[4,32,576]{2,1,0:T(8,128)(2,1)S(1)} %collective-permute-done.2.refs_0_, bf16[2,576,1024]{2,1,0:T(8,128)(2,1)S(1)} %get-tuple-element.37.refs_2_.refs_1_, s32[4,128]{1,0:T(4,128)S(1)} %get-tuple-element.38.refs_3_.refs_2_, bf16[4096,1792]{1,0:T(8,128)(2,1)} %refs_3_.3), custom_call_target="tpu_custom_call" | custom-call | flops 285212672 | bytes 4194304 | tf_op jit(solution)/shard_map/pallas_call | solution.py:46
  30.5 2.7 %collective-permute-start.3 = (bf16[136,512]{1,0:T(8,128)(2,1)S(1)}, bf16[136,512]{1,0:T(8,128)(2,1)S(1)}, u32[]{:S(2)}, u32[]{:S(2)}) collective-permute-start(bf16[136,512]{1,0:T(8,128)(2,1)S(1)} %get-tuple-element.41), channel_id=1, source_target_pairs={{0,8},{4,12},{8,0},{12,4},{1,9},{5,13},{9,1},{13,5},{2,10},{6,14},... | collective-permute-start | bytes 417800 | tf_op jit(solution)/shard_map/ppermute | solution.py:30
  33.1 0.0 collective-permute-done.refs_1_
  33.2 2.6 %shard_map.110 = (bf16[136,512]{1,0:T(8,128)(2,1)S(1)}, bf16[136,512]{1,0:T(8,128)(2,1)S(1)}, bf16[1536,1792]{1,0:T(8,128)(2,1)S(1)}) custom-call(bf16[4,32,576]{2,1,0:T(8,128)(2,1)S(1)} %get-tuple-element.36.refs_0_, bf16[4,32,576]{2,1,0:T(8,128)(2,1)S(1)} %collective-permute-done.refs_1_, bf16[2,576,1024]{2,1,0:T(8,128)(2,1)S(1)} %get-tuple-element.37.refs_2_.refs_1_, ...), custom_call_target="tpu_custom_call" | custom-call | flops 570425344 | bytes 4194304 | tf_op jit(solution)/shard_map/pallas_call | solution.py:46
  35.7 1.7 %collective-permute-start.1 = (bf16[136,512]{1,0:T(8,128)(2,1)S(1)}, bf16[136,512]{1,0:T(8,128)(2,1)S(1)}, u32[]{:S(2)}, u32[]{:S(2)}) collective-permute-start(bf16[136,512]{1,0:T(8,128)(2,1)S(1)} %get-tuple-element.40), channel_id=1, source_target_pairs={{0,4},{4,0},{8,12},{12,8},{1,5},{5,1},{9,13},{13,9},{2,6},{6,2},{1... | collective-permute-start | bytes 417800 | tf_op jit(solution)/shard_map/ppermute | solution.py:30
  37.4 2.9 %collective-permute-start.5 = (bf16[136,512]{1,0:T(8,128)(2,1)S(1)}, bf16[136,512]{1,0:T(8,128)(2,1)S(1)}, u32[]{:S(2)}, u32[]{:S(2)}) collective-permute-start(bf16[136,512]{1,0:T(8,128)(2,1)S(1)} %get-tuple-element.42), channel_id=1, source_target_pairs={{0,12},{4,8},{8,4},{12,0},{1,13},{5,9},{9,5},{13,1},{2,14},{6,10},... | collective-permute-start | bytes 417800 | tf_op jit(solution)/shard_map/ppermute | solution.py:30
  40.4 0.0 collective-permute-done.3.refs_2_
  40.4 5.9 %collective-permute-done.1.refs_1_ = bf16[136,512]{1,0:T(8,128)(2,1)S(1)} collective-permute-done((bf16[136,512]{1,0:T(8,128)(2,1)S(1)}, bf16[136,512]{1,0:T(8,128)(2,1)S(1)}, u32[]{:S(2)}, u32[]{:S(2)}) %collective-permute-start.1) | collective-permute-done | bytes 139296 | tf_op jit(solution)/shard_map/ppermute | solution.py:30
  46.2 0.0 collective-permute-done.5.refs_3_
  46.2 0.0 collective-permute-done.6.refs_5_
  46.2 0.0 collective-permute-done.8.refs_7_
  46.2 1.7 %shard_map.114.refs_0_ = bf16[4,4096]{1,0:T(4,128)(2,1)S(1)} custom-call(bf16[136,512]{1,0:T(8,128)(2,1)S(1)} %get-tuple-element.39.refs_0_, bf16[136,512]{1,0:T(8,128)(2,1)S(1)} %collective-permute-done.1.refs_1_, bf16[136,512]{1,0:T(8,128)(2,1)S(1)} %collective-permute-done.3.refs_2_, bf16[136,512]{1,0:T(8,128)(2,1)S(1)} %collective-permute-done.5.refs_3_, ...), custom_call_target="tpu_custom_call" | custom-call | flops 16777216 | bytes 4194304 | tf_op jit(solution)/shard_map/pallas_call | solution.py:46
  47.9 1.1 %collective-permute-start.11 = (bf16[4,4096]{1,0:T(4,128)(2,1)S(1)}, bf16[4,4096]{1,0:T(4,128)(2,1)S(1)}, u32[]{:S(2)}, u32[]{:S(2)}) collective-permute-start(bf16[4,4096]{1,0:T(4,128)(2,1)S(1)} %shard_map.114.refs_0_), channel_id=1, source_target_pairs={{0,3},{1,2},{2,1},{3,0},{4,7},{5,6},{6,5},{7,4},{8,11},{9,10},{10,... | collective-permute-start | bytes 98312 | tf_op jit(solution)/shard_map/ppermute | solution.py:30
  49.0 0.5 collective-permute-start.10
  49.6 0.2 collective-permute-start.9
  49.8 1.6 %collective-permute-done.11.refs_3_ = bf16[4,4096]{1,0:T(4,128)(2,1)S(1)} collective-permute-done((bf16[4,4096]{1,0:T(4,128)(2,1)S(1)}, bf16[4,4096]{1,0:T(4,128)(2,1)S(1)}, u32[]{:S(2)}, u32[]{:S(2)}) %collective-permute-start.11) | collective-permute-done | bytes 32800 | tf_op jit(solution)/shard_map/ppermute | solution.py:30
  51.4 1.5 %collective-permute-done.10.refs_2_ = bf16[4,4096]{1,0:T(4,128)(2,1)S(1)} collective-permute-done((bf16[4,4096]{1,0:T(4,128)(2,1)S(1)}, bf16[4,4096]{1,0:T(4,128)(2,1)S(1)}, u32[]{:S(2)}, u32[]{:S(2)}) %collective-permute-start.10) | collective-permute-done | bytes 32800 | tf_op jit(solution)/shard_map/ppermute | solution.py:30
  52.9 0.0 collective-permute-done.9.refs_1_
  52.9 2.0 %shard_map.115.refs_0_ = bf16[16,1792]{1,0:T(8,128)(2,1)S(1)} custom-call(bf16[4,4096]{1,0:T(4,128)(2,1)S(1)} %shard_map.114.refs_0_, bf16[4,4096]{1,0:T(4,128)(2,1)S(1)} %collective-permute-done.9.refs_1_, bf16[4,4096]{1,0:T(4,128)(2,1)S(1)} %collective-permute-done.10.refs_2_, bf16[4,4096]{1,0:T(4,128)(2,1)S(1)} %collective-permute-done.11.refs_3_, ...), custom_call_target="tpu_custom_call" | custom-call | flops 234881024 | bytes 4194304 | tf_op jit(solution)/shard_map/pallas_call | solution.py:46
  55.0 2.4 %collective-permute-start.14 = (bf16[16,1792]{1,0:T(8,128)(2,1)S(1)}, bf16[16,1792]{1,0:T(8,128)(2,1)S(1)}, u32[]{:S(2)}, u32[]{:S(2)}) collective-permute-start(bf16[16,1792]{1,0:T(8,128)(2,1)S(1)} %shard_map.115.refs_0_), channel_id=1, source_target_pairs={{0,12},{4,8},{8,4},{12,0},{1,13},{5,9},{9,5},{13,1},{2,14},{6,10},... | collective-permute-start | bytes 172040 | tf_op jit(solution)/shard_map/ppermute | solution.py:30
  57.3 0.0 collective-permute-start.13
  57.3 2.0 %collective-permute-start.12 = (bf16[16,1792]{1,0:T(8,128)(2,1)S(1)}, bf16[16,1792]{1,0:T(8,128)(2,1)S(1)}, u32[]{:S(2)}, u32[]{:S(2)}) collective-permute-start(bf16[16,1792]{1,0:T(8,128)(2,1)S(1)} %shard_map.115.refs_0_), channel_id=1, source_target_pairs={{0,4},{4,0},{8,12},{12,8},{1,5},{5,1},{9,13},{13,9},{2,6},{6,2},{1... | collective-permute-start | bytes 172040 | tf_op jit(solution)/shard_map/ppermute | solution.py:30
  59.4 1.7 %collective-permute-done.14.refs_3_ = bf16[16,1792]{1,0:T(8,128)(2,1)S(1)} collective-permute-done((bf16[16,1792]{1,0:T(8,128)(2,1)S(1)}, bf16[16,1792]{1,0:T(8,128)(2,1)S(1)}, u32[]{:S(2)}, u32[]{:S(2)}) %collective-permute-start.14) | collective-permute-done | bytes 57376 | tf_op jit(solution)/shard_map/ppermute | solution.py:30
  61.0 1.8 %collective-permute-done.13.refs_2_ = bf16[16,1792]{1,0:T(8,128)(2,1)S(1)} collective-permute-done((bf16[16,1792]{1,0:T(8,128)(2,1)S(1)}, bf16[16,1792]{1,0:T(8,128)(2,1)S(1)}, u32[]{:S(2)}, u32[]{:S(2)}) %collective-permute-start.13) | collective-permute-done | bytes 57376 | tf_op jit(solution)/shard_map/ppermute | solution.py:30
  62.8 0.0 collective-permute-done.12.refs_1_
  62.8 1.3 %shard_map.116 = (bf16[16,2432]{1,0:T(8,128)(2,1)S(1)}, bf16[16,1792]{1,0:T(8,128)(2,1)S(1)}, f32[16,128]{1,0:T(8,128)S(1)}, f32[4,1792]{1,0:T(4,128)S(1)}) custom-call(bf16[16,1792]{1,0:T(8,128)(2,1)S(1)} %shard_map.115.refs_0_, bf16[16,1792]{1,0:T(8,128)(2,1)S(1)} %collective-permute-done.12.refs_1_, bf16[16,1792]{1,0:T(8,128)(2,1)S(1)} %collective-permute-done.13.refs_2_, ...), custom_call_target="tpu_custom_call" | custom-call | flops 132120576 | bytes 4194304 | tf_op jit(solution)/shard_map/pallas_call | solution.py:46
  64.1 0.0 collective-permute-start.15
  64.1 1.2 %shard_map.117.keep_ref = f32[16,2304]{1,0:T(8,128)S(1)} custom-call(bf16[16,1792]{1,0:T(8,128)(2,1)S(1)} %get-tuple-element.57.scaled_ref, bf16[1792,2304]{1,0:T(8,128)(2,1)S(1)} %get-tuple-element.54.refs_6_.gate_ref, bf16[1792,2304]{1,0:T(8,128)(2,1)S(1)} %get-tuple-element.55.refs_7_.up_ref), custom_call_target="tpu_custom_call" | custom-call | flops 132120576 | bytes 4194304 | tf_op jit(solution)/shard_map/pallas_call | solution.py:46
  65.3 0.1 collective-permute-done.15.got_ref
  65.4 0.2 shard_map.118
  65.6 1.1 %collective-permute-start.16 = (bf16[16,2432]{1,0:T(8,128)(2,1)S(1)}, bf16[16,2432]{1,0:T(8,128)(2,1)S(1)}, u32[]{:S(2)}, u32[]{:S(2)}) collective-permute-start(bf16[16,2432]{1,0:T(8,128)(2,1)S(1)} %get-tuple-element.61), channel_id=1, source_target_pairs={{0,2},{2,0},{1,3},{3,1},{4,6},{6,4},{5,7},{7,5},{8,10},{10,8},{9,1... | collective-permute-start | bytes 233480 | tf_op jit(solution)/shard_map/ppermute | solution.py:30
  66.6 3.7 %collective-permute-done.16.refs_1_ = bf16[16,2432]{1,0:T(8,128)(2,1)S(1)} collective-permute-done((bf16[16,2432]{1,0:T(8,128)(2,1)S(1)}, bf16[16,2432]{1,0:T(8,128)(2,1)S(1)}, u32[]{:S(2)}, u32[]{:S(2)}) %collective-permute-start.16) | collective-permute-done | bytes 77856 | tf_op jit(solution)/shard_map/ppermute | solution.py:30
  70.3 0.2 shard_map.119.own_ref
  70.5 0.1 collective-permute-start.17
  70.6 3.4 %shard_map.120.weight_ref = bf16[2304,1792]{1,0:T(8,128)(2,1)S(1)} custom-call(bf16[2304,1792]{1,0:T(8,128)(2,1)} %refs_0_.3), custom_call_target="tpu_custom_call" | custom-call | bytes 16515072 | tf_op jit(solution)/shard_map/pallas_call | solution.py:46
  73.9 0.7 shard_map.121.partial_ref
  74.6 0.0 collective-permute-done.17.other_ref
  74.6 0.7 shard_map.122
  75.3 0.8 collective-permute-start.18
  76.1 2.1 %collective-permute-start.19 = (bf16[4,1792]{1,0:T(4,128)(2,1)S(1)}, bf16[4,1792]{1,0:T(4,128)(2,1)S(1)}, u32[]{:S(2)}, u32[]{:S(2)}) collective-permute-start(bf16[4,1792]{1,0:T(4,128)(2,1)S(1)} %get-tuple-element.65), channel_id=1, source_target_pairs={{0,8},{4,12},{8,0},{12,4},{1,9},{5,13},{9,1},{13,5},{2,10},{6,14},... | collective-permute-start | bytes 43016 | tf_op jit(solution)/shard_map/ppermute | solution.py:30
  78.2 1.6 %collective-permute-start.20 = (bf16[4,1792]{1,0:T(4,128)(2,1)S(1)}, bf16[4,1792]{1,0:T(4,128)(2,1)S(1)}, u32[]{:S(2)}, u32[]{:S(2)}) collective-permute-start(bf16[4,1792]{1,0:T(4,128)(2,1)S(1)} %get-tuple-element.66), channel_id=1, source_target_pairs={{0,12},{4,8},{8,4},{12,0},{1,13},{5,9},{9,5},{13,1},{2,14},{6,10},... | collective-permute-start | bytes 43016 | tf_op jit(solution)/shard_map/ppermute | solution.py:30
  79.7 0.0 collective-permute-done.18.refs_2_
  79.7 1.1 %collective-permute-done.19.refs_3_ = bf16[4,1792]{1,0:T(4,128)(2,1)S(1)} collective-permute-done((bf16[4,1792]{1,0:T(4,128)(2,1)S(1)}, bf16[4,1792]{1,0:T(4,128)(2,1)S(1)}, u32[]{:S(2)}, u32[]{:S(2)}) %collective-permute-start.19) | collective-permute-done | bytes 14368 | tf_op jit(solution)/shard_map/ppermute | solution.py:30
  80.8 2.9 %collective-permute-done.20.refs_4_ = bf16[4,1792]{1,0:T(4,128)(2,1)S(1)} collective-permute-done((bf16[4,1792]{1,0:T(4,128)(2,1)S(1)}, bf16[4,1792]{1,0:T(4,128)(2,1)S(1)}, u32[]{:S(2)}, u32[]{:S(2)}) %collective-permute-start.20) | collective-permute-done | bytes 14368 | tf_op jit(solution)/shard_map/ppermute | solution.py:30
  83.7 0.6 shard_map.123
Async XLA Ops:
  0.0 26.3 %collective-permute-start.7 = (bf16[32,128,128]{2,1,0:T(8,128)(2,1)}, bf16[32,128,128]{2,1,0:T(8,128)(2,1)S(1)}, u32[]{:S(2)}, u32[]{:S(2)}) collective-permute-start(bf16[32,128,128]{2,1,0:T(8,128)(2,1)} %refs_1_.2), channel_id=1, source_target_pairs={{0,2},{2,0},{1,3},{3,1},{4,6},{6,4},{5,7},{7,5},{8,10},{10,8},{9,1... | collective-permute-start | bytes 3145736 | tf_op jit(solution)/shard_map/ppermute | solution.py:30
  3.0 10.3 %collective-permute-start.2 = (bf16[4,32,576]{2,1,0:T(8,128)(2,1)}, bf16[4,32,576]{2,1,0:T(8,128)(2,1)S(1)}, u32[]{:S(2)}, u32[]{:S(2)}) collective-permute-start(bf16[4,32,576]{2,1,0:T(8,128)(2,1)} %refs_2_.2), channel_id=1, source_target_pairs={{0,8},{4,12},{8,0},{12,4},{1,9},{5,13},{9,1},{13,5},{2,10},{6,14},... | collective-permute-start | bytes 442376 | tf_op jit(solution)/shard_map/ppermute | solution.py:30
  13.2 5.3 %collective-permute-start.4 = (bf16[4,32,576]{2,1,0:T(8,128)(2,1)S(1)}, bf16[4,32,576]{2,1,0:T(8,128)(2,1)S(1)}, u32[]{:S(2)}, u32[]{:S(2)}) collective-permute-start(bf16[4,32,576]{2,1,0:T(8,128)(2,1)S(1)} %collective-permute-done.2.refs_0_), channel_id=1, source_target_pairs={{0,4},{4,0},{8,12},{12,8},{1,5},{5,1},{9,13},{13,9},{2,6},{6,2},{1... | collective-permute-start | bytes 442376 | tf_op jit(solution)/shard_map/ppermute | solution.py:30
  14.0 32.2 %collective-permute-start.6 = (bf16[32,128,128]{2,1,0:T(8,128)(2,1)}, bf16[32,128,128]{2,1,0:T(8,128)(2,1)S(1)}, u32[]{:S(2)}, u32[]{:S(2)}) collective-permute-start(bf16[32,128,128]{2,1,0:T(8,128)(2,1)} %refs_1_.2), channel_id=1, source_target_pairs={{0,1},{1,0},{2,3},{3,2},{4,5},{5,4},{6,7},{7,6},{8,9},{9,8},{10,11... | collective-permute-start | bytes 3145736 | tf_op jit(solution)/shard_map/ppermute | solution.py:30
  20.9 5.4 %copy-start = (bf16[4,32,576]{2,1,0:T(8,128)(2,1)S(1)}, bf16[4,32,576]{2,1,0:T(8,128)(2,1)}, u32[]{:S(2)}) copy-start(bf16[4,32,576]{2,1,0:T(8,128)(2,1)} %refs_2_.2) | copy-start | bytes 442372
  26.3 19.9 %collective-permute-start.8 = (bf16[32,128,128]{2,1,0:T(8,128)(2,1)S(1)}, bf16[32,128,128]{2,1,0:T(8,128)(2,1)S(1)}, u32[]{:S(2)}, u32[]{:S(2)}) collective-permute-start(bf16[32,128,128]{2,1,0:T(8,128)(2,1)S(1)} %collective-permute-done.7.refs_6_), channel_id=1, source_target_pairs={{0,1},{1,0},{2,3},{3,2},{4,5},{5,4},{6,7},{7,6},{8,9},{9,8},{10,11... | collective-permute-start | bytes 3145736 | tf_op jit(solution)/shard_map/ppermute | solution.py:30
  26.3 6.8 %collective-permute-start = (bf16[4,32,576]{2,1,0:T(8,128)(2,1)S(1)}, bf16[4,32,576]{2,1,0:T(8,128)(2,1)S(1)}, u32[]{:S(2)}, u32[]{:S(2)}) collective-permute-start(bf16[4,32,576]{2,1,0:T(8,128)(2,1)S(1)} %copy-done), channel_id=1, source_target_pairs={{0,4},{4,0},{8,12},{12,8},{1,5},{5,1},{9,13},{13,9},{2,6},{6,2},{1... | collective-permute-start | bytes 442376 | tf_op jit(solution)/shard_map/ppermute | solution.py:30
  30.5 9.9 %collective-permute-start.3 = (bf16[136,512]{1,0:T(8,128)(2,1)S(1)}, bf16[136,512]{1,0:T(8,128)(2,1)S(1)}, u32[]{:S(2)}, u32[]{:S(2)}) collective-permute-start(bf16[136,512]{1,0:T(8,128)(2,1)S(1)} %get-tuple-element.41), channel_id=1, source_target_pairs={{0,8},{4,12},{8,0},{12,4},{1,9},{5,13},{9,1},{13,5},{2,10},{6,14},... | collective-permute-start | bytes 417800 | tf_op jit(solution)/shard_map/ppermute | solution.py:30
  35.7 10.5 %collective-permute-start.1 = (bf16[136,512]{1,0:T(8,128)(2,1)S(1)}, bf16[136,512]{1,0:T(8,128)(2,1)S(1)}, u32[]{:S(2)}, u32[]{:S(2)}) collective-permute-start(bf16[136,512]{1,0:T(8,128)(2,1)S(1)} %get-tuple-element.40), channel_id=1, source_target_pairs={{0,4},{4,0},{8,12},{12,8},{1,5},{5,1},{9,13},{13,9},{2,6},{6,2},{1... | collective-permute-start | bytes 417800 | tf_op jit(solution)/shard_map/ppermute | solution.py:30
  37.4 8.8 %collective-permute-start.5 = (bf16[136,512]{1,0:T(8,128)(2,1)S(1)}, bf16[136,512]{1,0:T(8,128)(2,1)S(1)}, u32[]{:S(2)}, u32[]{:S(2)}) collective-permute-start(bf16[136,512]{1,0:T(8,128)(2,1)S(1)} %get-tuple-element.42), channel_id=1, source_target_pairs={{0,12},{4,8},{8,4},{12,0},{1,13},{5,9},{9,5},{13,1},{2,14},{6,10},... | collective-permute-start | bytes 417800 | tf_op jit(solution)/shard_map/ppermute | solution.py:30
  47.9 3.5 %collective-permute-start.11 = (bf16[4,4096]{1,0:T(4,128)(2,1)S(1)}, bf16[4,4096]{1,0:T(4,128)(2,1)S(1)}, u32[]{:S(2)}, u32[]{:S(2)}) collective-permute-start(bf16[4,4096]{1,0:T(4,128)(2,1)S(1)} %shard_map.114.refs_0_), channel_id=1, source_target_pairs={{0,3},{1,2},{2,1},{3,0},{4,7},{5,6},{6,5},{7,4},{8,11},{9,10},{10,... | collective-permute-start | bytes 98312 | tf_op jit(solution)/shard_map/ppermute | solution.py:30
  49.0 3.9 %collective-permute-start.10 = (bf16[4,4096]{1,0:T(4,128)(2,1)S(1)}, bf16[4,4096]{1,0:T(4,128)(2,1)S(1)}, u32[]{:S(2)}, u32[]{:S(2)}) collective-permute-start(bf16[4,4096]{1,0:T(4,128)(2,1)S(1)} %shard_map.114.refs_0_), channel_id=1, source_target_pairs={{0,2},{1,3},{2,0},{3,1},{4,6},{5,7},{6,4},{7,5},{8,10},{9,11},{10,... | collective-permute-start | bytes 98312 | tf_op jit(solution)/shard_map/ppermute | solution.py:30
  49.6 3.4 %collective-permute-start.9 = (bf16[4,4096]{1,0:T(4,128)(2,1)S(1)}, bf16[4,4096]{1,0:T(4,128)(2,1)S(1)}, u32[]{:S(2)}, u32[]{:S(2)}) collective-permute-start(bf16[4,4096]{1,0:T(4,128)(2,1)S(1)} %shard_map.114.refs_0_), channel_id=1, source_target_pairs={{0,1},{1,0},{2,3},{3,2},{4,5},{5,4},{6,7},{7,6},{8,9},{9,8},{10,11... | collective-permute-start | bytes 98312 | tf_op jit(solution)/shard_map/ppermute | solution.py:30
  55.0 6.0 %collective-permute-start.14 = (bf16[16,1792]{1,0:T(8,128)(2,1)S(1)}, bf16[16,1792]{1,0:T(8,128)(2,1)S(1)}, u32[]{:S(2)}, u32[]{:S(2)}) collective-permute-start(bf16[16,1792]{1,0:T(8,128)(2,1)S(1)} %shard_map.115.refs_0_), channel_id=1, source_target_pairs={{0,12},{4,8},{8,4},{12,0},{1,13},{5,9},{9,5},{13,1},{2,14},{6,10},... | collective-permute-start | bytes 172040 | tf_op jit(solution)/shard_map/ppermute | solution.py:30
  57.3 5.5 %collective-permute-start.13 = (bf16[16,1792]{1,0:T(8,128)(2,1)S(1)}, bf16[16,1792]{1,0:T(8,128)(2,1)S(1)}, u32[]{:S(2)}, u32[]{:S(2)}) collective-permute-start(bf16[16,1792]{1,0:T(8,128)(2,1)S(1)} %shard_map.115.refs_0_), channel_id=1, source_target_pairs={{0,8},{4,12},{8,0},{12,4},{1,9},{5,13},{9,1},{13,5},{2,10},{6,14},... | collective-permute-start | bytes 172040 | tf_op jit(solution)/shard_map/ppermute | solution.py:30
  57.3 5.5 %collective-permute-start.12 = (bf16[16,1792]{1,0:T(8,128)(2,1)S(1)}, bf16[16,1792]{1,0:T(8,128)(2,1)S(1)}, u32[]{:S(2)}, u32[]{:S(2)}) collective-permute-start(bf16[16,1792]{1,0:T(8,128)(2,1)S(1)} %shard_map.115.refs_0_), channel_id=1, source_target_pairs={{0,4},{4,0},{8,12},{12,8},{1,5},{5,1},{9,13},{13,9},{2,6},{6,2},{1... | collective-permute-start | bytes 172040 | tf_op jit(solution)/shard_map/ppermute | solution.py:30
  64.1 1.3 %collective-permute-start.15 = (bf16[16,2432]{1,0:T(8,128)(2,1)S(1)}, bf16[16,2432]{1,0:T(8,128)(2,1)S(1)}, u32[]{:S(2)}, u32[]{:S(2)}) collective-permute-start(bf16[16,2432]{1,0:T(8,128)(2,1)S(1)} %get-tuple-element.59), channel_id=1, source_target_pairs={{0,1},{1,0},{2,3},{3,2},{4,5},{5,4},{6,7},{7,6},{8,9},{9,8},{10,11... | collective-permute-start | bytes 233480 | tf_op jit(solution)/shard_map/ppermute | solution.py:30
  65.6 4.7 %collective-permute-start.16 = (bf16[16,2432]{1,0:T(8,128)(2,1)S(1)}, bf16[16,2432]{1,0:T(8,128)(2,1)S(1)}, u32[]{:S(2)}, u32[]{:S(2)}) collective-permute-start(bf16[16,2432]{1,0:T(8,128)(2,1)S(1)} %get-tuple-element.61), channel_id=1, source_target_pairs={{0,2},{2,0},{1,3},{3,1},{4,6},{6,4},{5,7},{7,5},{8,10},{10,8},{9,1... | collective-permute-start | bytes 233480 | tf_op jit(solution)/shard_map/ppermute | solution.py:30
  70.5 4.1 %collective-permute-start.17 = (bf16[16,1152]{1,0:T(8,128)(2,1)S(1)}, bf16[16,1152]{1,0:T(8,128)(2,1)S(1)}, u32[]{:S(2)}, u32[]{:S(2)}) collective-permute-start(bf16[16,1152]{1,0:T(8,128)(2,1)S(1)} %shard_map.119.own_ref), channel_id=1, source_target_pairs={{0,1},{1,0},{2,3},{3,2},{4,5},{5,4},{6,7},{7,6},{8,9},{9,8},{10,11... | collective-permute-start | bytes 110600 | tf_op jit(solution)/shard_map/ppermute | solution.py:30
  75.3 4.5 %collective-permute-start.18 = (bf16[4,1792]{1,0:T(4,128)(2,1)S(1)}, bf16[4,1792]{1,0:T(4,128)(2,1)S(1)}, u32[]{:S(2)}, u32[]{:S(2)}) collective-permute-start(bf16[4,1792]{1,0:T(4,128)(2,1)S(1)} %get-tuple-element.64), channel_id=1, source_target_pairs={{0,4},{4,0},{8,12},{12,8},{1,5},{5,1},{9,13},{13,9},{2,6},{6,2},{1... | collective-permute-start | bytes 43016 | tf_op jit(solution)/shard_map/ppermute | solution.py:30
  76.1 4.7 %collective-permute-start.19 = (bf16[4,1792]{1,0:T(4,128)(2,1)S(1)}, bf16[4,1792]{1,0:T(4,128)(2,1)S(1)}, u32[]{:S(2)}, u32[]{:S(2)}) collective-permute-start(bf16[4,1792]{1,0:T(4,128)(2,1)S(1)} %get-tuple-element.65), channel_id=1, source_target_pairs={{0,8},{4,12},{8,0},{12,4},{1,9},{5,13},{9,1},{13,5},{2,10},{6,14},... | collective-permute-start | bytes 43016 | tf_op jit(solution)/shard_map/ppermute | solution.py:30
  78.2 5.5 %collective-permute-start.20 = (bf16[4,1792]{1,0:T(4,128)(2,1)S(1)}, bf16[4,1792]{1,0:T(4,128)(2,1)S(1)}, u32[]{:S(2)}, u32[]{:S(2)}) collective-permute-start(bf16[4,1792]{1,0:T(4,128)(2,1)S(1)} %get-tuple-element.66), channel_id=1, source_target_pairs={{0,12},{4,8},{8,4},{12,0},{1,13},{5,9},{9,5},{13,1},{2,14},{6,10},... | collective-permute-start | bytes 43016 | tf_op jit(solution)/shard_map/ppermute | solution.py:30

commit v3 on v2

--- a/solution.py
+++ b/solution.py
@@ -1,4 +1,5 @@
 import functools
+import math
 
 import jax
 import jax.numpy as jnp
@@ -66,6 +67,9 @@
 
 
 def fetch(arrays, lengths=None, positions=None):
+    spans = [x[1] if isinstance(x, tuple) else (0, x.shape[0]) for x in arrays]
+    arrays = [x[0] if isinstance(x, tuple) else x for x in arrays]
+    shapes = [(last - first, *x.shape[1:]) for x, (first, last) in zip(arrays, spans)]
     count = len(arrays)
     scalars = [] if positions is None else [lengths, positions]
     rows = positions.shape[0] if scalars else 0
@@ -74,6 +78,10 @@
     def body(*refs):
         sources, refs = refs[:copied], refs[copied:]
         targets, refs = refs[:count], refs[count:]
+        sources = [
+            source if i >= count or spans[i] == (0, source.shape[0]) else source.at[pl.ds(spans[i][0], shapes[i][0])]
+            for i, source in enumerate(sources)
+        ]
         done, in_smem = refs[-1], refs[-1 - len(scalars) : -1]
         copies = [
             pltpu.make_async_copy(source, target, done.at[i])
@@ -94,10 +102,10 @@
         for copy in copies[:count]:
             copy.wait()
 
-    moved = sum(2 * x.size * x.dtype.itemsize for x in arrays)
-    return call(
-        body,
-        [pltpu.VMEM(x.shape, x.dtype) for x in arrays]
+    moved = sum(2 * math.prod(shape) * x.dtype.itemsize for shape, x in zip(shapes, arrays))
+    return call(
+        body,
+        [pltpu.VMEM(shape, x.dtype) for shape, x in zip(shapes, arrays)]
         + ([pltpu.VMEM((rows, LANES), jnp.int32)] if scalars else []),
         [pltpu.with_memory_space_constraint(x, pltpu.HBM) for x in [*arrays, *scalars]],
         [IN_HBM] * copied,
@@ -451,51 +459,49 @@
 
     along = listed(exchange([value_up_weight] * roles, "role"))
     groups = exchange([queries] * blocks, "ctx", [*evens, 1])
-    gate_fast, up_own, groups[0], cache_fast, seen = fetch(
-        [gate_weight, value_up_weight, queries, jnp.swapaxes(cache, 1, 2)], lengths, positions
-    )
+    unit = out_proj.shape[0] // 16
+    own_span, early_span, even_span, odd_span, late_span = [
+        (unit * first, unit * last) for first, last in ((0, 2), (2, 9), (9, 11), (11, 13), (13, 16))
+    ]
+    groups[0], cache_fast, seen = fetch([queries, jnp.swapaxes(cache, 1, 2)], lengths, positions)
+
+    def attend_some(source, span):
+        *outs, part = attend(list(source.values()), cache_fast, seen, out_proj, span)
+        return dict(zip(source, outs)), part
+
+    answers, own_part = attend_some({0: groups[0]}, own_span)
+    (early_part,) = fetch([(out_proj, early_span)])
     relayed = {}
     for mask in evens:
         relayed[mask + 1] = xor_permute(groups[mask], "ctx", 1)
-
-    unit = out_proj.shape[0] // 16
-    cuts = [0, 5 * unit, 11 * unit, 16 * unit]
-    out_parts = []
-
-    def attend_and_answer(source, masks):
-        k = len(out_parts)
-        *outs, part = attend(
-            [source[mask] for mask in masks], cache_fast, seen, out_proj, (cuts[k], cuts[k + 1])
-        )
-        out_parts.append(part)
-        return dict(zip(masks, outs))
-
-    partial = attend_and_answer(groups, evens)
-    answers = exchange({0: None, **partial}, "ctx", evens)
-    near = attend_and_answer(groups, [0, 1])
-    far = attend_and_answer(relayed, odds)
-    answers |= exchange({0: near[0], **far}, "ctx", odds)
-    answers |= exchange(near, "ctx", [1])
-
-    up_weight, part = lax.optimization_barrier((up_weight, out_parts[-1]))
-    out_parts[-1] = part
-    up_fast, residual, gain = fetch([up_weight, residual, norm_gain])
+    even, even_part = attend_some({mask: groups[mask] for mask in evens}, even_span)
+    answers |= exchange({0: answers[0], **even}, "ctx", evens)
+    far, odd_part = attend_some({**relayed, 1: groups[1]}, odd_span)
+    answers |= exchange({0: answers[0], **far}, "ctx", odds)
+    answers |= exchange({0: answers[0], **far}, "ctx", [1])
+
+    late_part, gate_fast, up_own, residual, gain = fetch(
+        [(out_proj, late_span), gate_weight, value_up_weight, residual, norm_gain]
+    )
     *far_rows, gain = lax.optimization_barrier((*along[1:], gain))
     across = [xor_permute(along[0], "seq", 1)]
     across += [xor_permute(piece, "seq", 1) for piece in far_rows]
     up_pieces = [up_own, *[piece for pair in zip([None, *far_rows], across) for piece in pair][1:]]
+    out_parts = [own_part, early_part, even_part, odd_part, late_part]
 
     values = join_and_project(listed(answers), up_pieces, rows, heads, gain)
     shared = listed(exchange([values] * members, ("role", "seq")))
     product = project_out(shared, out_parts)
-    down_weight, product = lax.optimization_barrier((down_weight, product))
+    up_weight, product = lax.optimization_barrier((up_weight, product))
     terms = listed(exchange([product] * blocks, "ctx"))
-    (down_fast,) = fetch([down_weight])
+    (up_fast,) = fetch([up_weight])
 
     send, scaled, squares, base = gate_and_up_away(terms, residual, gain, gate_fast, up_fast)
     got = xor_permute(send, "seq", 1)
     keep = gate_and_up_here(scaled, gate_fast, up_fast)
     keep, send = add_core(keep, squares, got)
+    down_weight, send = lax.optimization_barrier((down_weight, send))
+    (down_fast,) = fetch([down_weight])
     pieces = listed(exchange([send] * roles, "role"))[1:]
     features = norm_gain.shape[0] * members
     hidden = activate(keep, pieces, features)

time: 84.5 us -> 96.3 us (1.14)
  waiting for transfers between devices: 29.8 us -> 40 us
  Pallas kernels: 27.1 us -> 29.2 us
    ppermute x21, waiting for transfers between devices: 29.8 us -> 40 us  [xor_permute(): return lax.ppermute(x, axis, [(i, i ^ mask) for i in range(size)])]
    pallas_call x15 -> x17, Pallas kernels: 27.1 us -> 29.2 us  [call(): pl.pallas_call(body, out_shape=outs, in_specs=specs, out_specs=jax.tree.m...]
  transfers between devices with their start and end apart: 21 -> 21, of which waited for: 11 -> 10; matrix products, arithmetic and copies ran while one was open for 0% -> 0% of each run, Pallas kernels for 24% -> 23%
where the time goes in v3:
time: 96.3 us; the launch traced here: 96 us
  waiting for transfers between devices  40 us (42%)
  Pallas kernels  29.2 us (30%)
  starting transfers between devices  26.6 us (28%)
    ppermute x21, waiting for transfers between devices, xor_permute(): return lax.ppermute(x, axis, [(i, i ^ mask) for i in range(size)])  40 us
    pallas_call x17, Pallas kernels, call(): pl.pallas_call(body, out_shape=outs, in_specs=specs, out_specs=jax.tree.m...  29.2 us
    ppermute x21, starting transfers between devices, xor_permute(): return lax.ppermute(x, axis, [(i, i ^ mask) for i in range(size)])  26.6 us
  transfers between devices with their start and end apart: 21, of which 10 were waited for; matrix products, arithmetic and copies ran while one was open for 0% of the time, Pallas kernels for 23%

profile of v3, /device:TPU:0, one launch (start us, length us, event | category | flops | bytes accessed | tf_op | source)
XLA Modules:
  0.0 96.0 jit_solution(9771174723215560729)
XLA Ops:
  0.0 0.0 copy-start
  0.0 3.0 %collective-permute-start.7 = (bf16[32,128,128]{2,1,0:T(8,128)(2,1)}, bf16[32,128,128]{2,1,0:T(8,128)(2,1)S(1)}, u32[]{:S(2)}, u32[]{:S(2)}) collective-permute-start(bf16[32,128,128]{2,1,0:T(8,128)(2,1)} %refs_2_.3), channel_id=1, source_target_pairs={{0,2},{2,0},{1,3},{3,1},{4,6},{6,4},{5,7},{7,5},{8,10},{10,8},{9,1... | collective-permute-start | bytes 3145736 | tf_op jit(solution)/shard_map/ppermute | solution.py:31
  3.0 0.0 collective-permute-start.6
  3.0 4.5 %shard_map.113 = (bf16[768,1792]{1,0:T(8,128)(2,1)S(1)}, bf16[1792,2304]{1,0:T(8,128)(2,1)S(1)}, bf16[32,128,128]{2,1,0:T(8,128)(2,1)S(1)}, bf16[16,1792]{1,0:T(8,128)(2,1)S(1)}, f32[1792]{0:T(1024)S(1)}) custom-call(bf16[4096,1792]{1,0:T(8,128)(2,1)} %refs_0_.5, bf16[1792,2304]{1,0:T(8,128)(2,1)} %refs_1_.1, bf16[32,128,128]{2,1,0:T(8,128)(2,1)} %refs_2_.3, ...), custom_call_target="tpu_custom_call" | custom-call | bytes 24246272 | tf_op jit(solution)/shard_map/pallas_call | solution.py:47
  7.5 18.8 %collective-permute-done.7.refs_6_ = bf16[32,128,128]{2,1,0:T(8,128)(2,1)S(1)} collective-permute-done((bf16[32,128,128]{2,1,0:T(8,128)(2,1)}, bf16[32,128,128]{2,1,0:T(8,128)(2,1)S(1)}, u32[]{:S(2)}, u32[]{:S(2)}) %collective-permute-start.7) | collective-permute-done | bytes 1048608 | tf_op jit(solution)/shard_map/ppermute | solution.py:31
  26.3 0.0 collective-permute-start.8
  26.3 0.0 copy-done
  26.3 2.8 %collective-permute-start = (bf16[4,32,576]{2,1,0:T(8,128)(2,1)S(1)}, bf16[4,32,576]{2,1,0:T(8,128)(2,1)S(1)}, u32[]{:S(2)}, u32[]{:S(2)}) collective-permute-start(bf16[4,32,576]{2,1,0:T(8,128)(2,1)S(1)} %copy-done), channel_id=1, source_target_pairs={{0,8},{4,12},{8,0},{12,4},{1,9},{5,13},{9,1},{13,5},{2,10},{6,14},... | collective-permute-start | bytes 442376 | tf_op jit(solution)/shard_map/ppermute | solution.py:31
  29.2 1.6 %collective-permute-start.2 = (bf16[4,32,576]{2,1,0:T(8,128)(2,1)S(1)}, bf16[4,32,576]{2,1,0:T(8,128)(2,1)S(1)}, u32[]{:S(2)}, u32[]{:S(2)}) collective-permute-start(bf16[4,32,576]{2,1,0:T(8,128)(2,1)S(1)} %copy-done), channel_id=1, source_target_pairs={{0,4},{4,0},{8,12},{12,8},{1,5},{5,1},{9,13},{13,9},{2,6},{6,2},{1... | collective-permute-start | bytes 442376 | tf_op jit(solution)/shard_map/ppermute | solution.py:31
  30.8 6.9 %collective-permute-done.refs_0_ = bf16[4,32,576]{2,1,0:T(8,128)(2,1)S(1)} collective-permute-done((bf16[4,32,576]{2,1,0:T(8,128)(2,1)S(1)}, bf16[4,32,576]{2,1,0:T(8,128)(2,1)S(1)}, u32[]{:S(2)}, u32[]{:S(2)}) %collective-permute-start) | collective-permute-done | bytes 147488 | tf_op jit(solution)/shard_map/ppermute | solution.py:31
  37.7 0.6 collective-permute-start.1
  38.3 1.7 %shard_map.109 = (bf16[4,32,576]{2,1,0:T(8,128)(2,1)S(1)}, bf16[2,576,1024]{2,1,0:T(8,128)(2,1)S(1)}, s32[4,128]{1,0:T(4,128)S(1)}) custom-call(bf16[4,32,576]{2,1,0:T(8,128)(2,1)} %refs_0_.3, bf16[2,576,1024]{2,1,0:T(8,128)(2,1)} %bitcast.1, s32[2]{0:T(128)} %refs_2_.2, s32[4]{0:T(128)} %refs_3_.4), custom_call_target="tpu_custom_call" | custom-call | bytes 5013504 | tf_op jit(solution)/shard_map/pallas_call | solution.py:47
  40.0 1.6 %shard_map.112 = (bf16[136,512]{1,0:T(8,128)(2,1)S(1)}, bf16[512,1792]{1,0:T(8,128)(2,1)S(1)}) custom-call(bf16[4,32,576]{2,1,0:T(8,128)(2,1)S(1)} %collective-permute-done.refs_0_, bf16[2,576,1024]{2,1,0:T(8,128)(2,1)S(1)} %get-tuple-element.37.refs_1_.refs_2_, s32[4,128]{1,0:T(4,128)S(1)} %get-tuple-element.38.refs_2_.refs_3_, bf16[4096,1792]{1,0:T(8,128)(2,1)} %refs_0_.5), custom_call_target="tpu_custom_call" | custom-call | flops 285212672 | bytes 4194304 | tf_op jit(solution)/shard_map/pallas_call | solution.py:47
  41.6 3.4 %collective-permute-start.4 = (bf16[136,512]{1,0:T(8,128)(2,1)S(1)}, bf16[136,512]{1,0:T(8,128)(2,1)S(1)}, u32[]{:S(2)}, u32[]{:S(2)}) collective-permute-start(bf16[136,512]{1,0:T(8,128)(2,1)S(1)} %get-tuple-element.41), channel_id=1, source_target_pairs={{0,8},{4,12},{8,0},{12,4},{1,9},{5,13},{9,1},{13,5},{2,10},{6,14},... | collective-permute-start | bytes 417800 | tf_op jit(solution)/shard_map/ppermute | solution.py:31
  45.0 0.0 collective-permute-done.2.refs_1_
  45.0 0.0 collective-permute-done.1.refs_0_
  45.0 1.8 %shard_map.111 = (bf16[136,512]{1,0:T(8,128)(2,1)S(1)}, bf16[136,512]{1,0:T(8,128)(2,1)S(1)}, bf16[512,1792]{1,0:T(8,128)(2,1)S(1)}) custom-call(bf16[4,32,576]{2,1,0:T(8,128)(2,1)S(1)} %collective-permute-done.1.refs_0_, bf16[4,32,576]{2,1,0:T(8,128)(2,1)S(1)} %collective-permute-done.2.refs_1_, ...), custom_call_target="tpu_custom_call" | custom-call | flops 570425344 | bytes 4194304 | tf_op jit(solution)/shard_map/pallas_call | solution.py:47
  46.8 0.1 collective-permute-start.3
  46.9 2.6 %collective-permute-start.5 = (bf16[136,512]{1,0:T(8,128)(2,1)S(1)}, bf16[136,512]{1,0:T(8,128)(2,1)S(1)}, u32[]{:S(2)}, u32[]{:S(2)}) collective-permute-start(bf16[136,512]{1,0:T(8,128)(2,1)S(1)} %get-tuple-element.42), channel_id=1, source_target_pairs={{0,12},{4,8},{8,4},{12,0},{1,13},{5,9},{9,5},{13,1},{2,14},{6,10},... | collective-permute-start | bytes 417800 | tf_op jit(solution)/shard_map/ppermute | solution.py:31
  49.5 1.6 %shard_map.110 = (bf16[136,512]{1,0:T(8,128)(2,1)S(1)}, bf16[512,1792]{1,0:T(8,128)(2,1)S(1)}) custom-call(bf16[4,32,576]{2,1,0:T(8,128)(2,1)S(1)} %get-tuple-element.36.refs_0_, bf16[2,576,1024]{2,1,0:T(8,128)(2,1)S(1)} %get-tuple-element.37.refs_1_.refs_2_, s32[4,128]{1,0:T(4,128)S(1)} %get-tuple-element.38.refs_2_.refs_3_, bf16[4096,1792]{1,0:T(8,128)(2,1)} %refs_0_.5), custom_call_target="tpu_custom_call" | custom-call | flops 285212672 | bytes 4194304 | tf_op jit(solution)/shard_map/pallas_call | solution.py:47
  51.1 1.3 %collective-permute-done.4.refs_2_ = bf16[136,512]{1,0:T(8,128)(2,1)S(1)} collective-permute-done((bf16[136,512]{1,0:T(8,128)(2,1)S(1)}, bf16[136,512]{1,0:T(8,128)(2,1)S(1)}, u32[]{:S(2)}, u32[]{:S(2)}) %collective-permute-start.4) | collective-permute-done | bytes 139296 | tf_op jit(solution)/shard_map/ppermute | solution.py:31
  52.3 5.1 %collective-permute-done.3.refs_1_ = bf16[136,512]{1,0:T(8,128)(2,1)S(1)} collective-permute-done((bf16[136,512]{1,0:T(8,128)(2,1)S(1)}, bf16[136,512]{1,0:T(8,128)(2,1)S(1)}, u32[]{:S(2)}, u32[]{:S(2)}) %collective-permute-start.3) | collective-permute-done | bytes 139296 | tf_op jit(solution)/shard_map/ppermute | solution.py:31
  57.5 0.0 collective-permute-done.5.refs_3_
  57.5 0.0 collective-permute-done.6.refs_5_
  57.5 0.0 collective-permute-done.8.refs_7_
  57.5 1.7 %shard_map.114.refs_0_ = bf16[4,4096]{1,0:T(4,128)(2,1)S(1)} custom-call(bf16[136,512]{1,0:T(8,128)(2,1)S(1)} %get-tuple-element.39.refs_0_, bf16[136,512]{1,0:T(8,128)(2,1)S(1)} %collective-permute-done.3.refs_1_, bf16[136,512]{1,0:T(8,128)(2,1)S(1)} %collective-permute-done.4.refs_2_, bf16[136,512]{1,0:T(8,128)(2,1)S(1)} %collective-permute-done.5.refs_3_, ...), custom_call_target="tpu_custom_call" | custom-call | flops 16777216 | bytes 4194304 | tf_op jit(solution)/shard_map/pallas_call | solution.py:47
  59.2 1.5 %collective-permute-start.10 = (bf16[4,4096]{1,0:T(4,128)(2,1)S(1)}, bf16[4,4096]{1,0:T(4,128)(2,1)S(1)}, u32[]{:S(2)}, u32[]{:S(2)}) collective-permute-start(bf16[4,4096]{1,0:T(4,128)(2,1)S(1)} %shard_map.114.refs_0_), channel_id=1, source_target_pairs={{0,2},{1,3},{2,0},{3,1},{4,6},{5,7},{6,4},{7,5},{8,10},{9,11},{10,... | collective-permute-start | bytes 98312 | tf_op jit(solution)/shard_map/ppermute | solution.py:31
  60.6 0.0 collective-permute-start.11
  60.6 0.7 collective-permute-start.9
  61.3 2.8 %shard_map.115.refs_5_ = bf16[1792,1792]{1,0:T(8,128)(2,1)S(1)} custom-call(bf16[4096,1792]{1,0:T(8,128)(2,1)} %refs_0_.5), custom_call_target="tpu_custom_call" | custom-call | bytes 12845056 | tf_op jit(solution)/shard_map/pallas_call | solution.py:47
  64.1 0.0 collective-permute-done.10.refs_2_
  64.2 0.1 collective-permute-done.11.refs_3_
  64.2 0.0 collective-permute-done.9.refs_1_
  64.2 2.0 %shard_map.116.refs_0_ = bf16[16,1792]{1,0:T(8,128)(2,1)S(1)} custom-call(bf16[4,4096]{1,0:T(4,128)(2,1)S(1)} %shard_map.114.refs_0_, bf16[4,4096]{1,0:T(4,128)(2,1)S(1)} %collective-permute-done.9.refs_1_, bf16[4,4096]{1,0:T(4,128)(2,1)S(1)} %collective-permute-done.10.refs_2_, bf16[4,4096]{1,0:T(4,128)(2,1)S(1)} %collective-permute-done.11.refs_3_, ...), custom_call_target="tpu_custom_call" | custom-call | flops 234881024 | bytes 4194304 | tf_op jit(solution)/shard_map/pallas_call | solution.py:47
  66.3 0.6 collective-permute-start.12
  66.8 1.1 %collective-permute-start.13 = (bf16[16,1792]{1,0:T(8,128)(2,1)S(1)}, bf16[16,1792]{1,0:T(8,128)(2,1)S(1)}, u32[]{:S(2)}, u32[]{:S(2)}) collective-permute-start(bf16[16,1792]{1,0:T(8,128)(2,1)S(1)} %shard_map.116.refs_0_), channel_id=1, source_target_pairs={{0,8},{4,12},{8,0},{12,4},{1,9},{5,13},{9,1},{13,5},{2,10},{6,14},... | collective-permute-start | bytes 172040 | tf_op jit(solution)/shard_map/ppermute | solution.py:31
  67.9 2.8 %collective-permute-start.14 = (bf16[16,1792]{1,0:T(8,128)(2,1)S(1)}, bf16[16,1792]{1,0:T(8,128)(2,1)S(1)}, u32[]{:S(2)}, u32[]{:S(2)}) collective-permute-start(bf16[16,1792]{1,0:T(8,128)(2,1)S(1)} %shard_map.116.refs_0_), channel_id=1, source_target_pairs={{0,12},{4,8},{8,4},{12,0},{1,13},{5,9},{9,5},{13,1},{2,14},{6,10},... | collective-permute-start | bytes 172040 | tf_op jit(solution)/shard_map/ppermute | solution.py:31
  70.7 3.4 %shard_map.117.refs_7_.up_ref = bf16[1792,2304]{1,0:T(8,128)(2,1)S(1)} custom-call(bf16[1792,2304]{1,0:T(8,128)(2,1)} %refs_0_.6), custom_call_target="tpu_custom_call" | custom-call | bytes 16515072 | tf_op jit(solution)/shard_map/pallas_call | solution.py:47
  74.0 0.0 collective-permute-done.12.refs_1_
  74.0 0.8 collective-permute-done.13.refs_2_
  74.8 0.0 collective-permute-done.14.refs_3_
  74.8 1.3 %shard_map.118 = (bf16[16,2432]{1,0:T(8,128)(2,1)S(1)}, bf16[16,1792]{1,0:T(8,128)(2,1)S(1)}, f32[16,128]{1,0:T(8,128)S(1)}, f32[4,1792]{1,0:T(4,128)S(1)}) custom-call(bf16[16,1792]{1,0:T(8,128)(2,1)S(1)} %shard_map.116.refs_0_, bf16[16,1792]{1,0:T(8,128)(2,1)S(1)} %collective-permute-done.12.refs_1_, bf16[16,1792]{1,0:T(8,128)(2,1)S(1)} %collective-permute-done.13.refs_2_, ...), custom_call_target="tpu_custom_call" | custom-call | flops 132120576 | bytes 4194304 | tf_op jit(solution)/shard_map/pallas_call | solution.py:47
  76.1 0.0 collective-permute-start.15
  76.2 1.2 %shard_map.119.keep_ref = f32[16,2304]{1,0:T(8,128)S(1)} custom-call(bf16[16,1792]{1,0:T(8,128)(2,1)S(1)} %get-tuple-element.56.scaled_ref, bf16[1792,2304]{1,0:T(8,128)(2,1)S(1)} %get-tuple-element.53.refs_6_.gate_ref, bf16[1792,2304]{1,0:T(8,128)(2,1)S(1)} %shard_map.117.refs_7_.up_ref), custom_call_target="tpu_custom_call" | custom-call | flops 132120576 | bytes 4194304 | tf_op jit(solution)/shard_map/pallas_call | solution.py:47
  77.3 0.1 collective-permute-done.15.got_ref
  77.4 0.2 shard_map.120
  77.6 1.4 %collective-permute-start.16 = (bf16[16,2432]{1,0:T(8,128)(2,1)S(1)}, bf16[16,2432]{1,0:T(8,128)(2,1)S(1)}, u32[]{:S(2)}, u32[]{:S(2)}) collective-permute-start(bf16[16,2432]{1,0:T(8,128)(2,1)S(1)} %get-tuple-element.61), channel_id=1, source_target_pairs={{0,2},{2,0},{1,3},{3,1},{4,6},{6,4},{5,7},{7,5},{8,10},{10,8},{9,1... | collective-permute-start | bytes 233480 | tf_op jit(solution)/shard_map/ppermute | solution.py:31
  79.0 3.3 %collective-permute-done.16.refs_1_ = bf16[16,2432]{1,0:T(8,128)(2,1)S(1)} collective-permute-done((bf16[16,2432]{1,0:T(8,128)(2,1)S(1)}, bf16[16,2432]{1,0:T(8,128)(2,1)S(1)}, u32[]{:S(2)}, u32[]{:S(2)}) %collective-permute-start.16) | collective-permute-done | bytes 77856 | tf_op jit(solution)/shard_map/ppermute | solution.py:31
  82.3 0.2 shard_map.121.own_ref
  82.5 0.1 collective-permute-start.17
  82.6 3.4 %shard_map.122.weight_ref = bf16[2304,1792]{1,0:T(8,128)(2,1)S(1)} custom-call(bf16[2304,1792]{1,0:T(8,128)(2,1)} %refs_0_.7), custom_call_target="tpu_custom_call" | custom-call | bytes 16515072 | tf_op jit(solution)/shard_map/pallas_call | solution.py:47
  85.9 0.7 shard_map.123.partial_ref
  86.6 0.0 collective-permute-done.17.other_ref
  86.6 0.7 shard_map.124
  87.3 1.2 %collective-permute-start.18 = (bf16[4,1792]{1,0:T(4,128)(2,1)S(1)}, bf16[4,1792]{1,0:T(4,128)(2,1)S(1)}, u32[]{:S(2)}, u32[]{:S(2)}) collective-permute-start(bf16[4,1792]{1,0:T(4,128)(2,1)S(1)} %get-tuple-element.64), channel_id=1, source_target_pairs={{0,4},{4,0},{8,12},{12,8},{1,5},{5,1},{9,13},{13,9},{2,6},{6,2},{1... | collective-permute-start | bytes 43016 | tf_op jit(solution)/shard_map/ppermute | solution.py:31
  88.5 1.3 %collective-permute-start.19 = (bf16[4,1792]{1,0:T(4,128)(2,1)S(1)}, bf16[4,1792]{1,0:T(4,128)(2,1)S(1)}, u32[]{:S(2)}, u32[]{:S(2)}) collective-permute-start(bf16[4,1792]{1,0:T(4,128)(2,1)S(1)} %get-tuple-element.65), channel_id=1, source_target_pairs={{0,8},{4,12},{8,0},{12,4},{1,9},{5,13},{9,1},{13,5},{2,10},{6,14},... | collective-permute-start | bytes 43016 | tf_op jit(solution)/shard_map/ppermute | solution.py:31
  89.9 1.9 %collective-permute-start.20 = (bf16[4,1792]{1,0:T(4,128)(2,1)S(1)}, bf16[4,1792]{1,0:T(4,128)(2,1)S(1)}, u32[]{:S(2)}, u32[]{:S(2)}) collective-permute-start(bf16[4,1792]{1,0:T(4,128)(2,1)S(1)} %get-tuple-element.66), channel_id=1, source_target_pairs={{0,12},{4,8},{8,4},{12,0},{1,13},{5,9},{9,5},{13,1},{2,14},{6,10},... | collective-permute-start | bytes 43016 | tf_op jit(solution)/shard_map/ppermute | solution.py:31
  91.8 0.0 collective-permute-done.18.refs_2_
  91.8 1.4 %collective-permute-done.19.refs_3_ = bf16[4,1792]{1,0:T(4,128)(2,1)S(1)} collective-permute-done((bf16[4,1792]{1,0:T(4,128)(2,1)S(1)}, bf16[4,1792]{1,0:T(4,128)(2,1)S(1)}, u32[]{:S(2)}, u32[]{:S(2)}) %collective-permute-start.19) | collective-permute-done | bytes 14368 | tf_op jit(solution)/shard_map/ppermute | solution.py:31
  93.2 2.2 %collective-permute-done.20.refs_4_ = bf16[4,1792]{1,0:T(4,128)(2,1)S(1)} collective-permute-done((bf16[4,1792]{1,0:T(4,128)(2,1)S(1)}, bf16[4,1792]{1,0:T(4,128)(2,1)S(1)}, u32[]{:S(2)}, u32[]{:S(2)}) %collective-permute-start.20) | collective-permute-done | bytes 14368 | tf_op jit(solution)/shard_map/ppermute | solution.py:31
  95.4 0.6 shard_map.125
Async XLA Ops:
  0.0 26.3 %copy-start = (bf16[4,32,576]{2,1,0:T(8,128)(2,1)S(1)}, bf16[4,32,576]{2,1,0:T(8,128)(2,1)}, u32[]{:S(2)}) copy-start(bf16[4,32,576]{2,1,0:T(8,128)(2,1)} %refs_0_.3) | copy-start | bytes 442372
  0.0 26.3 %collective-permute-start.7 = (bf16[32,128,128]{2,1,0:T(8,128)(2,1)}, bf16[32,128,128]{2,1,0:T(8,128)(2,1)S(1)}, u32[]{:S(2)}, u32[]{:S(2)}) collective-permute-start(bf16[32,128,128]{2,1,0:T(8,128)(2,1)} %refs_2_.3), channel_id=1, source_target_pairs={{0,2},{2,0},{1,3},{3,1},{4,6},{6,4},{5,7},{7,5},{8,10},{10,8},{9,1... | collective-permute-start | bytes 3145736 | tf_op jit(solution)/shard_map/ppermute | solution.py:31
  3.0 54.5 %collective-permute-start.6 = (bf16[32,128,128]{2,1,0:T(8,128)(2,1)}, bf16[32,128,128]{2,1,0:T(8,128)(2,1)S(1)}, u32[]{:S(2)}, u32[]{:S(2)}) collective-permute-start(bf16[32,128,128]{2,1,0:T(8,128)(2,1)} %refs_2_.3), channel_id=1, source_target_pairs={{0,1},{1,0},{2,3},{3,2},{4,5},{5,4},{6,7},{7,6},{8,9},{9,8},{10,11... | collective-permute-start | bytes 3145736 | tf_op jit(solution)/shard_map/ppermute | solution.py:31
  26.3 31.1 %collective-permute-start.8 = (bf16[32,128,128]{2,1,0:T(8,128)(2,1)S(1)}, bf16[32,128,128]{2,1,0:T(8,128)(2,1)S(1)}, u32[]{:S(2)}, u32[]{:S(2)}) collective-permute-start(bf16[32,128,128]{2,1,0:T(8,128)(2,1)S(1)} %collective-permute-done.7.refs_6_), channel_id=1, source_target_pairs={{0,1},{1,0},{2,3},{3,2},{4,5},{5,4},{6,7},{7,6},{8,9},{9,8},{10,11... | collective-permute-start | bytes 3145736 | tf_op jit(solution)/shard_map/ppermute | solution.py:31
  26.3 11.3 %collective-permute-start = (bf16[4,32,576]{2,1,0:T(8,128)(2,1)S(1)}, bf16[4,32,576]{2,1,0:T(8,128)(2,1)S(1)}, u32[]{:S(2)}, u32[]{:S(2)}) collective-permute-start(bf16[4,32,576]{2,1,0:T(8,128)(2,1)S(1)} %copy-done), channel_id=1, source_target_pairs={{0,8},{4,12},{8,0},{12,4},{1,9},{5,13},{9,1},{13,5},{2,10},{6,14},... | collective-permute-start | bytes 442376 | tf_op jit(solution)/shard_map/ppermute | solution.py:31
  29.2 15.8 %collective-permute-start.2 = (bf16[4,32,576]{2,1,0:T(8,128)(2,1)S(1)}, bf16[4,32,576]{2,1,0:T(8,128)(2,1)S(1)}, u32[]{:S(2)}, u32[]{:S(2)}) collective-permute-start(bf16[4,32,576]{2,1,0:T(8,128)(2,1)S(1)} %copy-done), channel_id=1, source_target_pairs={{0,4},{4,0},{8,12},{12,8},{1,5},{5,1},{9,13},{13,9},{2,6},{6,2},{1... | collective-permute-start | bytes 442376 | tf_op jit(solution)/shard_map/ppermute | solution.py:31
  37.7 7.3 %collective-permute-start.1 = (bf16[4,32,576]{2,1,0:T(8,128)(2,1)S(1)}, bf16[4,32,576]{2,1,0:T(8,128)(2,1)S(1)}, u32[]{:S(2)}, u32[]{:S(2)}) collective-permute-start(bf16[4,32,576]{2,1,0:T(8,128)(2,1)S(1)} %collective-permute-done.refs_0_), channel_id=1, source_target_pairs={{0,4},{4,0},{8,12},{12,8},{1,5},{5,1},{9,13},{13,9},{2,6},{6,2},{1... | collective-permute-start | bytes 442376 | tf_op jit(solution)/shard_map/ppermute | solution.py:31
  41.6 10.7 %collective-permute-start.4 = (bf16[136,512]{1,0:T(8,128)(2,1)S(1)}, bf16[136,512]{1,0:T(8,128)(2,1)S(1)}, u32[]{:S(2)}, u32[]{:S(2)}) collective-permute-start(bf16[136,512]{1,0:T(8,128)(2,1)S(1)} %get-tuple-element.41), channel_id=1, source_target_pairs={{0,8},{4,12},{8,0},{12,4},{1,9},{5,13},{9,1},{13,5},{2,10},{6,14},... | collective-permute-start | bytes 417800 | tf_op jit(solution)/shard_map/ppermute | solution.py:31
  46.8 10.7 %collective-permute-start.3 = (bf16[136,512]{1,0:T(8,128)(2,1)S(1)}, bf16[136,512]{1,0:T(8,128)(2,1)S(1)}, u32[]{:S(2)}, u32[]{:S(2)}) collective-permute-start(bf16[136,512]{1,0:T(8,128)(2,1)S(1)} %get-tuple-element.40), channel_id=1, source_target_pairs={{0,4},{4,0},{8,12},{12,8},{1,5},{5,1},{9,13},{13,9},{2,6},{6,2},{1... | collective-permute-start | bytes 417800 | tf_op jit(solution)/shard_map/ppermute | solution.py:31
  46.9 10.6 %collective-permute-start.5 = (bf16[136,512]{1,0:T(8,128)(2,1)S(1)}, bf16[136,512]{1,0:T(8,128)(2,1)S(1)}, u32[]{:S(2)}, u32[]{:S(2)}) collective-permute-start(bf16[136,512]{1,0:T(8,128)(2,1)S(1)} %get-tuple-element.42), channel_id=1, source_target_pairs={{0,12},{4,8},{8,4},{12,0},{1,13},{5,9},{9,5},{13,1},{2,14},{6,10},... | collective-permute-start | bytes 417800 | tf_op jit(solution)/shard_map/ppermute | solution.py:31
  59.2 5.0 %collective-permute-start.10 = (bf16[4,4096]{1,0:T(4,128)(2,1)S(1)}, bf16[4,4096]{1,0:T(4,128)(2,1)S(1)}, u32[]{:S(2)}, u32[]{:S(2)}) collective-permute-start(bf16[4,4096]{1,0:T(4,128)(2,1)S(1)} %shard_map.114.refs_0_), channel_id=1, source_target_pairs={{0,2},{1,3},{2,0},{3,1},{4,6},{5,7},{6,4},{7,5},{8,10},{9,11},{10,... | collective-permute-start | bytes 98312 | tf_op jit(solution)/shard_map/ppermute | solution.py:31
  60.6 3.6 %collective-permute-start.11 = (bf16[4,4096]{1,0:T(4,128)(2,1)S(1)}, bf16[4,4096]{1,0:T(4,128)(2,1)S(1)}, u32[]{:S(2)}, u32[]{:S(2)}) collective-permute-start(bf16[4,4096]{1,0:T(4,128)(2,1)S(1)} %shard_map.114.refs_0_), channel_id=1, source_target_pairs={{0,3},{1,2},{2,1},{3,0},{4,7},{5,6},{6,5},{7,4},{8,11},{9,10},{10,... | collective-permute-start | bytes 98312 | tf_op jit(solution)/shard_map/ppermute | solution.py:31
  60.6 3.6 %collective-permute-start.9 = (bf16[4,4096]{1,0:T(4,128)(2,1)S(1)}, bf16[4,4096]{1,0:T(4,128)(2,1)S(1)}, u32[]{:S(2)}, u32[]{:S(2)}) collective-permute-start(bf16[4,4096]{1,0:T(4,128)(2,1)S(1)} %shard_map.114.refs_0_), channel_id=1, source_target_pairs={{0,1},{1,0},{2,3},{3,2},{4,5},{5,4},{6,7},{7,6},{8,9},{9,8},{10,11... | collective-permute-start | bytes 98312 | tf_op jit(solution)/shard_map/ppermute | solution.py:31
  66.3 7.8 %collective-permute-start.12 = (bf16[16,1792]{1,0:T(8,128)(2,1)S(1)}, bf16[16,1792]{1,0:T(8,128)(2,1)S(1)}, u32[]{:S(2)}, u32[]{:S(2)}) collective-permute-start(bf16[16,1792]{1,0:T(8,128)(2,1)S(1)} %shard_map.116.refs_0_), channel_id=1, source_target_pairs={{0,4},{4,0},{8,12},{12,8},{1,5},{5,1},{9,13},{13,9},{2,6},{6,2},{1... | collective-permute-start | bytes 172040 | tf_op jit(solution)/shard_map/ppermute | solution.py:31
  66.8 8.0 %collective-permute-start.13 = (bf16[16,1792]{1,0:T(8,128)(2,1)S(1)}, bf16[16,1792]{1,0:T(8,128)(2,1)S(1)}, u32[]{:S(2)}, u32[]{:S(2)}) collective-permute-start(bf16[16,1792]{1,0:T(8,128)(2,1)S(1)} %shard_map.116.refs_0_), channel_id=1, source_target_pairs={{0,8},{4,12},{8,0},{12,4},{1,9},{5,13},{9,1},{13,5},{2,10},{6,14},... | collective-permute-start | bytes 172040 | tf_op jit(solution)/shard_map/ppermute | solution.py:31
  67.9 6.9 %collective-permute-start.14 = (bf16[16,1792]{1,0:T(8,128)(2,1)S(1)}, bf16[16,1792]{1,0:T(8,128)(2,1)S(1)}, u32[]{:S(2)}, u32[]{:S(2)}) collective-permute-start(bf16[16,1792]{1,0:T(8,128)(2,1)S(1)} %shard_map.116.refs_0_), channel_id=1, source_target_pairs={{0,12},{4,8},{8,4},{12,0},{1,13},{5,9},{9,5},{13,1},{2,14},{6,10},... | collective-permute-start | bytes 172040 | tf_op jit(solution)/shard_map/ppermute | solution.py:31
  76.1 1.3 %collective-permute-start.15 = (bf16[16,2432]{1,0:T(8,128)(2,1)S(1)}, bf16[16,2432]{1,0:T(8,128)(2,1)S(1)}, u32[]{:S(2)}, u32[]{:S(2)}) collective-permute-start(bf16[16,2432]{1,0:T(8,128)(2,1)S(1)} %get-tuple-element.58), channel_id=1, source_target_pairs={{0,1},{1,0},{2,3},{3,2},{4,5},{5,4},{6,7},{7,6},{8,9},{9,8},{10,11... | collective-permute-start | bytes 233480 | tf_op jit(solution)/shard_map/ppermute | solution.py:31
  77.6 4.7 %collective-permute-start.16 = (bf16[16,2432]{1,0:T(8,128)(2,1)S(1)}, bf16[16,2432]{1,0:T(8,128)(2,1)S(1)}, u32[]{:S(2)}, u32[]{:S(2)}) collective-permute-start(bf16[16,2432]{1,0:T(8,128)(2,1)S(1)} %get-tuple-element.61), channel_id=1, source_target_pairs={{0,2},{2,0},{1,3},{3,1},{4,6},{6,4},{5,7},{7,5},{8,10},{10,8},{9,1... | collective-permute-start | bytes 233480 | tf_op jit(solution)/shard_map/ppermute | solution.py:31
  82.5 4.1 %collective-permute-start.17 = (bf16[16,1152]{1,0:T(8,128)(2,1)S(1)}, bf16[16,1152]{1,0:T(8,128)(2,1)S(1)}, u32[]{:S(2)}, u32[]{:S(2)}) collective-permute-start(bf16[16,1152]{1,0:T(8,128)(2,1)S(1)} %shard_map.121.own_ref), channel_id=1, source_target_pairs={{0,1},{1,0},{2,3},{3,2},{4,5},{5,4},{6,7},{7,6},{8,9},{9,8},{10,11... | collective-permute-start | bytes 110600 | tf_op jit(solution)/shard_map/ppermute | solution.py:31
  87.3 4.5 %collective-permute-start.18 = (bf16[4,1792]{1,0:T(4,128)(2,1)S(1)}, bf16[4,1792]{1,0:T(4,128)(2,1)S(1)}, u32[]{:S(2)}, u32[]{:S(2)}) collective-permute-start(bf16[4,1792]{1,0:T(4,128)(2,1)S(1)} %get-tuple-element.64), channel_id=1, source_target_pairs={{0,4},{4,0},{8,12},{12,8},{1,5},{5,1},{9,13},{13,9},{2,6},{6,2},{1... | collective-permute-start | bytes 43016 | tf_op jit(solution)/shard_map/ppermute | solution.py:31
  88.5 4.7 %collective-permute-start.19 = (bf16[4,1792]{1,0:T(4,128)(2,1)S(1)}, bf16[4,1792]{1,0:T(4,128)(2,1)S(1)}, u32[]{:S(2)}, u32[]{:S(2)}) collective-permute-start(bf16[4,1792]{1,0:T(4,128)(2,1)S(1)} %get-tuple-element.65), channel_id=1, source_target_pairs={{0,8},{4,12},{8,0},{12,4},{1,9},{5,13},{9,1},{13,5},{2,10},{6,14},... | collective-permute-start | bytes 43016 | tf_op jit(solution)/shard_map/ppermute | solution.py:31
  89.9 5.5 %collective-permute-start.20 = (bf16[4,1792]{1,0:T(4,128)(2,1)S(1)}, bf16[4,1792]{1,0:T(4,128)(2,1)S(1)}, u32[]{:S(2)}, u32[]{:S(2)}) collective-permute-start(bf16[4,1792]{1,0:T(4,128)(2,1)S(1)} %get-tuple-element.66), channel_id=1, source_target_pairs={{0,12},{4,8},{8,4},{12,0},{1,13},{5,9},{9,5},{13,1},{2,14},{6,10},... | collective-permute-start | bytes 43016 | tf_op jit(solution)/shard_map/ppermute | solution.py:31

commit v4 on v3

--- a/solution.py
+++ b/solution.py
@@ -460,9 +460,8 @@
     along = listed(exchange([value_up_weight] * roles, "role"))
     groups = exchange([queries] * blocks, "ctx", [*evens, 1])
     unit = out_proj.shape[0] // 16
-    own_span, early_span, even_span, odd_span, late_span = [
-        (unit * first, unit * last) for first, last in ((0, 2), (2, 9), (9, 11), (11, 13), (13, 16))
-    ]
+    cuts = [unit * k for k in (0, 2, 6, 8, 10, 13, 16)]
+    own_span, early_span, even_span, odd_span, late_span, last_span = zip(cuts, cuts[1:])
     groups[0], cache_fast, seen = fetch([queries, jnp.swapaxes(cache, 1, 2)], lengths, positions)
 
     def attend_some(source, span):
@@ -480,18 +479,18 @@
     answers |= exchange({0: answers[0], **far}, "ctx", odds)
     answers |= exchange({0: answers[0], **far}, "ctx", [1])
 
-    late_part, gate_fast, up_own, residual, gain = fetch(
-        [(out_proj, late_span), gate_weight, value_up_weight, residual, norm_gain]
-    )
+    gate_fast, up_own, residual, gain = fetch([gate_weight, value_up_weight, residual, norm_gain])
     *far_rows, gain = lax.optimization_barrier((*along[1:], gain))
     across = [xor_permute(along[0], "seq", 1)]
     across += [xor_permute(piece, "seq", 1) for piece in far_rows]
     up_pieces = [up_own, *[piece for pair in zip([None, *far_rows], across) for piece in pair][1:]]
-    out_parts = [own_part, early_part, even_part, odd_part, late_part]
+    (late_part,) = fetch([(out_proj, late_span)])
 
     values = join_and_project(listed(answers), up_pieces, rows, heads, gain)
+    last_out, values = lax.optimization_barrier((out_proj, values))
     shared = listed(exchange([values] * members, ("role", "seq")))
-    product = project_out(shared, out_parts)
+    (last_part,) = fetch([(last_out, last_span)])
+    product = project_out(shared, [own_part, early_part, even_part, odd_part, late_part, last_part])
     up_weight, product = lax.optimization_barrier((up_weight, product))
     terms = listed(exchange([product] * blocks, "ctx"))
     (up_fast,) = fetch([up_weight])

time: 96.3 us -> 99.1 us (1.029)
  Pallas kernels: 29.2 us -> 31.2 us
    pallas_call x17 -> x19, Pallas kernels: 29.2 us -> 31.2 us  [call(): pl.pallas_call(body, out_shape=outs, in_specs=specs, out_specs=jax.tree.m...]
  transfers between devices with their start and end apart: 21 -> 21, of which waited for: 10 -> 9; matrix products, arithmetic and copies ran while one was open for 0% -> 0% of each run, Pallas kernels for 23% -> 25%
where the time goes in v4:
time: 99.1 us; the launch traced here: 98.7 us
  waiting for transfers between devices  40.7 us (41%)
  Pallas kernels  31.2 us (31%)
  starting transfers between devices  26.7 us (27%)
    ppermute x21, waiting for transfers between devices, xor_permute(): return lax.ppermute(x, axis, [(i, i ^ mask) for i in range(size)])  40.7 us
    pallas_call x19, Pallas kernels, call(): pl.pallas_call(body, out_shape=outs, in_specs=specs, out_specs=jax.tree.m...  31.2 us
    ppermute x21, starting transfers between devices, xor_permute(): return lax.ppermute(x, axis, [(i, i ^ mask) for i in range(size)])  26.7 us
  transfers between devices with their start and end apart: 21, of which 9 were waited for; matrix products, arithmetic and copies ran while one was open for 0% of the time, Pallas kernels for 25%

profile of v4, /device:TPU:0, one launch (start us, length us, event | category | flops | bytes accessed | tf_op | source)
XLA Modules:
  0.0 98.7 jit_solution(15088890999197620959)
XLA Ops:
  0.0 0.0 copy-start
  0.0 3.0 %collective-permute-start.7 = (bf16[32,128,128]{2,1,0:T(8,128)(2,1)}, bf16[32,128,128]{2,1,0:T(8,128)(2,1)S(1)}, u32[]{:S(2)}, u32[]{:S(2)}) collective-permute-start(bf16[32,128,128]{2,1,0:T(8,128)(2,1)} %refs_1_.1), channel_id=1, source_target_pairs={{0,2},{2,0},{1,3},{3,1},{4,6},{6,4},{5,7},{7,5},{8,10},{10,8},{9,1... | collective-permute-start | bytes 3145736 | tf_op jit(solution)/shard_map/ppermute | solution.py:31
  3.0 0.0 collective-permute-start.6
  3.0 3.8 %shard_map.113 = (bf16[1792,2304]{1,0:T(8,128)(2,1)S(1)}, bf16[32,128,128]{2,1,0:T(8,128)(2,1)S(1)}, bf16[16,1792]{1,0:T(8,128)(2,1)S(1)}, f32[1792]{0:T(1024)S(1)}) custom-call(bf16[1792,2304]{1,0:T(8,128)(2,1)} %refs_0_.5, bf16[32,128,128]{2,1,0:T(8,128)(2,1)} %refs_1_.1, bf16[16,1792]{1,0:T(8,128)(2,1)} %refs_2_.3, f32[1792]{0:T(1024)} %refs_3_.7), custom_call_target="tpu_custom_call" | custom-call | bytes 18741248 | tf_op jit(solution)/shard_map/pallas_call | solution.py:47
  6.7 19.6 %collective-permute-done.7.refs_6_ = bf16[32,128,128]{2,1,0:T(8,128)(2,1)S(1)} collective-permute-done((bf16[32,128,128]{2,1,0:T(8,128)(2,1)}, bf16[32,128,128]{2,1,0:T(8,128)(2,1)S(1)}, u32[]{:S(2)}, u32[]{:S(2)}) %collective-permute-start.7) | collective-permute-done | bytes 1048608 | tf_op jit(solution)/shard_map/ppermute | solution.py:31
  26.3 0.0 collective-permute-start.8
  26.3 0.0 copy-done
  26.3 2.8 %collective-permute-start = (bf16[4,32,576]{2,1,0:T(8,128)(2,1)S(1)}, bf16[4,32,576]{2,1,0:T(8,128)(2,1)S(1)}, u32[]{:S(2)}, u32[]{:S(2)}) collective-permute-start(bf16[4,32,576]{2,1,0:T(8,128)(2,1)S(1)} %copy-done), channel_id=1, source_target_pairs={{0,8},{4,12},{8,0},{12,4},{1,9},{5,13},{9,1},{13,5},{2,10},{6,14},... | collective-permute-start | bytes 442376 | tf_op jit(solution)/shard_map/ppermute | solution.py:31
  29.2 1.6 %collective-permute-start.2 = (bf16[4,32,576]{2,1,0:T(8,128)(2,1)S(1)}, bf16[4,32,576]{2,1,0:T(8,128)(2,1)S(1)}, u32[]{:S(2)}, u32[]{:S(2)}) collective-permute-start(bf16[4,32,576]{2,1,0:T(8,128)(2,1)S(1)} %copy-done), channel_id=1, source_target_pairs={{0,4},{4,0},{8,12},{12,8},{1,5},{5,1},{9,13},{13,9},{2,6},{6,2},{1... | collective-permute-start | bytes 442376 | tf_op jit(solution)/shard_map/ppermute | solution.py:31
  30.8 6.9 %collective-permute-done.refs_0_ = bf16[4,32,576]{2,1,0:T(8,128)(2,1)S(1)} collective-permute-done((bf16[4,32,576]{2,1,0:T(8,128)(2,1)S(1)}, bf16[4,32,576]{2,1,0:T(8,128)(2,1)S(1)}, u32[]{:S(2)}, u32[]{:S(2)}) %collective-permute-start) | collective-permute-done | bytes 147488 | tf_op jit(solution)/shard_map/ppermute | solution.py:31
  37.7 0.6 collective-permute-start.1
  38.3 1.7 %shard_map.109 = (bf16[4,32,576]{2,1,0:T(8,128)(2,1)S(1)}, bf16[2,576,1024]{2,1,0:T(8,128)(2,1)S(1)}, s32[4,128]{1,0:T(4,128)S(1)}) custom-call(bf16[4,32,576]{2,1,0:T(8,128)(2,1)} %refs_0_.4, bf16[2,576,1024]{2,1,0:T(8,128)(2,1)} %bitcast.1, s32[2]{0:T(128)} %refs_2_.2, s32[4]{0:T(128)} %refs_3_.4), custom_call_target="tpu_custom_call" | custom-call | bytes 5013504 | tf_op jit(solution)/shard_map/pallas_call | solution.py:47
  40.0 1.6 %shard_map.112 = (bf16[136,512]{1,0:T(8,128)(2,1)S(1)}, bf16[512,1792]{1,0:T(8,128)(2,1)S(1)}) custom-call(bf16[4,32,576]{2,1,0:T(8,128)(2,1)S(1)} %collective-permute-done.refs_0_, bf16[2,576,1024]{2,1,0:T(8,128)(2,1)S(1)} %get-tuple-element.38.refs_1_.refs_2_, s32[4,128]{1,0:T(4,128)S(1)} %get-tuple-element.39.refs_2_.refs_3_, bf16[4096,1792]{1,0:T(8,128)(2,1)} %refs_0_.8), custom_call_target="tpu_custom_call" | custom-call | flops 285212672 | bytes 4194304 | tf_op jit(solution)/shard_map/pallas_call | solution.py:47
  41.6 3.4 %collective-permute-start.4 = (bf16[136,512]{1,0:T(8,128)(2,1)S(1)}, bf16[136,512]{1,0:T(8,128)(2,1)S(1)}, u32[]{:S(2)}, u32[]{:S(2)}) collective-permute-start(bf16[136,512]{1,0:T(8,128)(2,1)S(1)} %get-tuple-element.42), channel_id=1, source_target_pairs={{0,8},{4,12},{8,0},{12,4},{1,9},{5,13},{9,1},{13,5},{2,10},{6,14},... | collective-permute-start | bytes 417800 | tf_op jit(solution)/shard_map/ppermute | solution.py:31
  45.0 0.0 collective-permute-done.2.refs_1_
  45.0 0.0 collective-permute-done.1.refs_0_
  45.0 1.8 %shard_map.111 = (bf16[136,512]{1,0:T(8,128)(2,1)S(1)}, bf16[136,512]{1,0:T(8,128)(2,1)S(1)}, bf16[512,1792]{1,0:T(8,128)(2,1)S(1)}) custom-call(bf16[4,32,576]{2,1,0:T(8,128)(2,1)S(1)} %collective-permute-done.1.refs_0_, bf16[4,32,576]{2,1,0:T(8,128)(2,1)S(1)} %collective-permute-done.2.refs_1_, ...), custom_call_target="tpu_custom_call" | custom-call | flops 570425344 | bytes 4194304 | tf_op jit(solution)/shard_map/pallas_call | solution.py:47
  46.8 0.1 collective-permute-start.3
  46.9 2.6 %collective-permute-start.5 = (bf16[136,512]{1,0:T(8,128)(2,1)S(1)}, bf16[136,512]{1,0:T(8,128)(2,1)S(1)}, u32[]{:S(2)}, u32[]{:S(2)}) collective-permute-start(bf16[136,512]{1,0:T(8,128)(2,1)S(1)} %get-tuple-element.43), channel_id=1, source_target_pairs={{0,12},{4,8},{8,4},{12,0},{1,13},{5,9},{9,5},{13,1},{2,14},{6,10},... | collective-permute-start | bytes 417800 | tf_op jit(solution)/shard_map/ppermute | solution.py:31
  49.5 1.6 %shard_map.110 = (bf16[136,512]{1,0:T(8,128)(2,1)S(1)}, bf16[512,1792]{1,0:T(8,128)(2,1)S(1)}) custom-call(bf16[4,32,576]{2,1,0:T(8,128)(2,1)S(1)} %get-tuple-element.37.refs_0_, bf16[2,576,1024]{2,1,0:T(8,128)(2,1)S(1)} %get-tuple-element.38.refs_1_.refs_2_, s32[4,128]{1,0:T(4,128)S(1)} %get-tuple-element.39.refs_2_.refs_3_, bf16[4096,1792]{1,0:T(8,128)(2,1)} %refs_0_.8), custom_call_target="tpu_custom_call" | custom-call | flops 285212672 | bytes 4194304 | tf_op jit(solution)/shard_map/pallas_call | solution.py:47
  51.0 1.3 %collective-permute-done.4.refs_2_ = bf16[136,512]{1,0:T(8,128)(2,1)S(1)} collective-permute-done((bf16[136,512]{1,0:T(8,128)(2,1)S(1)}, bf16[136,512]{1,0:T(8,128)(2,1)S(1)}, u32[]{:S(2)}, u32[]{:S(2)}) %collective-permute-start.4) | collective-permute-done | bytes 139296 | tf_op jit(solution)/shard_map/ppermute | solution.py:31
  52.3 5.1 %collective-permute-done.3.refs_1_ = bf16[136,512]{1,0:T(8,128)(2,1)S(1)} collective-permute-done((bf16[136,512]{1,0:T(8,128)(2,1)S(1)}, bf16[136,512]{1,0:T(8,128)(2,1)S(1)}, u32[]{:S(2)}, u32[]{:S(2)}) %collective-permute-start.3) | collective-permute-done | bytes 139296 | tf_op jit(solution)/shard_map/ppermute | solution.py:31
  57.5 0.0 collective-permute-done.5.refs_3_
  57.5 0.0 collective-permute-done.6.refs_5_
  57.5 0.0 collective-permute-done.8.refs_7_
  57.5 1.7 %shard_map.114.refs_0_ = bf16[4,4096]{1,0:T(4,128)(2,1)S(1)} custom-call(bf16[136,512]{1,0:T(8,128)(2,1)S(1)} %get-tuple-element.40.refs_0_, bf16[136,512]{1,0:T(8,128)(2,1)S(1)} %collective-permute-done.3.refs_1_, bf16[136,512]{1,0:T(8,128)(2,1)S(1)} %collective-permute-done.4.refs_2_, bf16[136,512]{1,0:T(8,128)(2,1)S(1)} %collective-permute-done.5.refs_3_, ...), custom_call_target="tpu_custom_call" | custom-call | flops 16777216 | bytes 4194304 | tf_op jit(solution)/shard_map/pallas_call | solution.py:47
  59.2 1.5 %collective-permute-start.10 = (bf16[4,4096]{1,0:T(4,128)(2,1)S(1)}, bf16[4,4096]{1,0:T(4,128)(2,1)S(1)}, u32[]{:S(2)}, u32[]{:S(2)}) collective-permute-start(bf16[4,4096]{1,0:T(4,128)(2,1)S(1)} %shard_map.114.refs_0_), channel_id=1, source_target_pairs={{0,2},{1,3},{2,0},{3,1},{4,6},{5,7},{6,4},{7,5},{8,10},{9,11},{10,... | collective-permute-start | bytes 98312 | tf_op jit(solution)/shard_map/ppermute | solution.py:31
  60.6 0.0 collective-permute-start.11
  60.6 0.7 collective-permute-start.9
  61.3 2.0 %shard_map.115.refs_5_ = bf16[1024,1792]{1,0:T(8,128)(2,1)S(1)} custom-call(bf16[4096,1792]{1,0:T(8,128)(2,1)} %refs_0_.8), custom_call_target="tpu_custom_call" | custom-call | bytes 7340032 | tf_op jit(solution)/shard_map/pallas_call | solution.py:47
  63.4 1.8 %shard_map.116.refs_8_ = bf16[768,1792]{1,0:T(8,128)(2,1)S(1)} custom-call(bf16[4096,1792]{1,0:T(8,128)(2,1)} %refs_0_.8), custom_call_target="tpu_custom_call" | custom-call | bytes 5505024 | tf_op jit(solution)/shard_map/pallas_call | solution.py:47
  65.2 1.8 %shard_map.117.refs_9_ = bf16[768,1792]{1,0:T(8,128)(2,1)S(1)} custom-call(bf16[4096,1792]{1,0:T(8,128)(2,1)} %refs_0_.8), custom_call_target="tpu_custom_call" | custom-call | bytes 5505024 | tf_op jit(solution)/shard_map/pallas_call | solution.py:47
  67.0 0.0 collective-permute-done.10.refs_2_
  67.0 0.0 collective-permute-done.11.refs_3_
  67.0 0.0 collective-permute-done.9.refs_1_
  67.0 2.0 %shard_map.118.refs_0_ = bf16[16,1792]{1,0:T(8,128)(2,1)S(1)} custom-call(bf16[4,4096]{1,0:T(4,128)(2,1)S(1)} %shard_map.114.refs_0_, bf16[4,4096]{1,0:T(4,128)(2,1)S(1)} %collective-permute-done.9.refs_1_, bf16[4,4096]{1,0:T(4,128)(2,1)S(1)} %collective-permute-done.10.refs_2_, bf16[4,4096]{1,0:T(4,128)(2,1)S(1)} %collective-permute-done.11.refs_3_, ...), custom_call_target="tpu_custom_call" | custom-call | flops 234881024 | bytes 4194304 | tf_op jit(solution)/shard_map/pallas_call | solution.py:47
  69.0 0.6 collective-permute-start.12
  69.6 1.1 %collective-permute-start.13 = (bf16[16,1792]{1,0:T(8,128)(2,1)S(1)}, bf16[16,1792]{1,0:T(8,128)(2,1)S(1)}, u32[]{:S(2)}, u32[]{:S(2)}) collective-permute-start(bf16[16,1792]{1,0:T(8,128)(2,1)S(1)} %shard_map.118.refs_0_), channel_id=1, source_target_pairs={{0,8},{4,12},{8,0},{12,4},{1,9},{5,13},{9,1},{13,5},{2,10},{6,14},... | collective-permute-start | bytes 172040 | tf_op jit(solution)/shard_map/ppermute | solution.py:31
  70.7 2.7 %collective-permute-start.14 = (bf16[16,1792]{1,0:T(8,128)(2,1)S(1)}, bf16[16,1792]{1,0:T(8,128)(2,1)S(1)}, u32[]{:S(2)}, u32[]{:S(2)}) collective-permute-start(bf16[16,1792]{1,0:T(8,128)(2,1)S(1)} %shard_map.118.refs_0_), channel_id=1, source_target_pairs={{0,12},{4,8},{8,4},{12,0},{1,13},{5,9},{9,5},{13,1},{2,14},{6,10},... | collective-permute-start | bytes 172040 | tf_op jit(solution)/shard_map/ppermute | solution.py:31
  73.4 3.4 %shard_map.119.refs_7_.up_ref = bf16[1792,2304]{1,0:T(8,128)(2,1)S(1)} custom-call(bf16[1792,2304]{1,0:T(8,128)(2,1)} %refs_0_.9), custom_call_target="tpu_custom_call" | custom-call | bytes 16515072 | tf_op jit(solution)/shard_map/pallas_call | solution.py:47
  76.8 0.0 collective-permute-done.12.refs_1_
  76.8 0.8 collective-permute-done.13.refs_2_
  77.6 0.0 collective-permute-done.14.refs_3_
  77.6 1.3 %shard_map.120 = (bf16[16,2432]{1,0:T(8,128)(2,1)S(1)}, bf16[16,1792]{1,0:T(8,128)(2,1)S(1)}, f32[16,128]{1,0:T(8,128)S(1)}, f32[4,1792]{1,0:T(4,128)S(1)}) custom-call(bf16[16,1792]{1,0:T(8,128)(2,1)S(1)} %shard_map.118.refs_0_, bf16[16,1792]{1,0:T(8,128)(2,1)S(1)} %collective-permute-done.12.refs_1_, bf16[16,1792]{1,0:T(8,128)(2,1)S(1)} %collective-permute-done.13.refs_2_, ...), custom_call_target="tpu_custom_call" | custom-call | flops 132120576 | bytes 4194304 | tf_op jit(solution)/shard_map/pallas_call | solution.py:47
  78.9 0.0 collective-permute-start.15
  78.9 1.2 %shard_map.121.keep_ref = f32[16,2304]{1,0:T(8,128)S(1)} custom-call(bf16[16,1792]{1,0:T(8,128)(2,1)S(1)} %get-tuple-element.58.scaled_ref, bf16[1792,2304]{1,0:T(8,128)(2,1)S(1)} %get-tuple-element.55.refs_6_.gate_ref, bf16[1792,2304]{1,0:T(8,128)(2,1)S(1)} %shard_map.119.refs_7_.up_ref), custom_call_target="tpu_custom_call" | custom-call | flops 132120576 | bytes 4194304 | tf_op jit(solution)/shard_map/pallas_call | solution.py:47
  80.1 0.1 collective-permute-done.15.got_ref
  80.2 0.2 shard_map.122
  80.3 1.5 %collective-permute-start.16 = (bf16[16,2432]{1,0:T(8,128)(2,1)S(1)}, bf16[16,2432]{1,0:T(8,128)(2,1)S(1)}, u32[]{:S(2)}, u32[]{:S(2)}) collective-permute-start(bf16[16,2432]{1,0:T(8,128)(2,1)S(1)} %get-tuple-element.63), channel_id=1, source_target_pairs={{0,2},{2,0},{1,3},{3,1},{4,6},{6,4},{5,7},{7,5},{8,10},{10,8},{9,1... | collective-permute-start | bytes 233480 | tf_op jit(solution)/shard_map/ppermute | solution.py:31
  81.8 3.2 %collective-permute-done.16.refs_1_ = bf16[16,2432]{1,0:T(8,128)(2,1)S(1)} collective-permute-done((bf16[16,2432]{1,0:T(8,128)(2,1)S(1)}, bf16[16,2432]{1,0:T(8,128)(2,1)S(1)}, u32[]{:S(2)}, u32[]{:S(2)}) %collective-permute-start.16) | collective-permute-done | bytes 77856 | tf_op jit(solution)/shard_map/ppermute | solution.py:31
  85.0 0.2 shard_map.123.own_ref
  85.2 0.1 collective-permute-start.17
  85.3 3.4 %shard_map.124.weight_ref = bf16[2304,1792]{1,0:T(8,128)(2,1)S(1)} custom-call(bf16[2304,1792]{1,0:T(8,128)(2,1)} %refs_0_.10), custom_call_target="tpu_custom_call" | custom-call | bytes 16515072 | tf_op jit(solution)/shard_map/pallas_call | solution.py:47
  88.7 0.7 shard_map.125.partial_ref
  89.3 0.0 collective-permute-done.17.other_ref
  89.3 0.7 shard_map.126
  90.0 1.2 %collective-permute-start.18 = (bf16[4,1792]{1,0:T(4,128)(2,1)S(1)}, bf16[4,1792]{1,0:T(4,128)(2,1)S(1)}, u32[]{:S(2)}, u32[]{:S(2)}) collective-permute-start(bf16[4,1792]{1,0:T(4,128)(2,1)S(1)} %get-tuple-element.66), channel_id=1, source_target_pairs={{0,4},{4,0},{8,12},{12,8},{1,5},{5,1},{9,13},{13,9},{2,6},{6,2},{1... | collective-permute-start | bytes 43016 | tf_op jit(solution)/shard_map/ppermute | solution.py:31
  91.3 1.3 %collective-permute-start.19 = (bf16[4,1792]{1,0:T(4,128)(2,1)S(1)}, bf16[4,1792]{1,0:T(4,128)(2,1)S(1)}, u32[]{:S(2)}, u32[]{:S(2)}) collective-permute-start(bf16[4,1792]{1,0:T(4,128)(2,1)S(1)} %get-tuple-element.67), channel_id=1, source_target_pairs={{0,8},{4,12},{8,0},{12,4},{1,9},{5,13},{9,1},{13,5},{2,10},{6,14},... | collective-permute-start | bytes 43016 | tf_op jit(solution)/shard_map/ppermute | solution.py:31
  92.6 1.9 %collective-permute-start.20 = (bf16[4,1792]{1,0:T(4,128)(2,1)S(1)}, bf16[4,1792]{1,0:T(4,128)(2,1)S(1)}, u32[]{:S(2)}, u32[]{:S(2)}) collective-permute-start(bf16[4,1792]{1,0:T(4,128)(2,1)S(1)} %get-tuple-element.68), channel_id=1, source_target_pairs={{0,12},{4,8},{8,4},{12,0},{1,13},{5,9},{9,5},{13,1},{2,14},{6,10},... | collective-permute-start | bytes 43016 | tf_op jit(solution)/shard_map/ppermute | solution.py:31
  94.5 0.0 collective-permute-done.18.refs_2_
  94.5 1.5 %collective-permute-done.19.refs_3_ = bf16[4,1792]{1,0:T(4,128)(2,1)S(1)} collective-permute-done((bf16[4,1792]{1,0:T(4,128)(2,1)S(1)}, bf16[4,1792]{1,0:T(4,128)(2,1)S(1)}, u32[]{:S(2)}, u32[]{:S(2)}) %collective-permute-start.19) | collective-permute-done | bytes 14368 | tf_op jit(solution)/shard_map/ppermute | solution.py:31
  96.0 2.1 %collective-permute-done.20.refs_4_ = bf16[4,1792]{1,0:T(4,128)(2,1)S(1)} collective-permute-done((bf16[4,1792]{1,0:T(4,128)(2,1)S(1)}, bf16[4,1792]{1,0:T(4,128)(2,1)S(1)}, u32[]{:S(2)}, u32[]{:S(2)}) %collective-permute-start.20) | collective-permute-done | bytes 14368 | tf_op jit(solution)/shard_map/ppermute | solution.py:31
  98.1 0.6 shard_map.127
Async XLA Ops:
  0.0 26.3 %copy-start = (bf16[4,32,576]{2,1,0:T(8,128)(2,1)S(1)}, bf16[4,32,576]{2,1,0:T(8,128)(2,1)}, u32[]{:S(2)}) copy-start(bf16[4,32,576]{2,1,0:T(8,128)(2,1)} %refs_0_.4) | copy-start | bytes 442372
  0.0 26.3 %collective-permute-start.7 = (bf16[32,128,128]{2,1,0:T(8,128)(2,1)}, bf16[32,128,128]{2,1,0:T(8,128)(2,1)S(1)}, u32[]{:S(2)}, u32[]{:S(2)}) collective-permute-start(bf16[32,128,128]{2,1,0:T(8,128)(2,1)} %refs_1_.1), channel_id=1, source_target_pairs={{0,2},{2,0},{1,3},{3,1},{4,6},{6,4},{5,7},{7,5},{8,10},{10,8},{9,1... | collective-permute-start | bytes 3145736 | tf_op jit(solution)/shard_map/ppermute | solution.py:31
  3.0 54.5 %collective-permute-start.6 = (bf16[32,128,128]{2,1,0:T(8,128)(2,1)}, bf16[32,128,128]{2,1,0:T(8,128)(2,1)S(1)}, u32[]{:S(2)}, u32[]{:S(2)}) collective-permute-start(bf16[32,128,128]{2,1,0:T(8,128)(2,1)} %refs_1_.1), channel_id=1, source_target_pairs={{0,1},{1,0},{2,3},{3,2},{4,5},{5,4},{6,7},{7,6},{8,9},{9,8},{10,11... | collective-permute-start | bytes 3145736 | tf_op jit(solution)/shard_map/ppermute | solution.py:31
  26.3 31.1 %collective-permute-start.8 = (bf16[32,128,128]{2,1,0:T(8,128)(2,1)S(1)}, bf16[32,128,128]{2,1,0:T(8,128)(2,1)S(1)}, u32[]{:S(2)}, u32[]{:S(2)}) collective-permute-start(bf16[32,128,128]{2,1,0:T(8,128)(2,1)S(1)} %collective-permute-done.7.refs_6_), channel_id=1, source_target_pairs={{0,1},{1,0},{2,3},{3,2},{4,5},{5,4},{6,7},{7,6},{8,9},{9,8},{10,11... | collective-permute-start | bytes 3145736 | tf_op jit(solution)/shard_map/ppermute | solution.py:31
  26.3 11.3 %collective-permute-start = (bf16[4,32,576]{2,1,0:T(8,128)(2,1)S(1)}, bf16[4,32,576]{2,1,0:T(8,128)(2,1)S(1)}, u32[]{:S(2)}, u32[]{:S(2)}) collective-permute-start(bf16[4,32,576]{2,1,0:T(8,128)(2,1)S(1)} %copy-done), channel_id=1, source_target_pairs={{0,8},{4,12},{8,0},{12,4},{1,9},{5,13},{9,1},{13,5},{2,10},{6,14},... | collective-permute-start | bytes 442376 | tf_op jit(solution)/shard_map/ppermute | solution.py:31
  29.2 15.8 %collective-permute-start.2 = (bf16[4,32,576]{2,1,0:T(8,128)(2,1)S(1)}, bf16[4,32,576]{2,1,0:T(8,128)(2,1)S(1)}, u32[]{:S(2)}, u32[]{:S(2)}) collective-permute-start(bf16[4,32,576]{2,1,0:T(8,128)(2,1)S(1)} %copy-done), channel_id=1, source_target_pairs={{0,4},{4,0},{8,12},{12,8},{1,5},{5,1},{9,13},{13,9},{2,6},{6,2},{1... | collective-permute-start | bytes 442376 | tf_op jit(solution)/shard_map/ppermute | solution.py:31
  37.7 7.3 %collective-permute-start.1 = (bf16[4,32,576]{2,1,0:T(8,128)(2,1)S(1)}, bf16[4,32,576]{2,1,0:T(8,128)(2,1)S(1)}, u32[]{:S(2)}, u32[]{:S(2)}) collective-permute-start(bf16[4,32,576]{2,1,0:T(8,128)(2,1)S(1)} %collective-permute-done.refs_0_), channel_id=1, source_target_pairs={{0,4},{4,0},{8,12},{12,8},{1,5},{5,1},{9,13},{13,9},{2,6},{6,2},{1... | collective-permute-start | bytes 442376 | tf_op jit(solution)/shard_map/ppermute | solution.py:31
  41.6 10.8 %collective-permute-start.4 = (bf16[136,512]{1,0:T(8,128)(2,1)S(1)}, bf16[136,512]{1,0:T(8,128)(2,1)S(1)}, u32[]{:S(2)}, u32[]{:S(2)}) collective-permute-start(bf16[136,512]{1,0:T(8,128)(2,1)S(1)} %get-tuple-element.42), channel_id=1, source_target_pairs={{0,8},{4,12},{8,0},{12,4},{1,9},{5,13},{9,1},{13,5},{2,10},{6,14},... | collective-permute-start | bytes 417800 | tf_op jit(solution)/shard_map/ppermute | solution.py:31
  46.8 10.7 %collective-permute-start.3 = (bf16[136,512]{1,0:T(8,128)(2,1)S(1)}, bf16[136,512]{1,0:T(8,128)(2,1)S(1)}, u32[]{:S(2)}, u32[]{:S(2)}) collective-permute-start(bf16[136,512]{1,0:T(8,128)(2,1)S(1)} %get-tuple-element.41), channel_id=1, source_target_pairs={{0,4},{4,0},{8,12},{12,8},{1,5},{5,1},{9,13},{13,9},{2,6},{6,2},{1... | collective-permute-start | bytes 417800 | tf_op jit(solution)/shard_map/ppermute | solution.py:31
  46.9 10.6 %collective-permute-start.5 = (bf16[136,512]{1,0:T(8,128)(2,1)S(1)}, bf16[136,512]{1,0:T(8,128)(2,1)S(1)}, u32[]{:S(2)}, u32[]{:S(2)}) collective-permute-start(bf16[136,512]{1,0:T(8,128)(2,1)S(1)} %get-tuple-element.43), channel_id=1, source_target_pairs={{0,12},{4,8},{8,4},{12,0},{1,13},{5,9},{9,5},{13,1},{2,14},{6,10},... | collective-permute-start | bytes 417800 | tf_op jit(solution)/shard_map/ppermute | solution.py:31
  59.2 7.8 %collective-permute-start.10 = (bf16[4,4096]{1,0:T(4,128)(2,1)S(1)}, bf16[4,4096]{1,0:T(4,128)(2,1)S(1)}, u32[]{:S(2)}, u32[]{:S(2)}) collective-permute-start(bf16[4,4096]{1,0:T(4,128)(2,1)S(1)} %shard_map.114.refs_0_), channel_id=1, source_target_pairs={{0,2},{1,3},{2,0},{3,1},{4,6},{5,7},{6,4},{7,5},{8,10},{9,11},{10,... | collective-permute-start | bytes 98312 | tf_op jit(solution)/shard_map/ppermute | solution.py:31
  60.6 6.3 %collective-permute-start.11 = (bf16[4,4096]{1,0:T(4,128)(2,1)S(1)}, bf16[4,4096]{1,0:T(4,128)(2,1)S(1)}, u32[]{:S(2)}, u32[]{:S(2)}) collective-permute-start(bf16[4,4096]{1,0:T(4,128)(2,1)S(1)} %shard_map.114.refs_0_), channel_id=1, source_target_pairs={{0,3},{1,2},{2,1},{3,0},{4,7},{5,6},{6,5},{7,4},{8,11},{9,10},{10,... | collective-permute-start | bytes 98312 | tf_op jit(solution)/shard_map/ppermute | solution.py:31
  60.6 6.3 %collective-permute-start.9 = (bf16[4,4096]{1,0:T(4,128)(2,1)S(1)}, bf16[4,4096]{1,0:T(4,128)(2,1)S(1)}, u32[]{:S(2)}, u32[]{:S(2)}) collective-permute-start(bf16[4,4096]{1,0:T(4,128)(2,1)S(1)} %shard_map.114.refs_0_), channel_id=1, source_target_pairs={{0,1},{1,0},{2,3},{3,2},{4,5},{5,4},{6,7},{7,6},{8,9},{9,8},{10,11... | collective-permute-start | bytes 98312 | tf_op jit(solution)/shard_map/ppermute | solution.py:31
  69.0 7.8 %collective-permute-start.12 = (bf16[16,1792]{1,0:T(8,128)(2,1)S(1)}, bf16[16,1792]{1,0:T(8,128)(2,1)S(1)}, u32[]{:S(2)}, u32[]{:S(2)}) collective-permute-start(bf16[16,1792]{1,0:T(8,128)(2,1)S(1)} %shard_map.118.refs_0_), channel_id=1, source_target_pairs={{0,4},{4,0},{8,12},{12,8},{1,5},{5,1},{9,13},{13,9},{2,6},{6,2},{1... | collective-permute-start | bytes 172040 | tf_op jit(solution)/shard_map/ppermute | solution.py:31
  69.6 8.0 %collective-permute-start.13 = (bf16[16,1792]{1,0:T(8,128)(2,1)S(1)}, bf16[16,1792]{1,0:T(8,128)(2,1)S(1)}, u32[]{:S(2)}, u32[]{:S(2)}) collective-permute-start(bf16[16,1792]{1,0:T(8,128)(2,1)S(1)} %shard_map.118.refs_0_), channel_id=1, source_target_pairs={{0,8},{4,12},{8,0},{12,4},{1,9},{5,13},{9,1},{13,5},{2,10},{6,14},... | collective-permute-start | bytes 172040 | tf_op jit(solution)/shard_map/ppermute | solution.py:31
  70.7 6.9 %collective-permute-start.14 = (bf16[16,1792]{1,0:T(8,128)(2,1)S(1)}, bf16[16,1792]{1,0:T(8,128)(2,1)S(1)}, u32[]{:S(2)}, u32[]{:S(2)}) collective-permute-start(bf16[16,1792]{1,0:T(8,128)(2,1)S(1)} %shard_map.118.refs_0_), channel_id=1, source_target_pairs={{0,12},{4,8},{8,4},{12,0},{1,13},{5,9},{9,5},{13,1},{2,14},{6,10},... | collective-permute-start | bytes 172040 | tf_op jit(solution)/shard_map/ppermute | solution.py:31
  78.9 1.3 %collective-permute-start.15 = (bf16[16,2432]{1,0:T(8,128)(2,1)S(1)}, bf16[16,2432]{1,0:T(8,128)(2,1)S(1)}, u32[]{:S(2)}, u32[]{:S(2)}) collective-permute-start(bf16[16,2432]{1,0:T(8,128)(2,1)S(1)} %get-tuple-element.60), channel_id=1, source_target_pairs={{0,1},{1,0},{2,3},{3,2},{4,5},{5,4},{6,7},{7,6},{8,9},{9,8},{10,11... | collective-permute-start | bytes 233480 | tf_op jit(solution)/shard_map/ppermute | solution.py:31
  80.3 4.7 %collective-permute-start.16 = (bf16[16,2432]{1,0:T(8,128)(2,1)S(1)}, bf16[16,2432]{1,0:T(8,128)(2,1)S(1)}, u32[]{:S(2)}, u32[]{:S(2)}) collective-permute-start(bf16[16,2432]{1,0:T(8,128)(2,1)S(1)} %get-tuple-element.63), channel_id=1, source_target_pairs={{0,2},{2,0},{1,3},{3,1},{4,6},{6,4},{5,7},{7,5},{8,10},{10,8},{9,1... | collective-permute-start | bytes 233480 | tf_op jit(solution)/shard_map/ppermute | solution.py:31
  85.2 4.1 %collective-permute-start.17 = (bf16[16,1152]{1,0:T(8,128)(2,1)S(1)}, bf16[16,1152]{1,0:T(8,128)(2,1)S(1)}, u32[]{:S(2)}, u32[]{:S(2)}) collective-permute-start(bf16[16,1152]{1,0:T(8,128)(2,1)S(1)} %shard_map.123.own_ref), channel_id=1, source_target_pairs={{0,1},{1,0},{2,3},{3,2},{4,5},{5,4},{6,7},{7,6},{8,9},{9,8},{10,11... | collective-permute-start | bytes 110600 | tf_op jit(solution)/shard_map/ppermute | solution.py:31
  90.0 4.5 %collective-permute-start.18 = (bf16[4,1792]{1,0:T(4,128)(2,1)S(1)}, bf16[4,1792]{1,0:T(4,128)(2,1)S(1)}, u32[]{:S(2)}, u32[]{:S(2)}) collective-permute-start(bf16[4,1792]{1,0:T(4,128)(2,1)S(1)} %get-tuple-element.66), channel_id=1, source_target_pairs={{0,4},{4,0},{8,12},{12,8},{1,5},{5,1},{9,13},{13,9},{2,6},{6,2},{1... | collective-permute-start | bytes 43016 | tf_op jit(solution)/shard_map/ppermute | solution.py:31
  91.3 4.7 %collective-permute-start.19 = (bf16[4,1792]{1,0:T(4,128)(2,1)S(1)}, bf16[4,1792]{1,0:T(4,128)(2,1)S(1)}, u32[]{:S(2)}, u32[]{:S(2)}) collective-permute-start(bf16[4,1792]{1,0:T(4,128)(2,1)S(1)} %get-tuple-element.67), channel_id=1, source_target_pairs={{0,8},{4,12},{8,0},{12,4},{1,9},{5,13},{9,1},{13,5},{2,10},{6,14},... | collective-permute-start | bytes 43016 | tf_op jit(solution)/shard_map/ppermute | solution.py:31
  92.6 5.5 %collective-permute-start.20 = (bf16[4,1792]{1,0:T(4,128)(2,1)S(1)}, bf16[4,1792]{1,0:T(4,128)(2,1)S(1)}, u32[]{:S(2)}, u32[]{:S(2)}) collective-permute-start(bf16[4,1792]{1,0:T(4,128)(2,1)S(1)} %get-tuple-element.68), channel_id=1, source_target_pairs={{0,12},{4,8},{8,4},{12,0},{1,13},{5,9},{9,5},{13,1},{2,14},{6,10},... | collective-permute-start | bytes 43016 | tf_op jit(solution)/shard_map/ppermute | solution.py:31

commit v5 on v2

--- a/solution.py
+++ b/solution.py
@@ -65,10 +65,28 @@
     return high, middle, (rest - middle.astype(f32)).astype(bf16)
 
 
-def fetch(arrays, lengths=None, positions=None):
+def fetch_rows(array, first, last):
+    def body(source, target, done):
+        copy = pltpu.make_async_copy(source.at[pl.ds(first, last - first)], target, done)
+        copy.start()
+        copy.wait()
+
+    shape = (last - first, *array.shape[1:])
+    return call(
+        body,
+        pltpu.VMEM(shape, array.dtype),
+        [pltpu.with_memory_space_constraint(array, pltpu.HBM)],
+        [IN_HBM],
+        [pltpu.SemaphoreType.DMA],
+        limit=1 << 20,
+        cost=(0, 4 * shape[0] * array.shape[1]),
+    )
+
+
+def fetch(arrays, lengths, positions):
     count = len(arrays)
-    scalars = [] if positions is None else [lengths, positions]
-    rows = positions.shape[0] if scalars else 0
+    scalars = [lengths, positions]
+    rows = positions.shape[0]
     copied = count + len(scalars)
 
     def body(*refs):
@@ -83,14 +101,13 @@
             copy.start()
         for copy in copies[count:]:
             copy.wait()
-        if scalars:
-            length_ref, position_ref = in_smem
-            row = lax.broadcasted_iota(jnp.int32, (rows, LANES), 0)
-            seen = jnp.zeros((rows, LANES), jnp.int32)
-            for r in range(rows):
-                bound = jnp.minimum(length_ref[r // MTP], position_ref[r] + 1)
-                seen = jnp.where(row == r, bound, seen)
-            refs[0][...] = seen
+        length_ref, position_ref = in_smem
+        row = lax.broadcasted_iota(jnp.int32, (rows, LANES), 0)
+        seen = jnp.zeros((rows, LANES), jnp.int32)
+        for r in range(rows):
+            bound = jnp.minimum(length_ref[r // MTP], position_ref[r] + 1)
+            seen = jnp.where(row == r, bound, seen)
+        refs[0][...] = seen
         for copy in copies[:count]:
             copy.wait()
 
@@ -98,7 +115,7 @@
     return call(
         body,
         [pltpu.VMEM(x.shape, x.dtype) for x in arrays]
-        + ([pltpu.VMEM((rows, LANES), jnp.int32)] if scalars else []),
+        + [pltpu.VMEM((rows, LANES), jnp.int32)],
         [pltpu.with_memory_space_constraint(x, pltpu.HBM) for x in [*arrays, *scalars]],
         [IN_HBM] * copied,
         [pltpu.SMEM(x.shape, x.dtype) for x in scalars] + [pltpu.SemaphoreType.DMA((copied,))],
@@ -107,7 +124,7 @@
     )
 
 
-def attend(groups, cache, seen, weight, span):
+def attend(groups, cache, seen):
     count = len(groups)
     rows, heads, width = groups[0].shape
     seqs, _, context = cache.shape
@@ -116,11 +133,8 @@
 
     def body(*refs):
         query_refs = refs[:count]
-        cache_ref, seen_ref, weight_ref = refs[count : count + 3]
-        out_refs = refs[count + 3 : 2 * count + 3]
-        fetched, done = refs[2 * count + 3 :]
-        copy = pltpu.make_async_copy(weight_ref.at[pl.ds(span[0], span[1] - span[0])], fetched, done)
-        copy.start()
+        cache_ref, seen_ref = refs[count : count + 2]
+        out_refs = refs[count + 2 :]
         offset = lax.axis_index("ctx") * context
         total = count * per_seq
         tops, sums = [[] for _ in range(count)], [[] for _ in range(count)]
@@ -157,29 +171,27 @@
             for i, part in enumerate(three_parts(table[:STAT_ROWS])):
                 out_refs[g][per_group:, i * LANES : (i + 1) * LANES] = part
             out_refs[g][per_group:, 3 * LANES :] = jnp.zeros((STAT_ROWS, LATENT - 3 * LANES), bf16)
-        copy.wait()
 
     shape = jax.ShapeDtypeStruct((per_group + STAT_ROWS, LATENT), bf16)
     flops = 2 * count * rows * heads * context * (width + LATENT)
     return call(
         body,
-        [shape] * count + [pltpu.VMEM((span[1] - span[0], weight.shape[1]), weight.dtype)],
-        [*groups, in_vmem(cache), seen, pltpu.with_memory_space_constraint(weight, pltpu.HBM)],
-        [IN_VMEM] * (count + 2) + [IN_HBM],
-        [pltpu.SemaphoreType.DMA],
+        [shape] * count,
+        [*groups, in_vmem(cache), seen],
+        [IN_VMEM] * (count + 2),
         limit=ATTEND_LIMIT,
         cost=(flops, 4 << 20),
     )
 
 
-def join_and_project(parts, pieces, rows, heads, after):
+def join_and_project(parts, pieces, rows, heads):
     count, slices = len(parts), len(pieces)
     per_group = rows * heads
     _, depth, vdim = pieces[0].shape
 
     def body(*refs):
         part_refs, piece_refs = refs[:count], refs[count : count + slices]
-        value_ref, attended = refs[count + slices + 1 :]
+        value_ref, attended = refs[count + slices :]
         me = lax.axis_index(("role", "seq"))
         tops, sums = [], []
         for ref in part_refs:
@@ -207,8 +219,8 @@
     return call(
         body,
         jax.ShapeDtypeStruct((rows, heads * vdim), bf16),
-        [*parts, *[in_vmem(piece) for piece in pieces], after],
-        [IN_VMEM] * (count + slices + 1),
+        [*parts, *[in_vmem(piece) for piece in pieces]],
+        [IN_VMEM] * (count + slices),
         [pltpu.VMEM((slices, per_group, depth), f32)],
         cost=(2 * rows * heads * LATENT * vdim, 4 << 20),
     )
@@ -451,57 +463,41 @@
 
     along = listed(exchange([value_up_weight] * roles, "role"))
     groups = exchange([queries] * blocks, "ctx", [*evens, 1])
-    gate_fast, up_own, groups[0], cache_fast, seen = fetch(
-        [gate_weight, value_up_weight, queries, jnp.swapaxes(cache, 1, 2)], lengths, positions
-    )
+    groups[0], cache_fast, seen = fetch([queries, jnp.swapaxes(cache, 1, 2)], lengths, positions)
+
+    def attend_some(source):
+        return dict(zip(source, attend(list(source.values()), cache_fast, seen)))
+
+    answers = attend_some({0: groups[0]})
     relayed = {}
     for mask in evens:
         relayed[mask + 1] = xor_permute(groups[mask], "ctx", 1)
-
-    unit = out_proj.shape[0] // 16
-    cuts = [0, 5 * unit, 11 * unit, 16 * unit]
-    out_parts = []
-
-    def attend_and_answer(source, masks):
-        k = len(out_parts)
-        *outs, part = attend(
-            [source[mask] for mask in masks], cache_fast, seen, out_proj, (cuts[k], cuts[k + 1])
-        )
-        out_parts.append(part)
-        return dict(zip(masks, outs))
-
-    partial = attend_and_answer(groups, evens)
-    answers = exchange({0: None, **partial}, "ctx", evens)
-    near = attend_and_answer(groups, [0, 1])
-    far = attend_and_answer(relayed, odds)
-    answers |= exchange({0: near[0], **far}, "ctx", odds)
-    answers |= exchange(near, "ctx", [1])
-
-    up_weight, part = lax.optimization_barrier((up_weight, out_parts[-1]))
-    out_parts[-1] = part
-    up_fast, residual, gain = fetch([up_weight, residual, norm_gain])
-    *far_rows, gain = lax.optimization_barrier((*along[1:], gain))
-    across = [xor_permute(along[0], "seq", 1)]
-    across += [xor_permute(piece, "seq", 1) for piece in far_rows]
-    up_pieces = [up_own, *[piece for pair in zip([None, *far_rows], across) for piece in pair][1:]]
-
-    values = join_and_project(listed(answers), up_pieces, rows, heads, gain)
+    even = attend_some({mask: groups[mask] for mask in evens})
+    answers |= exchange({0: answers[0], **even}, "ctx", evens)
+    far = attend_some({**relayed, 1: groups[1]})
+    answers |= exchange({0: answers[0], **far}, "ctx", odds)
+    answers |= exchange({0: answers[0], **far}, "ctx", [1])
+
+    cut = out_proj.shape[0] // 8 * 5
+    out_a = fetch_rows(out_proj, 0, cut)
+    *along, out_a = lax.optimization_barrier((*along, out_a))
+    across = [xor_permute(piece, "seq", 1) for piece in along]
+    out_b = fetch_rows(out_proj, cut, out_proj.shape[0])
+    up_pieces = [piece for pair in zip(along, across) for piece in pair]
+
+    values = join_and_project(listed(answers), up_pieces, rows, heads)
     shared = listed(exchange([values] * members, ("role", "seq")))
-    product = project_out(shared, out_parts)
-    down_weight, product = lax.optimization_barrier((down_weight, product))
-    terms = listed(exchange([product] * blocks, "ctx"))
-    (down_fast,) = fetch([down_weight])
-
-    send, scaled, squares, base = gate_and_up_away(terms, residual, gain, gate_fast, up_fast)
+    terms = listed(exchange([project_out(shared, [out_a, out_b])] * blocks, "ctx"))
+    send, scaled, squares, base = gate_and_up_away(terms, residual, norm_gain, gate_weight, up_weight)
     got = xor_permute(send, "seq", 1)
-    keep = gate_and_up_here(scaled, gate_fast, up_fast)
+    keep = gate_and_up_here(scaled, gate_weight, up_weight)
     keep, send = add_core(keep, squares, got)
     pieces = listed(exchange([send] * roles, "role"))[1:]
     features = norm_gain.shape[0] * members
     hidden = activate(keep, pieces, features)
     other = xor_permute(hidden, "seq", 1)
-    own = project_down_own(hidden, down_fast)
-    last = exchange(project_down_other(other, down_fast, own), "ctx")
+    own = project_down_own(hidden, down_weight)
+    last = exchange(project_down_other(other, down_weight, own), "ctx")
     return finish(base, listed(last))
 
 

time: 84.5 us -> 93.8 us (1.11)
  waiting for transfers between devices: 29.8 us -> 44.1 us
  Pallas kernels: 27.1 us -> 22 us
    ppermute x21, waiting for transfers between devices: 29.8 us -> 44.1 us  [xor_permute(): return lax.ppermute(x, axis, [(i, i ^ mask) for i in range(size)])]
    pallas_call x15, Pallas kernels: 27.1 us -> 22 us  [call(): pl.pallas_call(body, out_shape=outs, in_specs=specs, out_specs=jax.tree.m...]
  transfers between devices with their start and end apart: 21 -> 21, of which waited for: 11 -> 11; matrix products, arithmetic and copies ran while one was open for 0% -> 0% of each run, Pallas kernels for 24% -> 16%
where the time goes in v5:
time: 93.8 us; the launch traced here: 93.6 us
  waiting for transfers between devices  44.1 us (47%)
  starting transfers between devices  27.2 us (29%)
  Pallas kernels  22 us (23%)
    ppermute x21, waiting for transfers between devices, xor_permute(): return lax.ppermute(x, axis, [(i, i ^ mask) for i in range(size)])  44.1 us
    ppermute x21, starting transfers between devices, xor_permute(): return lax.ppermute(x, axis, [(i, i ^ mask) for i in range(size)])  27.2 us
    pallas_call x15, Pallas kernels, call(): pl.pallas_call(body, out_shape=outs, in_specs=specs, out_specs=jax.tree.m...  22 us
  transfers between devices with their start and end apart: 21, of which 11 were waited for; matrix products, arithmetic and copies ran while one was open for 0% of the time, Pallas kernels for 16%

profile of v5, /device:TPU:0, one launch (start us, length us, event | category | flops | bytes accessed | tf_op | source)
XLA Modules:
  0.0 93.6 jit_solution(17735684937357636487)
XLA Ops:
  0.0 3.0 %collective-permute-start.6 = (bf16[32,128,128]{2,1,0:T(8,128)(2,1)}, bf16[32,128,128]{2,1,0:T(8,128)(2,1)S(1)}, u32[]{:S(2)}, u32[]{:S(2)}) collective-permute-start(bf16[32,128,128]{2,1,0:T(8,128)(2,1)} %refs_4_.1), channel_id=1, source_target_pairs={{0,2},{2,0},{1,3},{3,1},{4,6},{6,4},{5,7},{7,5},{8,10},{10,8},{9,1... | collective-permute-start | bytes 3145736 | tf_op jit(solution)/shard_map/ppermute | solution.py:30
  3.0 3.7 %shard_map.113.refs_4_ = bf16[2560,1792]{1,0:T(8,128)(2,1)S(1)} custom-call(bf16[4096,1792]{1,0:T(8,128)(2,1)} %source.3), custom_call_target="tpu_custom_call" | custom-call | bytes 18350080 | tf_op jit(solution)/shard_map/pallas_call | solution.py:46
  6.6 19.8 %collective-permute-done.6.refs_6_ = bf16[32,128,128]{2,1,0:T(8,128)(2,1)S(1)} collective-permute-done((bf16[32,128,128]{2,1,0:T(8,128)(2,1)}, bf16[32,128,128]{2,1,0:T(8,128)(2,1)S(1)}, u32[]{:S(2)}, u32[]{:S(2)}) %collective-permute-start.6) | collective-permute-done | bytes 1048608 | tf_op jit(solution)/shard_map/ppermute | solution.py:30
  26.4 0.0 collective-permute-start.7
  26.4 0.5 collective-permute-start.8
  26.9 2.8 %collective-permute-start = (bf16[4,32,576]{2,1,0:T(8,128)(2,1)S(1)}, bf16[4,32,576]{2,1,0:T(8,128)(2,1)S(1)}, u32[]{:S(2)}, u32[]{:S(2)}) collective-permute-start(bf16[4,32,576]{2,1,0:T(8,128)(2,1)S(1)} %copy-done.3), channel_id=1, source_target_pairs={{0,8},{4,12},{8,0},{12,4},{1,9},{5,13},{9,1},{13,5},{2,10},{6,14},... | collective-permute-start | bytes 442376 | tf_op jit(solution)/shard_map/ppermute | solution.py:30
  29.7 1.6 %collective-permute-start.2 = (bf16[4,32,576]{2,1,0:T(8,128)(2,1)S(1)}, bf16[4,32,576]{2,1,0:T(8,128)(2,1)S(1)}, u32[]{:S(2)}, u32[]{:S(2)}) collective-permute-start(bf16[4,32,576]{2,1,0:T(8,128)(2,1)S(1)} %copy-done.3), channel_id=1, source_target_pairs={{0,4},{4,0},{8,12},{12,8},{1,5},{5,1},{9,13},{13,9},{2,6},{6,2},{1... | collective-permute-start | bytes 442376 | tf_op jit(solution)/shard_map/ppermute | solution.py:30
  31.3 6.4 %collective-permute-done.refs_0_ = bf16[4,32,576]{2,1,0:T(8,128)(2,1)S(1)} collective-permute-done((bf16[4,32,576]{2,1,0:T(8,128)(2,1)S(1)}, bf16[4,32,576]{2,1,0:T(8,128)(2,1)S(1)}, u32[]{:S(2)}, u32[]{:S(2)}) %collective-permute-start) | collective-permute-done | bytes 147488 | tf_op jit(solution)/shard_map/ppermute | solution.py:30
  37.7 0.6 collective-permute-start.1
  38.3 1.7 %shard_map.109 = (bf16[4,32,576]{2,1,0:T(8,128)(2,1)S(1)}, bf16[2,576,1024]{2,1,0:T(8,128)(2,1)S(1)}, s32[4,128]{1,0:T(4,128)S(1)}) custom-call(bf16[4,32,576]{2,1,0:T(8,128)(2,1)} %refs_0_.1, bf16[2,576,1024]{2,1,0:T(8,128)(2,1)} %bitcast.7, s32[2]{0:T(128)} %refs_2_.1, s32[4]{0:T(128)} %refs_3_.1), custom_call_target="tpu_custom_call" | custom-call | bytes 5013504 | tf_op jit(solution)/shard_map/pallas_call | solution.py:46
  40.0 1.6 %shard_map.112 = bf16[136,512]{1,0:T(8,128)(2,1)S(1)} custom-call(bf16[4,32,576]{2,1,0:T(8,128)(2,1)S(1)} %collective-permute-done.refs_0_, bf16[2,576,1024]{2,1,0:T(8,128)(2,1)S(1)} %get-tuple-element.24.refs_1_.refs_2_, s32[4,128]{1,0:T(4,128)S(1)} %get-tuple-element.25.refs_2_.refs_3_), custom_call_target="tpu_custom_call" | custom-call | flops 285212672 | bytes 4194304 | tf_op jit(solution)/shard_map/pallas_call | solution.py:46
  41.6 3.4 %collective-permute-start.4 = (bf16[136,512]{1,0:T(8,128)(2,1)S(1)}, bf16[136,512]{1,0:T(8,128)(2,1)S(1)}, u32[]{:S(2)}, u32[]{:S(2)}) collective-permute-start(bf16[136,512]{1,0:T(8,128)(2,1)S(1)} %shard_map.112), channel_id=1, source_target_pairs={{0,8},{4,12},{8,0},{12,4},{1,9},{5,13},{9,1},{13,5},{2,10},{6,14},... | collective-permute-start | bytes 417800 | tf_op jit(solution)/shard_map/ppermute | solution.py:30
  45.0 0.0 collective-permute-done.2.refs_1_
  45.0 0.0 collective-permute-done.1.refs_0_
  45.0 1.8 %shard_map.111 = (bf16[136,512]{1,0:T(8,128)(2,1)S(1)}, bf16[136,512]{1,0:T(8,128)(2,1)S(1)}) custom-call(bf16[4,32,576]{2,1,0:T(8,128)(2,1)S(1)} %collective-permute-done.1.refs_0_, bf16[4,32,576]{2,1,0:T(8,128)(2,1)S(1)} %collective-permute-done.2.refs_1_, bf16[2,576,1024]{2,1,0:T(8,128)(2,1)S(1)} %get-tuple-element.24.refs_1_.refs_2_, ...), custom_call_target="tpu_custom_call" | custom-call | flops 570425344 | bytes 4194304 | tf_op jit(solution)/shard_map/pallas_call | solution.py:46
  46.8 0.1 collective-permute-start.3
  46.8 2.7 %collective-permute-start.5 = (bf16[136,512]{1,0:T(8,128)(2,1)S(1)}, bf16[136,512]{1,0:T(8,128)(2,1)S(1)}, u32[]{:S(2)}, u32[]{:S(2)}) collective-permute-start(bf16[136,512]{1,0:T(8,128)(2,1)S(1)} %get-tuple-element.27), channel_id=1, source_target_pairs={{0,12},{4,8},{8,4},{12,0},{1,13},{5,9},{9,5},{13,1},{2,14},{6,10},... | collective-permute-start | bytes 417800 | tf_op jit(solution)/shard_map/ppermute | solution.py:30
  49.5 1.5 %shard_map.110.refs_0_ = bf16[136,512]{1,0:T(8,128)(2,1)S(1)} custom-call(bf16[4,32,576]{2,1,0:T(8,128)(2,1)S(1)} %get-tuple-element.23.refs_0_, bf16[2,576,1024]{2,1,0:T(8,128)(2,1)S(1)} %get-tuple-element.24.refs_1_.refs_2_, s32[4,128]{1,0:T(4,128)S(1)} %get-tuple-element.25.refs_2_.refs_3_), custom_call_target="tpu_custom_call" | custom-call | flops 285212672 | bytes 4194304 | tf_op jit(solution)/shard_map/pallas_call | solution.py:46
  51.1 1.5 %collective-permute-done.4.refs_2_ = bf16[136,512]{1,0:T(8,128)(2,1)S(1)} collective-permute-done((bf16[136,512]{1,0:T(8,128)(2,1)S(1)}, bf16[136,512]{1,0:T(8,128)(2,1)S(1)}, u32[]{:S(2)}, u32[]{:S(2)}) %collective-permute-start.4) | collective-permute-done | bytes 139296 | tf_op jit(solution)/shard_map/ppermute | solution.py:30
  52.6 4.8 %collective-permute-done.3.refs_1_ = bf16[136,512]{1,0:T(8,128)(2,1)S(1)} collective-permute-done((bf16[136,512]{1,0:T(8,128)(2,1)S(1)}, bf16[136,512]{1,0:T(8,128)(2,1)S(1)}, u32[]{:S(2)}, u32[]{:S(2)}) %collective-permute-start.3) | collective-permute-done | bytes 139296 | tf_op jit(solution)/shard_map/ppermute | solution.py:30
  57.4 0.0 collective-permute-done.5.refs_3_
  57.4 0.0 collective-permute-done.7.refs_5_
  57.4 0.0 collective-permute-done.8.refs_7_
  57.4 0.0 slice-start
  57.4 0.0 slice-start.2
  57.4 1.7 %shard_map.114.refs_0_ = bf16[4,4096]{1,0:T(4,128)(2,1)S(1)} custom-call(bf16[136,512]{1,0:T(8,128)(2,1)S(1)} %shard_map.110.refs_0_, bf16[136,512]{1,0:T(8,128)(2,1)S(1)} %collective-permute-done.3.refs_1_, bf16[136,512]{1,0:T(8,128)(2,1)S(1)} %collective-permute-done.4.refs_2_, bf16[136,512]{1,0:T(8,128)(2,1)S(1)} %collective-permute-done.5.refs_3_, ...), custom_call_target="tpu_custom_call" | custom-call | flops 16777216 | bytes 4194304 | tf_op jit(solution)/shard_map/pallas_call | solution.py:46
  59.1 1.5 %collective-permute-start.10 = (bf16[4,4096]{1,0:T(4,128)(2,1)S(1)}, bf16[4,4096]{1,0:T(4,128)(2,1)S(1)}, u32[]{:S(2)}, u32[]{:S(2)}) collective-permute-start(bf16[4,4096]{1,0:T(4,128)(2,1)S(1)} %shard_map.114.refs_0_), channel_id=1, source_target_pairs={{0,2},{1,3},{2,0},{3,1},{4,6},{5,7},{6,4},{7,5},{8,10},{9,11},{10,... | collective-permute-start | bytes 98312 | tf_op jit(solution)/shard_map/ppermute | solution.py:30
  60.6 0.0 collective-permute-start.11
  60.6 0.6 collective-permute-start.9
  61.2 3.3 %shard_map.115.refs_5_ = bf16[1536,1792]{1,0:T(8,128)(2,1)S(1)} custom-call(bf16[4096,1792]{1,0:T(8,128)(2,1)} %source.3), custom_call_target="tpu_custom_call" | custom-call | bytes 11010048 | tf_op jit(solution)/shard_map/pallas_call | solution.py:46
  64.6 0.0 copy-start.1
  64.6 0.0 copy-start.2
  64.6 0.0 collective-permute-done.10.refs_2_
  64.6 0.0 collective-permute-done.11.refs_3_
  64.6 0.0 collective-permute-done.9.refs_1_
  64.6 2.0 %shard_map.116.refs_0_ = bf16[16,1792]{1,0:T(8,128)(2,1)S(1)} custom-call(bf16[4,4096]{1,0:T(4,128)(2,1)S(1)} %shard_map.114.refs_0_, bf16[4,4096]{1,0:T(4,128)(2,1)S(1)} %collective-permute-done.9.refs_1_, bf16[4,4096]{1,0:T(4,128)(2,1)S(1)} %collective-permute-done.10.refs_2_, bf16[4,4096]{1,0:T(4,128)(2,1)S(1)} %collective-permute-done.11.refs_3_, ...), custom_call_target="tpu_custom_call" | custom-call | flops 234881024 | bytes 4194304 | tf_op jit(solution)/shard_map/pallas_call | solution.py:46
  66.6 0.6 collective-permute-start.12
  67.2 1.1 %collective-permute-start.13 = (bf16[16,1792]{1,0:T(8,128)(2,1)S(1)}, bf16[16,1792]{1,0:T(8,128)(2,1)S(1)}, u32[]{:S(2)}, u32[]{:S(2)}) collective-permute-start(bf16[16,1792]{1,0:T(8,128)(2,1)S(1)} %shard_map.116.refs_0_), channel_id=1, source_target_pairs={{0,8},{4,12},{8,0},{12,4},{1,9},{5,13},{9,1},{13,5},{2,10},{6,14},... | collective-permute-start | bytes 172040 | tf_op jit(solution)/shard_map/ppermute | solution.py:30
  68.3 2.7 %collective-permute-start.14 = (bf16[16,1792]{1,0:T(8,128)(2,1)S(1)}, bf16[16,1792]{1,0:T(8,128)(2,1)S(1)}, u32[]{:S(2)}, u32[]{:S(2)}) collective-permute-start(bf16[16,1792]{1,0:T(8,128)(2,1)S(1)} %shard_map.116.refs_0_), channel_id=1, source_target_pairs={{0,12},{4,8},{8,4},{12,0},{1,13},{5,9},{9,5},{13,1},{2,14},{6,10},... | collective-permute-start | bytes 172040 | tf_op jit(solution)/shard_map/ppermute | solution.py:30
  71.0 0.4 collective-permute-done.12.refs_1_
  71.4 3.3 %collective-permute-done.13.refs_2_ = bf16[16,1792]{1,0:T(8,128)(2,1)S(1)} collective-permute-done((bf16[16,1792]{1,0:T(8,128)(2,1)S(1)}, bf16[16,1792]{1,0:T(8,128)(2,1)S(1)}, u32[]{:S(2)}, u32[]{:S(2)}) %collective-permute-start.13) | collective-permute-done | bytes 57376 | tf_op jit(solution)/shard_map/ppermute | solution.py:30
  74.8 0.0 collective-permute-done.14.refs_3_
  74.8 0.0 slice-done.2
  74.8 0.0 slice-start.4
  74.9 1.3 %shard_map.117 = (bf16[16,2432]{1,0:T(8,128)(2,1)S(1)}, bf16[16,1792]{1,0:T(8,128)(2,1)S(1)}, f32[16,128]{1,0:T(8,128)S(1)}, f32[4,1792]{1,0:T(4,128)S(1)}) custom-call(bf16[16,1792]{1,0:T(8,128)(2,1)S(1)} %shard_map.116.refs_0_, bf16[16,1792]{1,0:T(8,128)(2,1)S(1)} %collective-permute-done.12.refs_1_, bf16[16,1792]{1,0:T(8,128)(2,1)S(1)} %collective-permute-done.13.refs_2_, ...), custom_call_target="tpu_custom_call" | custom-call | flops 132120576 | bytes 4194304 | tf_op jit(solution)/shard_map/pallas_call | solution.py:46
  76.2 0.0 collective-permute-start.15
  76.2 0.0 slice-start.5
  76.2 1.2 %shard_map.118.keep_ref = f32[16,2304]{1,0:T(8,128)S(1)} custom-call(bf16[16,1792]{1,0:T(8,128)(2,1)S(1)} %get-tuple-element.32.scaled_ref, bf16[1792,2304]{1,0:T(8,128)(2,1)S(1)} %bitcast.2, bf16[1792,2304]{1,0:T(8,128)(2,1)S(1)} %bitcast.4), custom_call_target="tpu_custom_call" | custom-call | flops 132120576 | bytes 4194304 | tf_op jit(solution)/shard_map/pallas_call | solution.py:46
  77.4 0.1 collective-permute-done.15.got_ref
  77.5 0.2 shard_map.119
  77.6 1.5 %collective-permute-start.16 = (bf16[16,2432]{1,0:T(8,128)(2,1)S(1)}, bf16[16,2432]{1,0:T(8,128)(2,1)S(1)}, u32[]{:S(2)}, u32[]{:S(2)}) collective-permute-start(bf16[16,2432]{1,0:T(8,128)(2,1)S(1)} %get-tuple-element.36), channel_id=1, source_target_pairs={{0,2},{2,0},{1,3},{3,1},{4,6},{6,4},{5,7},{7,5},{8,10},{10,8},{9,1... | collective-permute-start | bytes 233480 | tf_op jit(solution)/shard_map/ppermute | solution.py:30
  79.1 3.2 %collective-permute-done.16.refs_1_ = bf16[16,2432]{1,0:T(8,128)(2,1)S(1)} collective-permute-done((bf16[16,2432]{1,0:T(8,128)(2,1)S(1)}, bf16[16,2432]{1,0:T(8,128)(2,1)S(1)}, u32[]{:S(2)}, u32[]{:S(2)}) %collective-permute-start.16) | collective-permute-done | bytes 77856 | tf_op jit(solution)/shard_map/ppermute | solution.py:30
  82.3 0.2 shard_map.120.own_ref
  82.5 0.1 collective-permute-start.17
  82.6 0.7 shard_map.121.partial_ref
  83.3 0.5 collective-permute-done.17.other_ref
  83.8 0.7 shard_map.122
  84.5 1.2 %collective-permute-start.18 = (bf16[4,1792]{1,0:T(4,128)(2,1)S(1)}, bf16[4,1792]{1,0:T(4,128)(2,1)S(1)}, u32[]{:S(2)}, u32[]{:S(2)}) collective-permute-start(bf16[4,1792]{1,0:T(4,128)(2,1)S(1)} %get-tuple-element.38), channel_id=1, source_target_pairs={{0,4},{4,0},{8,12},{12,8},{1,5},{5,1},{9,13},{13,9},{2,6},{6,2},{1... | collective-permute-start | bytes 43016 | tf_op jit(solution)/shard_map/ppermute | solution.py:30
  85.7 1.7 %collective-permute-start.19 = (bf16[4,1792]{1,0:T(4,128)(2,1)S(1)}, bf16[4,1792]{1,0:T(4,128)(2,1)S(1)}, u32[]{:S(2)}, u32[]{:S(2)}) collective-permute-start(bf16[4,1792]{1,0:T(4,128)(2,1)S(1)} %get-tuple-element.39), channel_id=1, source_target_pairs={{0,8},{4,12},{8,0},{12,4},{1,9},{5,13},{9,1},{13,5},{2,10},{6,14},... | collective-permute-start | bytes 43016 | tf_op jit(solution)/shard_map/ppermute | solution.py:30
  87.5 1.5 %collective-permute-start.20 = (bf16[4,1792]{1,0:T(4,128)(2,1)S(1)}, bf16[4,1792]{1,0:T(4,128)(2,1)S(1)}, u32[]{:S(2)}, u32[]{:S(2)}) collective-permute-start(bf16[4,1792]{1,0:T(4,128)(2,1)S(1)} %get-tuple-element.40), channel_id=1, source_target_pairs={{0,12},{4,8},{8,4},{12,0},{1,13},{5,9},{9,5},{13,1},{2,14},{6,10},... | collective-permute-start | bytes 43016 | tf_op jit(solution)/shard_map/ppermute | solution.py:30
  89.0 0.0 collective-permute-done.18.refs_2_
  89.0 1.4 %collective-permute-done.19.refs_3_ = bf16[4,1792]{1,0:T(4,128)(2,1)S(1)} collective-permute-done((bf16[4,1792]{1,0:T(4,128)(2,1)S(1)}, bf16[4,1792]{1,0:T(4,128)(2,1)S(1)}, u32[]{:S(2)}, u32[]{:S(2)}) %collective-permute-start.19) | collective-permute-done | bytes 14368 | tf_op jit(solution)/shard_map/ppermute | solution.py:30
  90.4 2.6 %collective-permute-done.20.refs_4_ = bf16[4,1792]{1,0:T(4,128)(2,1)S(1)} collective-permute-done((bf16[4,1792]{1,0:T(4,128)(2,1)S(1)}, bf16[4,1792]{1,0:T(4,128)(2,1)S(1)}, u32[]{:S(2)}, u32[]{:S(2)}) %collective-permute-start.20) | collective-permute-done | bytes 14368 | tf_op jit(solution)/shard_map/ppermute | solution.py:30
  93.0 0.6 shard_map.123
  (16 shorter events, 0.0 us)
Async XLA Ops:
  0.0 26.4 %copy-start = (bf16[32,128,128]{2,1,0:T(8,128)(2,1)S(1)}, bf16[32,128,128]{2,1,0:T(8,128)(2,1)}, u32[]{:S(2)}) copy-start(bf16[32,128,128]{2,1,0:T(8,128)(2,1)} %refs_4_.1) | copy-start | bytes 3145732
  0.0 26.9 %copy-start.3 = (bf16[4,32,576]{2,1,0:T(8,128)(2,1)S(1)}, bf16[4,32,576]{2,1,0:T(8,128)(2,1)}, u32[]{:S(2)}) copy-start(bf16[4,32,576]{2,1,0:T(8,128)(2,1)} %refs_0_.1) | copy-start | bytes 442372
  0.0 26.4 %collective-permute-start.6 = (bf16[32,128,128]{2,1,0:T(8,128)(2,1)}, bf16[32,128,128]{2,1,0:T(8,128)(2,1)S(1)}, u32[]{:S(2)}, u32[]{:S(2)}) collective-permute-start(bf16[32,128,128]{2,1,0:T(8,128)(2,1)} %refs_4_.1), channel_id=1, source_target_pairs={{0,2},{2,0},{1,3},{3,1},{4,6},{6,4},{5,7},{7,5},{8,10},{10,8},{9,1... | collective-permute-start | bytes 3145736 | tf_op jit(solution)/shard_map/ppermute | solution.py:30
  26.4 31.0 %collective-permute-start.7 = (bf16[32,128,128]{2,1,0:T(8,128)(2,1)S(1)}, bf16[32,128,128]{2,1,0:T(8,128)(2,1)S(1)}, u32[]{:S(2)}, u32[]{:S(2)}) collective-permute-start(bf16[32,128,128]{2,1,0:T(8,128)(2,1)S(1)} %copy-done), channel_id=1, source_target_pairs={{0,1},{1,0},{2,3},{3,2},{4,5},{5,4},{6,7},{7,6},{8,9},{9,8},{10,11... | collective-permute-start | bytes 3145736 | tf_op jit(solution)/shard_map/ppermute | solution.py:30
  26.4 31.0 %collective-permute-start.8 = (bf16[32,128,128]{2,1,0:T(8,128)(2,1)S(1)}, bf16[32,128,128]{2,1,0:T(8,128)(2,1)S(1)}, u32[]{:S(2)}, u32[]{:S(2)}) collective-permute-start(bf16[32,128,128]{2,1,0:T(8,128)(2,1)S(1)} %collective-permute-done.6.refs_6_), channel_id=1, source_target_pairs={{0,1},{1,0},{2,3},{3,2},{4,5},{5,4},{6,7},{7,6},{8,9},{9,8},{10,11... | collective-permute-start | bytes 3145736 | tf_op jit(solution)/shard_map/ppermute | solution.py:30
  26.9 10.8 %collective-permute-start = (bf16[4,32,576]{2,1,0:T(8,128)(2,1)S(1)}, bf16[4,32,576]{2,1,0:T(8,128)(2,1)S(1)}, u32[]{:S(2)}, u32[]{:S(2)}) collective-permute-start(bf16[4,32,576]{2,1,0:T(8,128)(2,1)S(1)} %copy-done.3), channel_id=1, source_target_pairs={{0,8},{4,12},{8,0},{12,4},{1,9},{5,13},{9,1},{13,5},{2,10},{6,14},... | collective-permute-start | bytes 442376 | tf_op jit(solution)/shard_map/ppermute | solution.py:30
  29.7 15.3 %collective-permute-start.2 = (bf16[4,32,576]{2,1,0:T(8,128)(2,1)S(1)}, bf16[4,32,576]{2,1,0:T(8,128)(2,1)S(1)}, u32[]{:S(2)}, u32[]{:S(2)}) collective-permute-start(bf16[4,32,576]{2,1,0:T(8,128)(2,1)S(1)} %copy-done.3), channel_id=1, source_target_pairs={{0,4},{4,0},{8,12},{12,8},{1,5},{5,1},{9,13},{13,9},{2,6},{6,2},{1... | collective-permute-start | bytes 442376 | tf_op jit(solution)/shard_map/ppermute | solution.py:30
  37.7 7.3 %collective-permute-start.1 = (bf16[4,32,576]{2,1,0:T(8,128)(2,1)S(1)}, bf16[4,32,576]{2,1,0:T(8,128)(2,1)S(1)}, u32[]{:S(2)}, u32[]{:S(2)}) collective-permute-start(bf16[4,32,576]{2,1,0:T(8,128)(2,1)S(1)} %collective-permute-done.refs_0_), channel_id=1, source_target_pairs={{0,4},{4,0},{8,12},{12,8},{1,5},{5,1},{9,13},{13,9},{2,6},{6,2},{1... | collective-permute-start | bytes 442376 | tf_op jit(solution)/shard_map/ppermute | solution.py:30
  41.6 11.0 %collective-permute-start.4 = (bf16[136,512]{1,0:T(8,128)(2,1)S(1)}, bf16[136,512]{1,0:T(8,128)(2,1)S(1)}, u32[]{:S(2)}, u32[]{:S(2)}) collective-permute-start(bf16[136,512]{1,0:T(8,128)(2,1)S(1)} %shard_map.112), channel_id=1, source_target_pairs={{0,8},{4,12},{8,0},{12,4},{1,9},{5,13},{9,1},{13,5},{2,10},{6,14},... | collective-permute-start | bytes 417800 | tf_op jit(solution)/shard_map/ppermute | solution.py:30
  46.8 10.6 %collective-permute-start.3 = (bf16[136,512]{1,0:T(8,128)(2,1)S(1)}, bf16[136,512]{1,0:T(8,128)(2,1)S(1)}, u32[]{:S(2)}, u32[]{:S(2)}) collective-permute-start(bf16[136,512]{1,0:T(8,128)(2,1)S(1)} %get-tuple-element.26), channel_id=1, source_target_pairs={{0,4},{4,0},{8,12},{12,8},{1,5},{5,1},{9,13},{13,9},{2,6},{6,2},{1... | collective-permute-start | bytes 417800 | tf_op jit(solution)/shard_map/ppermute | solution.py:30
  46.8 10.6 %collective-permute-start.5 = (bf16[136,512]{1,0:T(8,128)(2,1)S(1)}, bf16[136,512]{1,0:T(8,128)(2,1)S(1)}, u32[]{:S(2)}, u32[]{:S(2)}) collective-permute-start(bf16[136,512]{1,0:T(8,128)(2,1)S(1)} %get-tuple-element.27), channel_id=1, source_target_pairs={{0,12},{4,8},{8,4},{12,0},{1,13},{5,9},{9,5},{13,1},{2,14},{6,10},... | collective-permute-start | bytes 417800 | tf_op jit(solution)/shard_map/ppermute | solution.py:30
  57.4 17.4 %slice-start = ((s8[8257536]{0:T(1024)(128)(4,1)}), s8[4194304]{0:T(1024)(128)(4,1)S(1)}, s32[]{:S(2)}) async-start(s8[8257536]{0:T(1024)(128)(4,1)} %bitcast.1), calls=%async_computation | async-start | bytes 8388608
  57.4 17.4 %slice-start.2 = ((s8[8257536]{0:T(1024)(128)(4,1)}), s8[4194304]{0:T(1024)(128)(4,1)S(1)}, s32[]{:S(2)}) async-start(s8[8257536]{0:T(1024)(128)(4,1)} %bitcast.3), calls=%async_computation.2 | async-start | bytes 8388608
  59.1 15.7 %slice-start.1 = ((s8[8257536]{0:T(1024)(128)(4,1)}), s8[4063232]{0:T(1024)(128)(4,1)S(1)}, s32[]{:S(2)}) async-start(s8[8257536]{0:T(1024)(128)(4,1)} %bitcast.1), calls=%async_computation.1 | async-start | bytes 8126464
  59.1 15.7 %slice-start.3 = ((s8[8257536]{0:T(1024)(128)(4,1)}), s8[4063232]{0:T(1024)(128)(4,1)S(1)}, s32[]{:S(2)}) async-start(s8[8257536]{0:T(1024)(128)(4,1)} %bitcast.3), calls=%async_computation.3 | async-start | bytes 8126464
  59.1 5.5 %collective-permute-start.10 = (bf16[4,4096]{1,0:T(4,128)(2,1)S(1)}, bf16[4,4096]{1,0:T(4,128)(2,1)S(1)}, u32[]{:S(2)}, u32[]{:S(2)}) collective-permute-start(bf16[4,4096]{1,0:T(4,128)(2,1)S(1)} %shard_map.114.refs_0_), channel_id=1, source_target_pairs={{0,2},{1,3},{2,0},{3,1},{4,6},{5,7},{6,4},{7,5},{8,10},{9,11},{10,... | collective-permute-start | bytes 98312 | tf_op jit(solution)/shard_map/ppermute | solution.py:30
  60.6 4.0 %collective-permute-start.11 = (bf16[4,4096]{1,0:T(4,128)(2,1)S(1)}, bf16[4,4096]{1,0:T(4,128)(2,1)S(1)}, u32[]{:S(2)}, u32[]{:S(2)}) collective-permute-start(bf16[4,4096]{1,0:T(4,128)(2,1)S(1)} %shard_map.114.refs_0_), channel_id=1, source_target_pairs={{0,3},{1,2},{2,1},{3,0},{4,7},{5,6},{6,5},{7,4},{8,11},{9,10},{10,... | collective-permute-start | bytes 98312 | tf_op jit(solution)/shard_map/ppermute | solution.py:30
  60.6 4.0 %collective-permute-start.9 = (bf16[4,4096]{1,0:T(4,128)(2,1)S(1)}, bf16[4,4096]{1,0:T(4,128)(2,1)S(1)}, u32[]{:S(2)}, u32[]{:S(2)}) collective-permute-start(bf16[4,4096]{1,0:T(4,128)(2,1)S(1)} %shard_map.114.refs_0_), channel_id=1, source_target_pairs={{0,1},{1,0},{2,3},{3,2},{4,5},{5,4},{6,7},{7,6},{8,9},{9,8},{10,11... | collective-permute-start | bytes 98312 | tf_op jit(solution)/shard_map/ppermute | solution.py:30
  64.6 10.2 %copy-start.1 = (bf16[16,1792]{1,0:T(8,128)(2,1)S(1)}, bf16[16,1792]{1,0:T(8,128)(2,1)}, u32[]{:S(2)}) copy-start(bf16[16,1792]{1,0:T(8,128)(2,1)} %refs_4_.2) | copy-start | bytes 172036
  64.6 10.2 %copy-start.2 = (f32[1792]{0:T(1024)S(1)}, f32[1792]{0:T(1024)}, u32[]{:S(2)}) copy-start(f32[1792]{0:T(1024)} %refs_5_.1) | copy-start | bytes 21508
  66.6 4.8 %collective-permute-start.12 = (bf16[16,1792]{1,0:T(8,128)(2,1)S(1)}, bf16[16,1792]{1,0:T(8,128)(2,1)S(1)}, u32[]{:S(2)}, u32[]{:S(2)}) collective-permute-start(bf16[16,1792]{1,0:T(8,128)(2,1)S(1)} %shard_map.116.refs_0_), channel_id=1, source_target_pairs={{0,4},{4,0},{8,12},{12,8},{1,5},{5,1},{9,13},{13,9},{2,6},{6,2},{1... | collective-permute-start | bytes 172040 | tf_op jit(solution)/shard_map/ppermute | solution.py:30
  67.2 7.5 %collective-permute-start.13 = (bf16[16,1792]{1,0:T(8,128)(2,1)S(1)}, bf16[16,1792]{1,0:T(8,128)(2,1)S(1)}, u32[]{:S(2)}, u32[]{:S(2)}) collective-permute-start(bf16[16,1792]{1,0:T(8,128)(2,1)S(1)} %shard_map.116.refs_0_), channel_id=1, source_target_pairs={{0,8},{4,12},{8,0},{12,4},{1,9},{5,13},{9,1},{13,5},{2,10},{6,14},... | collective-permute-start | bytes 172040 | tf_op jit(solution)/shard_map/ppermute | solution.py:30
  68.3 6.4 %collective-permute-start.14 = (bf16[16,1792]{1,0:T(8,128)(2,1)S(1)}, bf16[16,1792]{1,0:T(8,128)(2,1)S(1)}, u32[]{:S(2)}, u32[]{:S(2)}) collective-permute-start(bf16[16,1792]{1,0:T(8,128)(2,1)S(1)} %shard_map.116.refs_0_), channel_id=1, source_target_pairs={{0,12},{4,8},{8,4},{12,0},{1,13},{5,9},{9,5},{13,1},{2,14},{6,10},... | collective-permute-start | bytes 172040 | tf_op jit(solution)/shard_map/ppermute | solution.py:30
  74.8 7.8 %slice-start.4 = ((s8[8257536]{0:T(1024)(128)(4,1)}), s8[4194304]{0:T(1024)(128)(4,1)S(1)}, s32[]{:S(2)}) async-start(s8[8257536]{0:T(1024)(128)(4,1)} %bitcast.5), calls=%async_computation.4 | async-start | bytes 8388608
  76.2 1.3 %collective-permute-start.15 = (bf16[16,2432]{1,0:T(8,128)(2,1)S(1)}, bf16[16,2432]{1,0:T(8,128)(2,1)S(1)}, u32[]{:S(2)}, u32[]{:S(2)}) collective-permute-start(bf16[16,2432]{1,0:T(8,128)(2,1)S(1)} %get-tuple-element.34), channel_id=1, source_target_pairs={{0,1},{1,0},{2,3},{3,2},{4,5},{5,4},{6,7},{7,6},{8,9},{9,8},{10,11... | collective-permute-start | bytes 233480 | tf_op jit(solution)/shard_map/ppermute | solution.py:30
  76.2 6.4 %slice-start.5 = ((s8[8257536]{0:T(1024)(128)(4,1)}), s8[4063232]{0:T(1024)(128)(4,1)S(1)}, s32[]{:S(2)}) async-start(s8[8257536]{0:T(1024)(128)(4,1)} %bitcast.5), calls=%async_computation.5 | async-start | bytes 8126464
  77.6 4.7 %collective-permute-start.16 = (bf16[16,2432]{1,0:T(8,128)(2,1)S(1)}, bf16[16,2432]{1,0:T(8,128)(2,1)S(1)}, u32[]{:S(2)}, u32[]{:S(2)}) collective-permute-start(bf16[16,2432]{1,0:T(8,128)(2,1)S(1)} %get-tuple-element.36), channel_id=1, source_target_pairs={{0,2},{2,0},{1,3},{3,1},{4,6},{6,4},{5,7},{7,5},{8,10},{10,8},{9,1... | collective-permute-start | bytes 233480 | tf_op jit(solution)/shard_map/ppermute | solution.py:30
  82.5 1.3 %collective-permute-start.17 = (bf16[16,1152]{1,0:T(8,128)(2,1)S(1)}, bf16[16,1152]{1,0:T(8,128)(2,1)S(1)}, u32[]{:S(2)}, u32[]{:S(2)}) collective-permute-start(bf16[16,1152]{1,0:T(8,128)(2,1)S(1)} %shard_map.120.own_ref), channel_id=1, source_target_pairs={{0,1},{1,0},{2,3},{3,2},{4,5},{5,4},{6,7},{7,6},{8,9},{9,8},{10,11... | collective-permute-start | bytes 110600 | tf_op jit(solution)/shard_map/ppermute | solution.py:30
  84.5 4.5 %collective-permute-start.18 = (bf16[4,1792]{1,0:T(4,128)(2,1)S(1)}, bf16[4,1792]{1,0:T(4,128)(2,1)S(1)}, u32[]{:S(2)}, u32[]{:S(2)}) collective-permute-start(bf16[4,1792]{1,0:T(4,128)(2,1)S(1)} %get-tuple-element.38), channel_id=1, source_target_pairs={{0,4},{4,0},{8,12},{12,8},{1,5},{5,1},{9,13},{13,9},{2,6},{6,2},{1... | collective-permute-start | bytes 43016 | tf_op jit(solution)/shard_map/ppermute | solution.py:30
  85.7 4.6 %collective-permute-start.19 = (bf16[4,1792]{1,0:T(4,128)(2,1)S(1)}, bf16[4,1792]{1,0:T(4,128)(2,1)S(1)}, u32[]{:S(2)}, u32[]{:S(2)}) collective-permute-start(bf16[4,1792]{1,0:T(4,128)(2,1)S(1)} %get-tuple-element.39), channel_id=1, source_target_pairs={{0,8},{4,12},{8,0},{12,4},{1,9},{5,13},{9,1},{13,5},{2,10},{6,14},... | collective-permute-start | bytes 43016 | tf_op jit(solution)/shard_map/ppermute | solution.py:30
  87.5 5.5 %collective-permute-start.20 = (bf16[4,1792]{1,0:T(4,128)(2,1)S(1)}, bf16[4,1792]{1,0:T(4,128)(2,1)S(1)}, u32[]{:S(2)}, u32[]{:S(2)}) collective-permute-start(bf16[4,1792]{1,0:T(4,128)(2,1)S(1)} %get-tuple-element.40), channel_id=1, source_target_pairs={{0,12},{4,8},{8,4},{12,0},{1,13},{5,9},{9,5},{13,1},{2,14},{6,10},... | collective-permute-start | bytes 43016 | tf_op jit(solution)/shard_map/ppermute | solution.py:30

commit v6 on v4

--- a/solution.py
+++ b/solution.py
@@ -180,14 +180,14 @@
     )
 
 
-def join_and_project(parts, pieces, rows, heads, after):
-    count, slices = len(parts), len(pieces)
+def join_blocks(parts, pieces, rows, heads, slices):
+    count, near = len(parts), len(pieces)
     per_group = rows * heads
     _, depth, vdim = pieces[0].shape
 
     def body(*refs):
-        part_refs, piece_refs = refs[:count], refs[count : count + slices]
-        value_ref, attended = refs[count + slices + 1 :]
+        part_refs, piece_refs = refs[:count], refs[count : count + near]
+        attended, sum_ref = refs[count + near :]
         me = lax.axis_index(("role", "seq"))
         tops, sums = [], []
         for ref in part_refs:
@@ -204,21 +204,46 @@
         joined = (numer / denom).astype(bf16).astype(f32)
         for k in range(slices):
             attended[k] = joined[:, k * depth : (k + 1) * depth]
-        for h in range(heads):
-            total = None
-            for m in range(slices):
-                left = attended[me ^ m, pl.ds(h, rows, stride=heads), :].astype(bf16)
-                term = jnp.dot(left, piece_refs[m][h], preferred_element_type=f32)
-                total = term if total is None else total + term
-            value_ref[:, h * vdim : (h + 1) * vdim] = total.astype(bf16)
-
-    return call(
-        body,
-        jax.ShapeDtypeStruct((rows, heads * vdim), bf16),
-        [*parts, *[in_vmem(piece) for piece in pieces], after],
-        [IN_VMEM] * (count + slices + 1),
-        [pltpu.VMEM((slices, per_group, depth), f32)],
-        cost=(2 * rows * heads * LATENT * vdim, 4 << 20),
+        project_values(attended, piece_refs, range(near), me, rows, heads, sum_ref, None)
+
+    return call(
+        body,
+        [
+            jax.ShapeDtypeStruct((slices, per_group, depth), f32),
+            jax.ShapeDtypeStruct((rows, heads * vdim), f32),
+        ],
+        [*parts, *[in_vmem(piece) for piece in pieces]],
+        [IN_VMEM] * (count + near),
+        cost=(rows * heads * LATENT * vdim, 4 << 20),
+    )
+
+
+def project_values(attended, piece_refs, masks, me, rows, heads, out_ref, sum_ref):
+    vdim = piece_refs[0].shape[2]
+    for h in range(heads):
+        part = slice(h * vdim, (h + 1) * vdim)
+        total = None if sum_ref is None else sum_ref[:, part]
+        for ref, m in zip(piece_refs, masks):
+            left = attended[me ^ m, pl.ds(h, rows, stride=heads), :].astype(bf16)
+            term = jnp.dot(left, ref[h], preferred_element_type=f32)
+            total = term if total is None else total + term
+        out_ref[:, part] = total.astype(out_ref.dtype)
+
+
+def add_values(attended, sums, pieces, masks, heads):
+    far = len(pieces)
+    rows = sums.shape[0]
+
+    def body(attended_ref, sum_ref, *refs):
+        me = lax.axis_index(("role", "seq"))
+        project_values(attended_ref, refs[:far], masks, me, rows, heads, refs[far], sum_ref)
+
+    return call(
+        body,
+        jax.ShapeDtypeStruct(sums.shape, bf16),
+        [attended, sums, *[in_vmem(piece) for piece in pieces]],
+        [IN_VMEM] * (far + 2),
+        cost=(rows * LATENT * sums.shape[1], 4 << 20),
     )
 
 
@@ -473,20 +498,20 @@
     relayed = {}
     for mask in evens:
         relayed[mask + 1] = xor_permute(groups[mask], "ctx", 1)
-    even, even_part = attend_some({mask: groups[mask] for mask in evens}, even_span)
+    even, even_part = attend_some({mask: groups[mask] for mask in [*evens, 1]}, even_span)
     answers |= exchange({0: answers[0], **even}, "ctx", evens)
-    far, odd_part = attend_some({**relayed, 1: groups[1]}, odd_span)
+    far, odd_part = attend_some(relayed, odd_span)
     answers |= exchange({0: answers[0], **far}, "ctx", odds)
-    answers |= exchange({0: answers[0], **far}, "ctx", [1])
+    answers |= exchange({0: answers[0], **even}, "ctx", [1])
 
     gate_fast, up_own, residual, gain = fetch([gate_weight, value_up_weight, residual, norm_gain])
     *far_rows, gain = lax.optimization_barrier((*along[1:], gain))
-    across = [xor_permute(along[0], "seq", 1)]
-    across += [xor_permute(piece, "seq", 1) for piece in far_rows]
-    up_pieces = [up_own, *[piece for pair in zip([None, *far_rows], across) for piece in pair][1:]]
+    near_rows = [up_own, xor_permute(along[0], "seq", 1)]
+    far_rows = [part for piece in far_rows for part in (piece, xor_permute(piece, "seq", 1))]
     (late_part,) = fetch([(out_proj, late_span)])
 
-    values = join_and_project(listed(answers), up_pieces, rows, heads, gain)
+    attended, sums = join_blocks(listed(answers), near_rows, rows, heads, members)
+    values = add_values(attended, sums, far_rows, range(2, members), heads)
     last_out, values = lax.optimization_barrier((out_proj, values))
     shared = listed(exchange([values] * members, ("role", "seq")))
     (last_part,) = fetch([(last_out, last_span)])

time: 99.1 us -> 100 us (level)
  starting transfers between devices: 26.7 us -> 27.8 us
    ppermute x21, starting transfers between devices: 26.7 us -> 27.8 us  [xor_permute(): return lax.ppermute(x, axis, [(i, i ^ mask) for i in range(size)])]
    pallas_call x19 -> x20, Pallas kernels: 31.2 us -> 31.3 us  [call(): pl.pallas_call(body, out_shape=outs, in_specs=specs, out_specs=jax.tree.m...]
  transfers between devices with their start and end apart: 21 -> 21, of which waited for: 9 -> 8; matrix products, arithmetic and copies ran while one was open for 0% -> 0% of each run, Pallas kernels for 25% -> 26%
where the time goes in v6:
time: 100 us
  waiting for transfers between devices  40.7 us (41%)
  Pallas kernels  31.3 us (31%)
  starting transfers between devices  27.8 us (28%)
    ppermute x21, waiting for transfers between devices, xor_permute(): return lax.ppermute(x, axis, [(i, i ^ mask) for i in range(size)])  40.7 us
    pallas_call x20, Pallas kernels, call(): pl.pallas_call(body, out_shape=outs, in_specs=specs, out_specs=jax.tree.m...  31.3 us
    ppermute x21, starting transfers between devices, xor_permute(): return lax.ppermute(x, axis, [(i, i ^ mask) for i in range(size)])  27.8 us
  transfers between devices with their start and end apart: 21, of which 8 were waited for; matrix products, arithmetic and copies ran while one was open for 0% of the time, Pallas kernels for 26%

profile of v6, /device:TPU:0, one launch (start us, length us, event | category | flops | bytes accessed | tf_op | source)
XLA Modules:
  0.0 100.0 jit_solution(14509801148286641297)
XLA Ops:
  0.0 0.0 copy-start
  0.0 3.0 %collective-permute-start.7 = (bf16[32,128,128]{2,1,0:T(8,128)(2,1)}, bf16[32,128,128]{2,1,0:T(8,128)(2,1)S(1)}, u32[]{:S(2)}, u32[]{:S(2)}) collective-permute-start(bf16[32,128,128]{2,1,0:T(8,128)(2,1)} %refs_1_.1), channel_id=1, source_target_pairs={{0,2},{2,0},{1,3},{3,1},{4,6},{6,4},{5,7},{7,5},{8,10},{10,8},{9,1... | collective-permute-start | bytes 3145736 | tf_op jit(solution)/shard_map/ppermute | solution.py:31
  3.0 0.0 collective-permute-start.6
  3.0 3.8 %shard_map.113 = (bf16[1792,2304]{1,0:T(8,128)(2,1)S(1)}, bf16[32,128,128]{2,1,0:T(8,128)(2,1)S(1)}, bf16[16,1792]{1,0:T(8,128)(2,1)S(1)}, f32[1792]{0:T(1024)S(1)}) custom-call(bf16[1792,2304]{1,0:T(8,128)(2,1)} %refs_0_.5, bf16[32,128,128]{2,1,0:T(8,128)(2,1)} %refs_1_.1, bf16[16,1792]{1,0:T(8,128)(2,1)} %refs_2_.3, f32[1792]{0:T(1024)} %refs_3_.7), custom_call_target="tpu_custom_call" | custom-call | bytes 18741248 | tf_op jit(solution)/shard_map/pallas_call | solution.py:47
  6.7 19.6 %collective-permute-done.7.refs_0_ = bf16[32,128,128]{2,1,0:T(8,128)(2,1)S(1)} collective-permute-done((bf16[32,128,128]{2,1,0:T(8,128)(2,1)}, bf16[32,128,128]{2,1,0:T(8,128)(2,1)S(1)}, u32[]{:S(2)}, u32[]{:S(2)}) %collective-permute-start.7) | collective-permute-done | bytes 1048608 | tf_op jit(solution)/shard_map/ppermute | solution.py:31
  26.3 0.0 collective-permute-start.8
  26.3 0.0 copy-done
  26.3 2.8 %collective-permute-start = (bf16[4,32,576]{2,1,0:T(8,128)(2,1)S(1)}, bf16[4,32,576]{2,1,0:T(8,128)(2,1)S(1)}, u32[]{:S(2)}, u32[]{:S(2)}) collective-permute-start(bf16[4,32,576]{2,1,0:T(8,128)(2,1)S(1)} %copy-done), channel_id=1, source_target_pairs={{0,8},{4,12},{8,0},{12,4},{1,9},{5,13},{9,1},{13,5},{2,10},{6,14},... | collective-permute-start | bytes 442376 | tf_op jit(solution)/shard_map/ppermute | solution.py:31
  29.2 1.6 %collective-permute-start.1 = (bf16[4,32,576]{2,1,0:T(8,128)(2,1)S(1)}, bf16[4,32,576]{2,1,0:T(8,128)(2,1)S(1)}, u32[]{:S(2)}, u32[]{:S(2)}) collective-permute-start(bf16[4,32,576]{2,1,0:T(8,128)(2,1)S(1)} %copy-done), channel_id=1, source_target_pairs={{0,4},{4,0},{8,12},{12,8},{1,5},{5,1},{9,13},{13,9},{2,6},{6,2},{1... | collective-permute-start | bytes 442376 | tf_op jit(solution)/shard_map/ppermute | solution.py:31
  30.8 6.9 %collective-permute-done.refs_0_ = bf16[4,32,576]{2,1,0:T(8,128)(2,1)S(1)} collective-permute-done((bf16[4,32,576]{2,1,0:T(8,128)(2,1)S(1)}, bf16[4,32,576]{2,1,0:T(8,128)(2,1)S(1)}, u32[]{:S(2)}, u32[]{:S(2)}) %collective-permute-start) | collective-permute-done | bytes 147488 | tf_op jit(solution)/shard_map/ppermute | solution.py:31
  37.7 0.6 collective-permute-start.4
  38.3 1.7 %shard_map.109 = (bf16[4,32,576]{2,1,0:T(8,128)(2,1)S(1)}, bf16[2,576,1024]{2,1,0:T(8,128)(2,1)S(1)}, s32[4,128]{1,0:T(4,128)S(1)}) custom-call(bf16[4,32,576]{2,1,0:T(8,128)(2,1)} %refs_0_.4, bf16[2,576,1024]{2,1,0:T(8,128)(2,1)} %bitcast.1, s32[2]{0:T(128)} %refs_2_.2, s32[4]{0:T(128)} %refs_3_.4), custom_call_target="tpu_custom_call" | custom-call | bytes 5013504 | tf_op jit(solution)/shard_map/pallas_call | solution.py:47
  40.0 0.0 collective-permute-done.1.refs_1_
  40.0 1.8 %shard_map.111 = (bf16[136,512]{1,0:T(8,128)(2,1)S(1)}, bf16[136,512]{1,0:T(8,128)(2,1)S(1)}, bf16[512,1792]{1,0:T(8,128)(2,1)S(1)}) custom-call(bf16[4,32,576]{2,1,0:T(8,128)(2,1)S(1)} %collective-permute-done.refs_0_, bf16[4,32,576]{2,1,0:T(8,128)(2,1)S(1)} %collective-permute-done.1.refs_1_, bf16[2,576,1024]{2,1,0:T(8,128)(2,1)S(1)} %get-tuple-element.40.refs_1_.refs_2_, ...), custom_call_target="tpu_custom_call" | custom-call | flops 570425344 | bytes 4194304 | tf_op jit(solution)/shard_map/pallas_call | solution.py:47
  41.8 1.4 %collective-permute-start.2 = (bf16[136,512]{1,0:T(8,128)(2,1)S(1)}, bf16[136,512]{1,0:T(8,128)(2,1)S(1)}, u32[]{:S(2)}, u32[]{:S(2)}) collective-permute-start(bf16[136,512]{1,0:T(8,128)(2,1)S(1)} %get-tuple-element.43), channel_id=1, source_target_pairs={{0,4},{4,0},{8,12},{12,8},{1,5},{5,1},{9,13},{13,9},{2,6},{6,2},{1... | collective-permute-start | bytes 417800 | tf_op jit(solution)/shard_map/ppermute | solution.py:31
  43.3 2.1 %collective-permute-start.3 = (bf16[136,512]{1,0:T(8,128)(2,1)S(1)}, bf16[136,512]{1,0:T(8,128)(2,1)S(1)}, u32[]{:S(2)}, u32[]{:S(2)}) collective-permute-start(bf16[136,512]{1,0:T(8,128)(2,1)S(1)} %get-tuple-element.44), channel_id=1, source_target_pairs={{0,8},{4,12},{8,0},{12,4},{1,9},{5,13},{9,1},{13,5},{2,10},{6,14},... | collective-permute-start | bytes 417800 | tf_op jit(solution)/shard_map/ppermute | solution.py:31
  45.3 0.0 collective-permute-done.4.refs_0_
  45.3 1.6 %shard_map.112 = (bf16[136,512]{1,0:T(8,128)(2,1)S(1)}, bf16[512,1792]{1,0:T(8,128)(2,1)S(1)}) custom-call(bf16[4,32,576]{2,1,0:T(8,128)(2,1)S(1)} %collective-permute-done.4.refs_0_, bf16[2,576,1024]{2,1,0:T(8,128)(2,1)S(1)} %get-tuple-element.40.refs_1_.refs_2_, s32[4,128]{1,0:T(4,128)S(1)} %get-tuple-element.41.refs_2_.refs_3_, bf16[4096,1792]{1,0:T(8,128)(2,1)} %refs_0_.8), custom_call_target="tpu_custom_call" | custom-call | flops 285212672 | bytes 4194304 | tf_op jit(solution)/shard_map/pallas_call | solution.py:47
  46.9 2.0 %collective-permute-start.5 = (bf16[136,512]{1,0:T(8,128)(2,1)S(1)}, bf16[136,512]{1,0:T(8,128)(2,1)S(1)}, u32[]{:S(2)}, u32[]{:S(2)}) collective-permute-start(bf16[136,512]{1,0:T(8,128)(2,1)S(1)} %get-tuple-element.45), channel_id=1, source_target_pairs={{0,12},{4,8},{8,4},{12,0},{1,13},{5,9},{9,5},{13,1},{2,14},{6,10},... | collective-permute-start | bytes 417800 | tf_op jit(solution)/shard_map/ppermute | solution.py:31
  48.9 1.6 %shard_map.110 = (bf16[136,512]{1,0:T(8,128)(2,1)S(1)}, bf16[512,1792]{1,0:T(8,128)(2,1)S(1)}) custom-call(bf16[4,32,576]{2,1,0:T(8,128)(2,1)S(1)} %get-tuple-element.39.refs_0_, bf16[2,576,1024]{2,1,0:T(8,128)(2,1)S(1)} %get-tuple-element.40.refs_1_.refs_2_, s32[4,128]{1,0:T(4,128)S(1)} %get-tuple-element.41.refs_2_.refs_3_, bf16[4096,1792]{1,0:T(8,128)(2,1)} %refs_0_.8), custom_call_target="tpu_custom_call" | custom-call | flops 285212672 | bytes 4194304 | tf_op jit(solution)/shard_map/pallas_call | solution.py:47
  50.5 0.0 collective-permute-done.2.refs_1_
  50.5 0.0 collective-permute-done.3.refs_2_
  50.5 5.6 %collective-permute-done.5.refs_3_ = bf16[136,512]{1,0:T(8,128)(2,1)S(1)} collective-permute-done((bf16[136,512]{1,0:T(8,128)(2,1)S(1)}, bf16[136,512]{1,0:T(8,128)(2,1)S(1)}, u32[]{:S(2)}, u32[]{:S(2)}) %collective-permute-start.5) | collective-permute-done | bytes 139296 | tf_op jit(solution)/shard_map/ppermute | solution.py:31
  56.1 0.0 collective-permute-done.6.refs_5_
  56.1 1.1 %shard_map.114 = (f32[4,128,128]{2,1,0:T(8,128)S(1)}, f32[4,4096]{1,0:T(4,128)S(1)}) custom-call(bf16[136,512]{1,0:T(8,128)(2,1)S(1)} %get-tuple-element.42.refs_0_, bf16[136,512]{1,0:T(8,128)(2,1)S(1)} %collective-permute-done.2.refs_1_, bf16[136,512]{1,0:T(8,128)(2,1)S(1)} %collective-permute-done.3.refs_2_, ...), custom_call_target="tpu_custom_call" | custom-call | flops 8388608 | bytes 4194304 | tf_op jit(solution)/shard_map/pallas_call | solution.py:47
  57.2 0.0 collective-permute-done.8.refs_1_
  57.2 0.7 shard_map.115.refs_0_
  57.9 1.5 %collective-permute-start.10 = (bf16[4,4096]{1,0:T(4,128)(2,1)S(1)}, bf16[4,4096]{1,0:T(4,128)(2,1)S(1)}, u32[]{:S(2)}, u32[]{:S(2)}) collective-permute-start(bf16[4,4096]{1,0:T(4,128)(2,1)S(1)} %shard_map.115.refs_0_), channel_id=1, source_target_pairs={{0,2},{1,3},{2,0},{3,1},{4,6},{5,7},{6,4},{7,5},{8,10},{9,11},{10,... | collective-permute-start | bytes 98312 | tf_op jit(solution)/shard_map/ppermute | solution.py:31
  59.4 0.0 collective-permute-start.11
  59.4 0.6 collective-permute-start.9
  60.1 2.0 %shard_map.116.refs_5_ = bf16[1024,1792]{1,0:T(8,128)(2,1)S(1)} custom-call(bf16[4096,1792]{1,0:T(8,128)(2,1)} %refs_0_.8), custom_call_target="tpu_custom_call" | custom-call | bytes 7340032 | tf_op jit(solution)/shard_map/pallas_call | solution.py:47
  62.1 1.8 %shard_map.117.refs_8_ = bf16[768,1792]{1,0:T(8,128)(2,1)S(1)} custom-call(bf16[4096,1792]{1,0:T(8,128)(2,1)} %refs_0_.8), custom_call_target="tpu_custom_call" | custom-call | bytes 5505024 | tf_op jit(solution)/shard_map/pallas_call | solution.py:47
  63.9 1.8 %shard_map.118.refs_9_ = bf16[768,1792]{1,0:T(8,128)(2,1)S(1)} custom-call(bf16[4096,1792]{1,0:T(8,128)(2,1)} %refs_0_.8), custom_call_target="tpu_custom_call" | custom-call | bytes 5505024 | tf_op jit(solution)/shard_map/pallas_call | solution.py:47
  65.7 0.0 collective-permute-done.10.refs_2_
  65.7 0.0 collective-permute-done.11.refs_3_
  65.7 0.0 collective-permute-done.9.refs_1_
  65.7 2.0 %shard_map.119.refs_0_ = bf16[16,1792]{1,0:T(8,128)(2,1)S(1)} custom-call(bf16[4,4096]{1,0:T(4,128)(2,1)S(1)} %shard_map.115.refs_0_, bf16[4,4096]{1,0:T(4,128)(2,1)S(1)} %collective-permute-done.9.refs_1_, bf16[4,4096]{1,0:T(4,128)(2,1)S(1)} %collective-permute-done.10.refs_2_, bf16[4,4096]{1,0:T(4,128)(2,1)S(1)} %collective-permute-done.11.refs_3_, ...), custom_call_target="tpu_custom_call" | custom-call | flops 234881024 | bytes 4194304 | tf_op jit(solution)/shard_map/pallas_call | solution.py:47
  67.7 2.9 %collective-permute-start.12 = (bf16[16,1792]{1,0:T(8,128)(2,1)S(1)}, bf16[16,1792]{1,0:T(8,128)(2,1)S(1)}, u32[]{:S(2)}, u32[]{:S(2)}) collective-permute-start(bf16[16,1792]{1,0:T(8,128)(2,1)S(1)} %shard_map.119.refs_0_), channel_id=1, source_target_pairs={{0,4},{4,0},{8,12},{12,8},{1,5},{5,1},{9,13},{13,9},{2,6},{6,2},{1... | collective-permute-start | bytes 172040 | tf_op jit(solution)/shard_map/ppermute | solution.py:31
  70.7 1.6 %collective-permute-start.13 = (bf16[16,1792]{1,0:T(8,128)(2,1)S(1)}, bf16[16,1792]{1,0:T(8,128)(2,1)S(1)}, u32[]{:S(2)}, u32[]{:S(2)}) collective-permute-start(bf16[16,1792]{1,0:T(8,128)(2,1)S(1)} %shard_map.119.refs_0_), channel_id=1, source_target_pairs={{0,8},{4,12},{8,0},{12,4},{1,9},{5,13},{9,1},{13,5},{2,10},{6,14},... | collective-permute-start | bytes 172040 | tf_op jit(solution)/shard_map/ppermute | solution.py:31
  72.3 1.4 %collective-permute-start.14 = (bf16[16,1792]{1,0:T(8,128)(2,1)S(1)}, bf16[16,1792]{1,0:T(8,128)(2,1)S(1)}, u32[]{:S(2)}, u32[]{:S(2)}) collective-permute-start(bf16[16,1792]{1,0:T(8,128)(2,1)S(1)} %shard_map.119.refs_0_), channel_id=1, source_target_pairs={{0,12},{4,8},{8,4},{12,0},{1,13},{5,9},{9,5},{13,1},{2,14},{6,10},... | collective-permute-start | bytes 172040 | tf_op jit(solution)/shard_map/ppermute | solution.py:31
  73.8 3.4 %shard_map.120.refs_7_.up_ref = bf16[1792,2304]{1,0:T(8,128)(2,1)S(1)} custom-call(bf16[1792,2304]{1,0:T(8,128)(2,1)} %refs_0_.9), custom_call_target="tpu_custom_call" | custom-call | bytes 16515072 | tf_op jit(solution)/shard_map/pallas_call | solution.py:47
  77.1 0.0 collective-permute-done.12.refs_1_
  77.1 1.2 %collective-permute-done.13.refs_2_ = bf16[16,1792]{1,0:T(8,128)(2,1)S(1)} collective-permute-done((bf16[16,1792]{1,0:T(8,128)(2,1)S(1)}, bf16[16,1792]{1,0:T(8,128)(2,1)S(1)}, u32[]{:S(2)}, u32[]{:S(2)}) %collective-permute-start.13) | collective-permute-done | bytes 57376 | tf_op jit(solution)/shard_map/ppermute | solution.py:31
  78.4 0.0 collective-permute-done.14.refs_3_
  78.4 1.3 %shard_map.121 = (bf16[16,2432]{1,0:T(8,128)(2,1)S(1)}, bf16[16,1792]{1,0:T(8,128)(2,1)S(1)}, f32[16,128]{1,0:T(8,128)S(1)}, f32[4,1792]{1,0:T(4,128)S(1)}) custom-call(bf16[16,1792]{1,0:T(8,128)(2,1)S(1)} %shard_map.119.refs_0_, bf16[16,1792]{1,0:T(8,128)(2,1)S(1)} %collective-permute-done.12.refs_1_, bf16[16,1792]{1,0:T(8,128)(2,1)S(1)} %collective-permute-done.13.refs_2_, ...), custom_call_target="tpu_custom_call" | custom-call | flops 132120576 | bytes 4194304 | tf_op jit(solution)/shard_map/pallas_call | solution.py:47
  79.7 0.0 collective-permute-start.15
  79.7 1.2 %shard_map.122.keep_ref = f32[16,2304]{1,0:T(8,128)S(1)} custom-call(bf16[16,1792]{1,0:T(8,128)(2,1)S(1)} %get-tuple-element.62.scaled_ref, bf16[1792,2304]{1,0:T(8,128)(2,1)S(1)} %get-tuple-element.59.refs_6_.gate_ref, bf16[1792,2304]{1,0:T(8,128)(2,1)S(1)} %shard_map.120.refs_7_.up_ref), custom_call_target="tpu_custom_call" | custom-call | flops 132120576 | bytes 4194304 | tf_op jit(solution)/shard_map/pallas_call | solution.py:47
  80.9 0.1 collective-permute-done.15.got_ref
  81.0 0.2 shard_map.123
  81.1 1.5 %collective-permute-start.16 = (bf16[16,2432]{1,0:T(8,128)(2,1)S(1)}, bf16[16,2432]{1,0:T(8,128)(2,1)S(1)}, u32[]{:S(2)}, u32[]{:S(2)}) collective-permute-start(bf16[16,2432]{1,0:T(8,128)(2,1)S(1)} %get-tuple-element.67), channel_id=1, source_target_pairs={{0,2},{2,0},{1,3},{3,1},{4,6},{6,4},{5,7},{7,5},{8,10},{10,8},{9,1... | collective-permute-start | bytes 233480 | tf_op jit(solution)/shard_map/ppermute | solution.py:31
  82.6 3.2 %collective-permute-done.16.refs_1_ = bf16[16,2432]{1,0:T(8,128)(2,1)S(1)} collective-permute-done((bf16[16,2432]{1,0:T(8,128)(2,1)S(1)}, bf16[16,2432]{1,0:T(8,128)(2,1)S(1)}, u32[]{:S(2)}, u32[]{:S(2)}) %collective-permute-start.16) | collective-permute-done | bytes 77856 | tf_op jit(solution)/shard_map/ppermute | solution.py:31
  85.8 0.2 shard_map.124.own_ref
  86.0 0.1 collective-permute-start.17
  86.1 3.4 %shard_map.125.weight_ref = bf16[2304,1792]{1,0:T(8,128)(2,1)S(1)} custom-call(bf16[2304,1792]{1,0:T(8,128)(2,1)} %refs_0_.10), custom_call_target="tpu_custom_call" | custom-call | bytes 16515072 | tf_op jit(solution)/shard_map/pallas_call | solution.py:47
  89.5 0.7 shard_map.126.partial_ref
  90.2 0.0 collective-permute-done.17.other_ref
  90.2 0.7 shard_map.127
  90.9 1.5 %collective-permute-start.18 = (bf16[4,1792]{1,0:T(4,128)(2,1)S(1)}, bf16[4,1792]{1,0:T(4,128)(2,1)S(1)}, u32[]{:S(2)}, u32[]{:S(2)}) collective-permute-start(bf16[4,1792]{1,0:T(4,128)(2,1)S(1)} %get-tuple-element.70), channel_id=1, source_target_pairs={{0,4},{4,0},{8,12},{12,8},{1,5},{5,1},{9,13},{13,9},{2,6},{6,2},{1... | collective-permute-start | bytes 43016 | tf_op jit(solution)/shard_map/ppermute | solution.py:31
  92.3 1.5 %collective-permute-start.19 = (bf16[4,1792]{1,0:T(4,128)(2,1)S(1)}, bf16[4,1792]{1,0:T(4,128)(2,1)S(1)}, u32[]{:S(2)}, u32[]{:S(2)}) collective-permute-start(bf16[4,1792]{1,0:T(4,128)(2,1)S(1)} %get-tuple-element.71), channel_id=1, source_target_pairs={{0,8},{4,12},{8,0},{12,4},{1,9},{5,13},{9,1},{13,5},{2,10},{6,14},... | collective-permute-start | bytes 43016 | tf_op jit(solution)/shard_map/ppermute | solution.py:31
  93.9 1.4 %collective-permute-start.20 = (bf16[4,1792]{1,0:T(4,128)(2,1)S(1)}, bf16[4,1792]{1,0:T(4,128)(2,1)S(1)}, u32[]{:S(2)}, u32[]{:S(2)}) collective-permute-start(bf16[4,1792]{1,0:T(4,128)(2,1)S(1)} %get-tuple-element.72), channel_id=1, source_target_pairs={{0,12},{4,8},{8,4},{12,0},{1,13},{5,9},{9,5},{13,1},{2,14},{6,10},... | collective-permute-start | bytes 43016 | tf_op jit(solution)/shard_map/ppermute | solution.py:31
  95.3 0.0 collective-permute-done.18.refs_2_
  95.3 1.8 %collective-permute-done.19.refs_3_ = bf16[4,1792]{1,0:T(4,128)(2,1)S(1)} collective-permute-done((bf16[4,1792]{1,0:T(4,128)(2,1)S(1)}, bf16[4,1792]{1,0:T(4,128)(2,1)S(1)}, u32[]{:S(2)}, u32[]{:S(2)}) %collective-permute-start.19) | collective-permute-done | bytes 14368 | tf_op jit(solution)/shard_map/ppermute | solution.py:31
  97.1 2.3 %collective-permute-done.20.refs_4_ = bf16[4,1792]{1,0:T(4,128)(2,1)S(1)} collective-permute-done((bf16[4,1792]{1,0:T(4,128)(2,1)S(1)}, bf16[4,1792]{1,0:T(4,128)(2,1)S(1)}, u32[]{:S(2)}, u32[]{:S(2)}) %collective-permute-start.20) | collective-permute-done | bytes 14368 | tf_op jit(solution)/shard_map/ppermute | solution.py:31
  99.4 0.6 shard_map.128
Async XLA Ops:
  0.0 26.3 %copy-start = (bf16[4,32,576]{2,1,0:T(8,128)(2,1)S(1)}, bf16[4,32,576]{2,1,0:T(8,128)(2,1)}, u32[]{:S(2)}) copy-start(bf16[4,32,576]{2,1,0:T(8,128)(2,1)} %refs_0_.4) | copy-start | bytes 442372
  0.0 26.3 %collective-permute-start.7 = (bf16[32,128,128]{2,1,0:T(8,128)(2,1)}, bf16[32,128,128]{2,1,0:T(8,128)(2,1)S(1)}, u32[]{:S(2)}, u32[]{:S(2)}) collective-permute-start(bf16[32,128,128]{2,1,0:T(8,128)(2,1)} %refs_1_.1), channel_id=1, source_target_pairs={{0,2},{2,0},{1,3},{3,1},{4,6},{6,4},{5,7},{7,5},{8,10},{10,8},{9,1... | collective-permute-start | bytes 3145736 | tf_op jit(solution)/shard_map/ppermute | solution.py:31
  3.0 53.1 %collective-permute-start.6 = (bf16[32,128,128]{2,1,0:T(8,128)(2,1)}, bf16[32,128,128]{2,1,0:T(8,128)(2,1)S(1)}, u32[]{:S(2)}, u32[]{:S(2)}) collective-permute-start(bf16[32,128,128]{2,1,0:T(8,128)(2,1)} %refs_1_.1), channel_id=1, source_target_pairs={{0,1},{1,0},{2,3},{3,2},{4,5},{5,4},{6,7},{7,6},{8,9},{9,8},{10,11... | collective-permute-start | bytes 3145736 | tf_op jit(solution)/shard_map/ppermute | solution.py:31
  26.3 30.9 %collective-permute-start.8 = (bf16[32,128,128]{2,1,0:T(8,128)(2,1)S(1)}, bf16[32,128,128]{2,1,0:T(8,128)(2,1)S(1)}, u32[]{:S(2)}, u32[]{:S(2)}) collective-permute-start(bf16[32,128,128]{2,1,0:T(8,128)(2,1)S(1)} %collective-permute-done.7.refs_0_), channel_id=1, source_target_pairs={{0,1},{1,0},{2,3},{3,2},{4,5},{5,4},{6,7},{7,6},{8,9},{9,8},{10,11... | collective-permute-start | bytes 3145736 | tf_op jit(solution)/shard_map/ppermute | solution.py:31
  26.3 11.3 %collective-permute-start = (bf16[4,32,576]{2,1,0:T(8,128)(2,1)S(1)}, bf16[4,32,576]{2,1,0:T(8,128)(2,1)S(1)}, u32[]{:S(2)}, u32[]{:S(2)}) collective-permute-start(bf16[4,32,576]{2,1,0:T(8,128)(2,1)S(1)} %copy-done), channel_id=1, source_target_pairs={{0,8},{4,12},{8,0},{12,4},{1,9},{5,13},{9,1},{13,5},{2,10},{6,14},... | collective-permute-start | bytes 442376 | tf_op jit(solution)/shard_map/ppermute | solution.py:31
  29.2 10.8 %collective-permute-start.1 = (bf16[4,32,576]{2,1,0:T(8,128)(2,1)S(1)}, bf16[4,32,576]{2,1,0:T(8,128)(2,1)S(1)}, u32[]{:S(2)}, u32[]{:S(2)}) collective-permute-start(bf16[4,32,576]{2,1,0:T(8,128)(2,1)S(1)} %copy-done), channel_id=1, source_target_pairs={{0,4},{4,0},{8,12},{12,8},{1,5},{5,1},{9,13},{13,9},{2,6},{6,2},{1... | collective-permute-start | bytes 442376 | tf_op jit(solution)/shard_map/ppermute | solution.py:31
  37.7 7.7 %collective-permute-start.4 = (bf16[4,32,576]{2,1,0:T(8,128)(2,1)S(1)}, bf16[4,32,576]{2,1,0:T(8,128)(2,1)S(1)}, u32[]{:S(2)}, u32[]{:S(2)}) collective-permute-start(bf16[4,32,576]{2,1,0:T(8,128)(2,1)S(1)} %collective-permute-done.refs_0_), channel_id=1, source_target_pairs={{0,4},{4,0},{8,12},{12,8},{1,5},{5,1},{9,13},{13,9},{2,6},{6,2},{1... | collective-permute-start | bytes 442376 | tf_op jit(solution)/shard_map/ppermute | solution.py:31
  41.8 8.7 %collective-permute-start.2 = (bf16[136,512]{1,0:T(8,128)(2,1)S(1)}, bf16[136,512]{1,0:T(8,128)(2,1)S(1)}, u32[]{:S(2)}, u32[]{:S(2)}) collective-permute-start(bf16[136,512]{1,0:T(8,128)(2,1)S(1)} %get-tuple-element.43), channel_id=1, source_target_pairs={{0,4},{4,0},{8,12},{12,8},{1,5},{5,1},{9,13},{13,9},{2,6},{6,2},{1... | collective-permute-start | bytes 417800 | tf_op jit(solution)/shard_map/ppermute | solution.py:31
  43.3 7.2 %collective-permute-start.3 = (bf16[136,512]{1,0:T(8,128)(2,1)S(1)}, bf16[136,512]{1,0:T(8,128)(2,1)S(1)}, u32[]{:S(2)}, u32[]{:S(2)}) collective-permute-start(bf16[136,512]{1,0:T(8,128)(2,1)S(1)} %get-tuple-element.44), channel_id=1, source_target_pairs={{0,8},{4,12},{8,0},{12,4},{1,9},{5,13},{9,1},{13,5},{2,10},{6,14},... | collective-permute-start | bytes 417800 | tf_op jit(solution)/shard_map/ppermute | solution.py:31
  46.9 9.2 %collective-permute-start.5 = (bf16[136,512]{1,0:T(8,128)(2,1)S(1)}, bf16[136,512]{1,0:T(8,128)(2,1)S(1)}, u32[]{:S(2)}, u32[]{:S(2)}) collective-permute-start(bf16[136,512]{1,0:T(8,128)(2,1)S(1)} %get-tuple-element.45), channel_id=1, source_target_pairs={{0,12},{4,8},{8,4},{12,0},{1,13},{5,9},{9,5},{13,1},{2,14},{6,10},... | collective-permute-start | bytes 417800 | tf_op jit(solution)/shard_map/ppermute | solution.py:31
  57.9 7.8 %collective-permute-start.10 = (bf16[4,4096]{1,0:T(4,128)(2,1)S(1)}, bf16[4,4096]{1,0:T(4,128)(2,1)S(1)}, u32[]{:S(2)}, u32[]{:S(2)}) collective-permute-start(bf16[4,4096]{1,0:T(4,128)(2,1)S(1)} %shard_map.115.refs_0_), channel_id=1, source_target_pairs={{0,2},{1,3},{2,0},{3,1},{4,6},{5,7},{6,4},{7,5},{8,10},{9,11},{10,... | collective-permute-start | bytes 98312 | tf_op jit(solution)/shard_map/ppermute | solution.py:31
  59.4 6.3 %collective-permute-start.11 = (bf16[4,4096]{1,0:T(4,128)(2,1)S(1)}, bf16[4,4096]{1,0:T(4,128)(2,1)S(1)}, u32[]{:S(2)}, u32[]{:S(2)}) collective-permute-start(bf16[4,4096]{1,0:T(4,128)(2,1)S(1)} %shard_map.115.refs_0_), channel_id=1, source_target_pairs={{0,3},{1,2},{2,1},{3,0},{4,7},{5,6},{6,5},{7,4},{8,11},{9,10},{10,... | collective-permute-start | bytes 98312 | tf_op jit(solution)/shard_map/ppermute | solution.py:31
  59.4 6.3 %collective-permute-start.9 = (bf16[4,4096]{1,0:T(4,128)(2,1)S(1)}, bf16[4,4096]{1,0:T(4,128)(2,1)S(1)}, u32[]{:S(2)}, u32[]{:S(2)}) collective-permute-start(bf16[4,4096]{1,0:T(4,128)(2,1)S(1)} %shard_map.115.refs_0_), channel_id=1, source_target_pairs={{0,1},{1,0},{2,3},{3,2},{4,5},{5,4},{6,7},{7,6},{8,9},{9,8},{10,11... | collective-permute-start | bytes 98312 | tf_op jit(solution)/shard_map/ppermute | solution.py:31
  67.7 9.4 %collective-permute-start.12 = (bf16[16,1792]{1,0:T(8,128)(2,1)S(1)}, bf16[16,1792]{1,0:T(8,128)(2,1)S(1)}, u32[]{:S(2)}, u32[]{:S(2)}) collective-permute-start(bf16[16,1792]{1,0:T(8,128)(2,1)S(1)} %shard_map.119.refs_0_), channel_id=1, source_target_pairs={{0,4},{4,0},{8,12},{12,8},{1,5},{5,1},{9,13},{13,9},{2,6},{6,2},{1... | collective-permute-start | bytes 172040 | tf_op jit(solution)/shard_map/ppermute | solution.py:31
  70.7 7.7 %collective-permute-start.13 = (bf16[16,1792]{1,0:T(8,128)(2,1)S(1)}, bf16[16,1792]{1,0:T(8,128)(2,1)S(1)}, u32[]{:S(2)}, u32[]{:S(2)}) collective-permute-start(bf16[16,1792]{1,0:T(8,128)(2,1)S(1)} %shard_map.119.refs_0_), channel_id=1, source_target_pairs={{0,8},{4,12},{8,0},{12,4},{1,9},{5,13},{9,1},{13,5},{2,10},{6,14},... | collective-permute-start | bytes 172040 | tf_op jit(solution)/shard_map/ppermute | solution.py:31
  72.3 6.1 %collective-permute-start.14 = (bf16[16,1792]{1,0:T(8,128)(2,1)S(1)}, bf16[16,1792]{1,0:T(8,128)(2,1)S(1)}, u32[]{:S(2)}, u32[]{:S(2)}) collective-permute-start(bf16[16,1792]{1,0:T(8,128)(2,1)S(1)} %shard_map.119.refs_0_), channel_id=1, source_target_pairs={{0,12},{4,8},{8,4},{12,0},{1,13},{5,9},{9,5},{13,1},{2,14},{6,10},... | collective-permute-start | bytes 172040 | tf_op jit(solution)/shard_map/ppermute | solution.py:31
  79.7 1.3 %collective-permute-start.15 = (bf16[16,2432]{1,0:T(8,128)(2,1)S(1)}, bf16[16,2432]{1,0:T(8,128)(2,1)S(1)}, u32[]{:S(2)}, u32[]{:S(2)}) collective-permute-start(bf16[16,2432]{1,0:T(8,128)(2,1)S(1)} %get-tuple-element.64), channel_id=1, source_target_pairs={{0,1},{1,0},{2,3},{3,2},{4,5},{5,4},{6,7},{7,6},{8,9},{9,8},{10,11... | collective-permute-start | bytes 233480 | tf_op jit(solution)/shard_map/ppermute | solution.py:31
  81.1 4.7 %collective-permute-start.16 = (bf16[16,2432]{1,0:T(8,128)(2,1)S(1)}, bf16[16,2432]{1,0:T(8,128)(2,1)S(1)}, u32[]{:S(2)}, u32[]{:S(2)}) collective-permute-start(bf16[16,2432]{1,0:T(8,128)(2,1)S(1)} %get-tuple-element.67), channel_id=1, source_target_pairs={{0,2},{2,0},{1,3},{3,1},{4,6},{6,4},{5,7},{7,5},{8,10},{10,8},{9,1... | collective-permute-start | bytes 233480 | tf_op jit(solution)/shard_map/ppermute | solution.py:31
  86.0 4.1 %collective-permute-start.17 = (bf16[16,1152]{1,0:T(8,128)(2,1)S(1)}, bf16[16,1152]{1,0:T(8,128)(2,1)S(1)}, u32[]{:S(2)}, u32[]{:S(2)}) collective-permute-start(bf16[16,1152]{1,0:T(8,128)(2,1)S(1)} %shard_map.124.own_ref), channel_id=1, source_target_pairs={{0,1},{1,0},{2,3},{3,2},{4,5},{5,4},{6,7},{7,6},{8,9},{9,8},{10,11... | collective-permute-start | bytes 110600 | tf_op jit(solution)/shard_map/ppermute | solution.py:31
  90.9 4.5 %collective-permute-start.18 = (bf16[4,1792]{1,0:T(4,128)(2,1)S(1)}, bf16[4,1792]{1,0:T(4,128)(2,1)S(1)}, u32[]{:S(2)}, u32[]{:S(2)}) collective-permute-start(bf16[4,1792]{1,0:T(4,128)(2,1)S(1)} %get-tuple-element.70), channel_id=1, source_target_pairs={{0,4},{4,0},{8,12},{12,8},{1,5},{5,1},{9,13},{13,9},{2,6},{6,2},{1... | collective-permute-start | bytes 43016 | tf_op jit(solution)/shard_map/ppermute | solution.py:31
  92.3 4.8 %collective-permute-start.19 = (bf16[4,1792]{1,0:T(4,128)(2,1)S(1)}, bf16[4,1792]{1,0:T(4,128)(2,1)S(1)}, u32[]{:S(2)}, u32[]{:S(2)}) collective-permute-start(bf16[4,1792]{1,0:T(4,128)(2,1)S(1)} %get-tuple-element.71), channel_id=1, source_target_pairs={{0,8},{4,12},{8,0},{12,4},{1,9},{5,13},{9,1},{13,5},{2,10},{6,14},... | collective-permute-start | bytes 43016 | tf_op jit(solution)/shard_map/ppermute | solution.py:31
  93.9 5.5 %collective-permute-start.20 = (bf16[4,1792]{1,0:T(4,128)(2,1)S(1)}, bf16[4,1792]{1,0:T(4,128)(2,1)S(1)}, u32[]{:S(2)}, u32[]{:S(2)}) collective-permute-start(bf16[4,1792]{1,0:T(4,128)(2,1)S(1)} %get-tuple-element.72), channel_id=1, source_target_pairs={{0,12},{4,8},{8,4},{12,0},{1,13},{5,9},{9,5},{13,1},{2,14},{6,10},... | collective-permute-start | bytes 43016 | tf_op jit(solution)/shard_map/ppermute | solution.py:31

commit v7 on v6

--- a/solution.py
+++ b/solution.py
@@ -485,8 +485,8 @@
     along = listed(exchange([value_up_weight] * roles, "role"))
     groups = exchange([queries] * blocks, "ctx", [*evens, 1])
     unit = out_proj.shape[0] // 16
-    cuts = [unit * k for k in (0, 2, 6, 8, 10, 13, 16)]
-    own_span, early_span, even_span, odd_span, late_span, last_span = zip(cuts, cuts[1:])
+    cuts = [unit * k for k in (0, 2, 6, 8, 10, 16)]
+    own_span, early_span, even_span, odd_span, last_span = zip(cuts, cuts[1:])
     groups[0], cache_fast, seen = fetch([queries, jnp.swapaxes(cache, 1, 2)], lengths, positions)
 
     def attend_some(source, span):
@@ -500,32 +500,29 @@
         relayed[mask + 1] = xor_permute(groups[mask], "ctx", 1)
     even, even_part = attend_some({mask: groups[mask] for mask in [*evens, 1]}, even_span)
     answers |= exchange({0: answers[0], **even}, "ctx", evens)
+    answers |= exchange({0: answers[0], **even}, "ctx", [1])
     far, odd_part = attend_some(relayed, odd_span)
     answers |= exchange({0: answers[0], **far}, "ctx", odds)
-    answers |= exchange({0: answers[0], **even}, "ctx", [1])
 
     gate_fast, up_own, residual, gain = fetch([gate_weight, value_up_weight, residual, norm_gain])
     *far_rows, gain = lax.optimization_barrier((*along[1:], gain))
     near_rows = [up_own, xor_permute(along[0], "seq", 1)]
     far_rows = [part for piece in far_rows for part in (piece, xor_permute(piece, "seq", 1))]
-    (late_part,) = fetch([(out_proj, late_span)])
-
     attended, sums = join_blocks(listed(answers), near_rows, rows, heads, members)
     values = add_values(attended, sums, far_rows, range(2, members), heads)
     last_out, values = lax.optimization_barrier((out_proj, values))
     shared = listed(exchange([values] * members, ("role", "seq")))
     (last_part,) = fetch([(last_out, last_span)])
-    product = project_out(shared, [own_part, early_part, even_part, odd_part, late_part, last_part])
+    product = project_out(shared, [own_part, early_part, even_part, odd_part, last_part])
     up_weight, product = lax.optimization_barrier((up_weight, product))
     terms = listed(exchange([product] * blocks, "ctx"))
-    (up_fast,) = fetch([up_weight])
+    up_fast = up_weight
 
     send, scaled, squares, base = gate_and_up_away(terms, residual, gain, gate_fast, up_fast)
     got = xor_permute(send, "seq", 1)
     keep = gate_and_up_here(scaled, gate_fast, up_fast)
     keep, send = add_core(keep, squares, got)
-    down_weight, send = lax.optimization_barrier((down_weight, send))
-    (down_fast,) = fetch([down_weight])
+    down_fast = down_weight
     pieces = listed(exchange([send] * roles, "role"))[1:]
     features = norm_gain.shape[0] * members
     hidden = activate(keep, pieces, features)

time: 100 us -> 96 us (0.960)
  Pallas kernels: 31.3 us -> 23.6 us
  waiting for transfers between devices: 40.7 us -> 45.6 us
  starting transfers between devices: 27.8 us -> 26.4 us
    pallas_call x20 -> x17, Pallas kernels: 31.3 us -> 23.6 us  [call(): pl.pallas_call(body, out_shape=outs, in_specs=specs, out_specs=jax.tree.m...]
    ppermute x21, waiting for transfers between devices: 40.7 us -> 45.6 us  [xor_permute(): return lax.ppermute(x, axis, [(i, i ^ mask) for i in range(size)])]
    ppermute x21, starting transfers between devices: 27.8 us -> 26.4 us  [xor_permute(): return lax.ppermute(x, axis, [(i, i ^ mask) for i in range(size)])]
  transfers between devices with their start and end apart: 21 -> 21, of which waited for: 8 -> 11; matrix products, arithmetic and copies ran while one was open for 0% -> 0% of each run, Pallas kernels for 26% -> 19%
where the time goes in v7:
time: 96 us; the launch traced here: 95.8 us
  waiting for transfers between devices  45.6 us (48%)
  starting transfers between devices  26.4 us (28%)
  Pallas kernels  23.6 us (25%)
    ppermute x21, waiting for transfers between devices, xor_permute(): return lax.ppermute(x, axis, [(i, i ^ mask) for i in range(size)])  45.6 us
    ppermute x21, starting transfers between devices, xor_permute(): return lax.ppermute(x, axis, [(i, i ^ mask) for i in range(size)])  26.4 us
    pallas_call x17, Pallas kernels, call(): pl.pallas_call(body, out_shape=outs, in_specs=specs, out_specs=jax.tree.m...  23.6 us
  transfers between devices with their start and end apart: 21, of which 11 were waited for; matrix products, arithmetic and copies ran while one was open for 0% of the time, Pallas kernels for 19%

profile of v7, /device:TPU:0, one launch (start us, length us, event | category | flops | bytes accessed | tf_op | source)
XLA Modules:
  0.0 95.8 jit_solution(12444221566626725678)
XLA Ops:
  0.0 3.0 %collective-permute-start.7 = (bf16[32,128,128]{2,1,0:T(8,128)(2,1)}, bf16[32,128,128]{2,1,0:T(8,128)(2,1)S(1)}, u32[]{:S(2)}, u32[]{:S(2)}) collective-permute-start(bf16[32,128,128]{2,1,0:T(8,128)(2,1)} %refs_1_.1), channel_id=1, source_target_pairs={{0,2},{2,0},{1,3},{3,1},{4,6},{6,4},{5,7},{7,5},{8,10},{10,8},{9,1... | collective-permute-start | bytes 3145736 | tf_op jit(solution)/shard_map/ppermute | solution.py:31
  3.0 0.0 collective-permute-start.6
  3.0 3.8 %shard_map.113 = (bf16[1792,2304]{1,0:T(8,128)(2,1)S(1)}, bf16[32,128,128]{2,1,0:T(8,128)(2,1)S(1)}, bf16[16,1792]{1,0:T(8,128)(2,1)S(1)}, f32[1792]{0:T(1024)S(1)}) custom-call(bf16[1792,2304]{1,0:T(8,128)(2,1)} %refs_0_.4, bf16[32,128,128]{2,1,0:T(8,128)(2,1)} %refs_1_.1, bf16[16,1792]{1,0:T(8,128)(2,1)} %refs_2_.3, f32[1792]{0:T(1024)} %refs_3_.7), custom_call_target="tpu_custom_call" | custom-call | bytes 18741248 | tf_op jit(solution)/shard_map/pallas_call | solution.py:47
  6.7 19.6 %collective-permute-done.7.refs_0_ = bf16[32,128,128]{2,1,0:T(8,128)(2,1)S(1)} collective-permute-done((bf16[32,128,128]{2,1,0:T(8,128)(2,1)}, bf16[32,128,128]{2,1,0:T(8,128)(2,1)S(1)}, u32[]{:S(2)}, u32[]{:S(2)}) %collective-permute-start.7) | collective-permute-done | bytes 1048608 | tf_op jit(solution)/shard_map/ppermute | solution.py:31
  26.3 0.0 collective-permute-start.8
  26.3 0.0 copy-done
  26.3 2.8 %collective-permute-start = (bf16[4,32,576]{2,1,0:T(8,128)(2,1)S(1)}, bf16[4,32,576]{2,1,0:T(8,128)(2,1)S(1)}, u32[]{:S(2)}, u32[]{:S(2)}) collective-permute-start(bf16[4,32,576]{2,1,0:T(8,128)(2,1)S(1)} %copy-done), channel_id=1, source_target_pairs={{0,8},{4,12},{8,0},{12,4},{1,9},{5,13},{9,1},{13,5},{2,10},{6,14},... | collective-permute-start | bytes 442376 | tf_op jit(solution)/shard_map/ppermute | solution.py:31
  29.2 1.6 %collective-permute-start.1 = (bf16[4,32,576]{2,1,0:T(8,128)(2,1)S(1)}, bf16[4,32,576]{2,1,0:T(8,128)(2,1)S(1)}, u32[]{:S(2)}, u32[]{:S(2)}) collective-permute-start(bf16[4,32,576]{2,1,0:T(8,128)(2,1)S(1)} %copy-done), channel_id=1, source_target_pairs={{0,4},{4,0},{8,12},{12,8},{1,5},{5,1},{9,13},{13,9},{2,6},{6,2},{1... | collective-permute-start | bytes 442376 | tf_op jit(solution)/shard_map/ppermute | solution.py:31
  30.8 6.9 %collective-permute-done.refs_0_ = bf16[4,32,576]{2,1,0:T(8,128)(2,1)S(1)} collective-permute-done((bf16[4,32,576]{2,1,0:T(8,128)(2,1)S(1)}, bf16[4,32,576]{2,1,0:T(8,128)(2,1)S(1)}, u32[]{:S(2)}, u32[]{:S(2)}) %collective-permute-start) | collective-permute-done | bytes 147488 | tf_op jit(solution)/shard_map/ppermute | solution.py:31
  37.7 0.6 collective-permute-start.4
  38.3 1.7 %shard_map.109 = (bf16[4,32,576]{2,1,0:T(8,128)(2,1)S(1)}, bf16[2,576,1024]{2,1,0:T(8,128)(2,1)S(1)}, s32[4,128]{1,0:T(4,128)S(1)}) custom-call(bf16[4,32,576]{2,1,0:T(8,128)(2,1)} %refs_0_.3, bf16[2,576,1024]{2,1,0:T(8,128)(2,1)} %bitcast.5, s32[2]{0:T(128)} %refs_2_.2, s32[4]{0:T(128)} %refs_3_.4), custom_call_target="tpu_custom_call" | custom-call | bytes 5013504 | tf_op jit(solution)/shard_map/pallas_call | solution.py:47
  40.0 0.0 collective-permute-done.1.refs_1_
  40.0 1.8 %shard_map.111 = (bf16[136,512]{1,0:T(8,128)(2,1)S(1)}, bf16[136,512]{1,0:T(8,128)(2,1)S(1)}, bf16[512,1792]{1,0:T(8,128)(2,1)S(1)}) custom-call(bf16[4,32,576]{2,1,0:T(8,128)(2,1)S(1)} %collective-permute-done.refs_0_, bf16[4,32,576]{2,1,0:T(8,128)(2,1)S(1)} %collective-permute-done.1.refs_1_, bf16[2,576,1024]{2,1,0:T(8,128)(2,1)S(1)} %get-tuple-element.38.refs_1_.refs_2_, ...), custom_call_target="tpu_custom_call" | custom-call | flops 570425344 | bytes 4194304 | tf_op jit(solution)/shard_map/pallas_call | solution.py:47
  41.8 1.4 %collective-permute-start.2 = (bf16[136,512]{1,0:T(8,128)(2,1)S(1)}, bf16[136,512]{1,0:T(8,128)(2,1)S(1)}, u32[]{:S(2)}, u32[]{:S(2)}) collective-permute-start(bf16[136,512]{1,0:T(8,128)(2,1)S(1)} %get-tuple-element.41), channel_id=1, source_target_pairs={{0,4},{4,0},{8,12},{12,8},{1,5},{5,1},{9,13},{13,9},{2,6},{6,2},{1... | collective-permute-start | bytes 417800 | tf_op jit(solution)/shard_map/ppermute | solution.py:31
  43.3 2.1 %collective-permute-start.3 = (bf16[136,512]{1,0:T(8,128)(2,1)S(1)}, bf16[136,512]{1,0:T(8,128)(2,1)S(1)}, u32[]{:S(2)}, u32[]{:S(2)}) collective-permute-start(bf16[136,512]{1,0:T(8,128)(2,1)S(1)} %get-tuple-element.42), channel_id=1, source_target_pairs={{0,8},{4,12},{8,0},{12,4},{1,9},{5,13},{9,1},{13,5},{2,10},{6,14},... | collective-permute-start | bytes 417800 | tf_op jit(solution)/shard_map/ppermute | solution.py:31
  45.3 0.0 collective-permute-done.4.refs_0_
  45.3 1.6 %shard_map.112 = (bf16[136,512]{1,0:T(8,128)(2,1)S(1)}, bf16[512,1792]{1,0:T(8,128)(2,1)S(1)}) custom-call(bf16[4,32,576]{2,1,0:T(8,128)(2,1)S(1)} %collective-permute-done.4.refs_0_, bf16[2,576,1024]{2,1,0:T(8,128)(2,1)S(1)} %get-tuple-element.38.refs_1_.refs_2_, s32[4,128]{1,0:T(4,128)S(1)} %get-tuple-element.39.refs_2_.refs_3_, bf16[4096,1792]{1,0:T(8,128)(2,1)} %refs_0_.6), custom_call_target="tpu_custom_call" | custom-call | flops 285212672 | bytes 4194304 | tf_op jit(solution)/shard_map/pallas_call | solution.py:47
  46.9 2.0 %collective-permute-start.5 = (bf16[136,512]{1,0:T(8,128)(2,1)S(1)}, bf16[136,512]{1,0:T(8,128)(2,1)S(1)}, u32[]{:S(2)}, u32[]{:S(2)}) collective-permute-start(bf16[136,512]{1,0:T(8,128)(2,1)S(1)} %get-tuple-element.43), channel_id=1, source_target_pairs={{0,12},{4,8},{8,4},{12,0},{1,13},{5,9},{9,5},{13,1},{2,14},{6,10},... | collective-permute-start | bytes 417800 | tf_op jit(solution)/shard_map/ppermute | solution.py:31
  48.9 1.6 %shard_map.110 = (bf16[136,512]{1,0:T(8,128)(2,1)S(1)}, bf16[512,1792]{1,0:T(8,128)(2,1)S(1)}) custom-call(bf16[4,32,576]{2,1,0:T(8,128)(2,1)S(1)} %get-tuple-element.37.refs_0_, bf16[2,576,1024]{2,1,0:T(8,128)(2,1)S(1)} %get-tuple-element.38.refs_1_.refs_2_, s32[4,128]{1,0:T(4,128)S(1)} %get-tuple-element.39.refs_2_.refs_3_, bf16[4096,1792]{1,0:T(8,128)(2,1)} %refs_0_.6), custom_call_target="tpu_custom_call" | custom-call | flops 285212672 | bytes 4194304 | tf_op jit(solution)/shard_map/pallas_call | solution.py:47
  50.5 0.0 collective-permute-done.2.refs_1_
  50.5 0.0 collective-permute-done.3.refs_2_
  50.5 5.6 %collective-permute-done.5.refs_3_ = bf16[136,512]{1,0:T(8,128)(2,1)S(1)} collective-permute-done((bf16[136,512]{1,0:T(8,128)(2,1)S(1)}, bf16[136,512]{1,0:T(8,128)(2,1)S(1)}, u32[]{:S(2)}, u32[]{:S(2)}) %collective-permute-start.5) | collective-permute-done | bytes 139296 | tf_op jit(solution)/shard_map/ppermute | solution.py:31
  56.1 0.0 collective-permute-done.6.refs_5_
  56.1 1.1 %shard_map.114 = (f32[4,128,128]{2,1,0:T(8,128)S(1)}, f32[4,4096]{1,0:T(4,128)S(1)}) custom-call(bf16[136,512]{1,0:T(8,128)(2,1)S(1)} %get-tuple-element.40.refs_0_, bf16[136,512]{1,0:T(8,128)(2,1)S(1)} %collective-permute-done.2.refs_1_, bf16[136,512]{1,0:T(8,128)(2,1)S(1)} %collective-permute-done.3.refs_2_, ...), custom_call_target="tpu_custom_call" | custom-call | flops 8388608 | bytes 4194304 | tf_op jit(solution)/shard_map/pallas_call | solution.py:47
  57.2 0.0 collective-permute-done.8.refs_1_
  57.2 0.7 shard_map.115.refs_0_
  57.9 0.0 collective-permute-start.11
  57.9 1.6 %collective-permute-start.10 = (bf16[4,4096]{1,0:T(4,128)(2,1)S(1)}, bf16[4,4096]{1,0:T(4,128)(2,1)S(1)}, u32[]{:S(2)}, u32[]{:S(2)}) collective-permute-start(bf16[4,4096]{1,0:T(4,128)(2,1)S(1)} %shard_map.115.refs_0_), channel_id=1, source_target_pairs={{0,2},{1,3},{2,0},{3,1},{4,6},{5,7},{6,4},{7,5},{8,10},{9,11},{10,... | collective-permute-start | bytes 98312 | tf_op jit(solution)/shard_map/ppermute | solution.py:31
  59.5 0.3 collective-permute-start.9
  59.8 2.0 %shard_map.116.refs_5_ = bf16[1024,1792]{1,0:T(8,128)(2,1)S(1)} custom-call(bf16[4096,1792]{1,0:T(8,128)(2,1)} %refs_0_.6), custom_call_target="tpu_custom_call" | custom-call | bytes 7340032 | tf_op jit(solution)/shard_map/pallas_call | solution.py:47
  61.8 2.6 %shard_map.117.refs_8_ = bf16[1536,1792]{1,0:T(8,128)(2,1)S(1)} custom-call(bf16[4096,1792]{1,0:T(8,128)(2,1)} %refs_0_.6), custom_call_target="tpu_custom_call" | custom-call | bytes 11010048 | tf_op jit(solution)/shard_map/pallas_call | solution.py:47
  64.4 0.0 collective-permute-done.11.refs_3_
  64.4 0.0 collective-permute-done.10.refs_2_
  64.4 0.0 collective-permute-done.9.refs_1_
  64.4 0.0 slice-start
  64.5 0.0 slice-start.1
  64.5 2.0 %shard_map.118.refs_0_ = bf16[16,1792]{1,0:T(8,128)(2,1)S(1)} custom-call(bf16[4,4096]{1,0:T(4,128)(2,1)S(1)} %shard_map.115.refs_0_, bf16[4,4096]{1,0:T(4,128)(2,1)S(1)} %collective-permute-done.9.refs_1_, bf16[4,4096]{1,0:T(4,128)(2,1)S(1)} %collective-permute-done.10.refs_2_, bf16[4,4096]{1,0:T(4,128)(2,1)S(1)} %collective-permute-done.11.refs_3_, ...), custom_call_target="tpu_custom_call" | custom-call | flops 234881024 | bytes 4194304 | tf_op jit(solution)/shard_map/pallas_call | solution.py:47
  66.5 3.1 %collective-permute-start.14 = (bf16[16,1792]{1,0:T(8,128)(2,1)S(1)}, bf16[16,1792]{1,0:T(8,128)(2,1)S(1)}, u32[]{:S(2)}, u32[]{:S(2)}) collective-permute-start(bf16[16,1792]{1,0:T(8,128)(2,1)S(1)} %shard_map.118.refs_0_), channel_id=1, source_target_pairs={{0,12},{4,8},{8,4},{12,0},{1,13},{5,9},{9,5},{13,1},{2,14},{6,10},... | collective-permute-start | bytes 172040 | tf_op jit(solution)/shard_map/ppermute | solution.py:31
  69.6 1.5 %collective-permute-start.13 = (bf16[16,1792]{1,0:T(8,128)(2,1)S(1)}, bf16[16,1792]{1,0:T(8,128)(2,1)S(1)}, u32[]{:S(2)}, u32[]{:S(2)}) collective-permute-start(bf16[16,1792]{1,0:T(8,128)(2,1)S(1)} %shard_map.118.refs_0_), channel_id=1, source_target_pairs={{0,8},{4,12},{8,0},{12,4},{1,9},{5,13},{9,1},{13,5},{2,10},{6,14},... | collective-permute-start | bytes 172040 | tf_op jit(solution)/shard_map/ppermute | solution.py:31
  71.1 0.5 collective-permute-start.12
  71.6 0.9 collective-permute-done.14.refs_3_
  72.5 3.1 %collective-permute-done.13.refs_2_ = bf16[16,1792]{1,0:T(8,128)(2,1)S(1)} collective-permute-done((bf16[16,1792]{1,0:T(8,128)(2,1)S(1)}, bf16[16,1792]{1,0:T(8,128)(2,1)S(1)}, u32[]{:S(2)}, u32[]{:S(2)}) %collective-permute-start.13) | collective-permute-done | bytes 57376 | tf_op jit(solution)/shard_map/ppermute | solution.py:31
  75.6 0.4 collective-permute-done.12.refs_1_
  76.1 1.3 %shard_map.119 = (bf16[16,2432]{1,0:T(8,128)(2,1)S(1)}, bf16[16,1792]{1,0:T(8,128)(2,1)S(1)}, f32[16,128]{1,0:T(8,128)S(1)}, f32[4,1792]{1,0:T(4,128)S(1)}) custom-call(bf16[16,1792]{1,0:T(8,128)(2,1)S(1)} %shard_map.118.refs_0_, bf16[16,1792]{1,0:T(8,128)(2,1)S(1)} %collective-permute-done.12.refs_1_, bf16[16,1792]{1,0:T(8,128)(2,1)S(1)} %collective-permute-done.13.refs_2_, ...), custom_call_target="tpu_custom_call" | custom-call | flops 132120576 | bytes 4194304 | tf_op jit(solution)/shard_map/pallas_call | solution.py:47
  77.4 0.0 collective-permute-start.15
  77.4 0.0 slice-start.2
  77.4 0.0 slice-start.3
  77.4 1.2 %shard_map.120.keep_ref = f32[16,2304]{1,0:T(8,128)S(1)} custom-call(bf16[16,1792]{1,0:T(8,128)(2,1)S(1)} %get-tuple-element.60.scaled_ref, bf16[1792,2304]{1,0:T(8,128)(2,1)S(1)} %get-tuple-element.57.refs_6_.gate_ref, bf16[1792,2304]{1,0:T(8,128)(2,1)S(1)} %bitcast.2), custom_call_target="tpu_custom_call" | custom-call | flops 132120576 | bytes 4194304 | tf_op jit(solution)/shard_map/pallas_call | solution.py:47
  78.6 0.1 collective-permute-done.15.got_ref
  78.7 0.2 shard_map.121
  78.8 1.3 %collective-permute-start.16 = (bf16[16,2432]{1,0:T(8,128)(2,1)S(1)}, bf16[16,2432]{1,0:T(8,128)(2,1)S(1)}, u32[]{:S(2)}, u32[]{:S(2)}) collective-permute-start(bf16[16,2432]{1,0:T(8,128)(2,1)S(1)} %get-tuple-element.64), channel_id=1, source_target_pairs={{0,2},{2,0},{1,3},{3,1},{4,6},{6,4},{5,7},{7,5},{8,10},{10,8},{9,1... | collective-permute-start | bytes 233480 | tf_op jit(solution)/shard_map/ppermute | solution.py:31
  80.1 3.4 %collective-permute-done.16.refs_1_ = bf16[16,2432]{1,0:T(8,128)(2,1)S(1)} collective-permute-done((bf16[16,2432]{1,0:T(8,128)(2,1)S(1)}, bf16[16,2432]{1,0:T(8,128)(2,1)S(1)}, u32[]{:S(2)}, u32[]{:S(2)}) %collective-permute-start.16) | collective-permute-done | bytes 77856 | tf_op jit(solution)/shard_map/ppermute | solution.py:31
  83.5 0.2 shard_map.122.own_ref
  83.7 0.1 collective-permute-start.17
  83.8 0.7 shard_map.123.partial_ref
  84.5 0.5 collective-permute-done.17.other_ref
  85.0 0.7 shard_map.124
  85.7 0.9 collective-permute-start.18
  86.6 3.0 %collective-permute-start.19 = (bf16[4,1792]{1,0:T(4,128)(2,1)S(1)}, bf16[4,1792]{1,0:T(4,128)(2,1)S(1)}, u32[]{:S(2)}, u32[]{:S(2)}) collective-permute-start(bf16[4,1792]{1,0:T(4,128)(2,1)S(1)} %get-tuple-element.67), channel_id=1, source_target_pairs={{0,8},{4,12},{8,0},{12,4},{1,9},{5,13},{9,1},{13,5},{2,10},{6,14},... | collective-permute-start | bytes 43016 | tf_op jit(solution)/shard_map/ppermute | solution.py:31
  89.6 0.5 collective-permute-start.20
  90.2 0.0 collective-permute-done.18.refs_2_
  90.2 1.2 %collective-permute-done.19.refs_3_ = bf16[4,1792]{1,0:T(4,128)(2,1)S(1)} collective-permute-done((bf16[4,1792]{1,0:T(4,128)(2,1)S(1)}, bf16[4,1792]{1,0:T(4,128)(2,1)S(1)}, u32[]{:S(2)}, u32[]{:S(2)}) %collective-permute-start.19) | collective-permute-done | bytes 14368 | tf_op jit(solution)/shard_map/ppermute | solution.py:31
  91.3 3.8 %collective-permute-done.20.refs_4_ = bf16[4,1792]{1,0:T(4,128)(2,1)S(1)} collective-permute-done((bf16[4,1792]{1,0:T(4,128)(2,1)S(1)}, bf16[4,1792]{1,0:T(4,128)(2,1)S(1)}, u32[]{:S(2)}, u32[]{:S(2)}) %collective-permute-start.20) | collective-permute-done | bytes 14368 | tf_op jit(solution)/shard_map/ppermute | solution.py:31
  95.2 0.6 shard_map.125
  (7 shorter events, 0.0 us)
Async XLA Ops:
  0.0 26.3 %copy-start = (bf16[4,32,576]{2,1,0:T(8,128)(2,1)S(1)}, bf16[4,32,576]{2,1,0:T(8,128)(2,1)}, u32[]{:S(2)}) copy-start(bf16[4,32,576]{2,1,0:T(8,128)(2,1)} %refs_0_.3) | copy-start | bytes 442372
  0.0 26.3 %collective-permute-start.7 = (bf16[32,128,128]{2,1,0:T(8,128)(2,1)}, bf16[32,128,128]{2,1,0:T(8,128)(2,1)S(1)}, u32[]{:S(2)}, u32[]{:S(2)}) collective-permute-start(bf16[32,128,128]{2,1,0:T(8,128)(2,1)} %refs_1_.1), channel_id=1, source_target_pairs={{0,2},{2,0},{1,3},{3,1},{4,6},{6,4},{5,7},{7,5},{8,10},{10,8},{9,1... | collective-permute-start | bytes 3145736 | tf_op jit(solution)/shard_map/ppermute | solution.py:31
  3.0 53.1 %collective-permute-start.6 = (bf16[32,128,128]{2,1,0:T(8,128)(2,1)}, bf16[32,128,128]{2,1,0:T(8,128)(2,1)S(1)}, u32[]{:S(2)}, u32[]{:S(2)}) collective-permute-start(bf16[32,128,128]{2,1,0:T(8,128)(2,1)} %refs_1_.1), channel_id=1, source_target_pairs={{0,1},{1,0},{2,3},{3,2},{4,5},{5,4},{6,7},{7,6},{8,9},{9,8},{10,11... | collective-permute-start | bytes 3145736 | tf_op jit(solution)/shard_map/ppermute | solution.py:31
  26.3 30.9 %collective-permute-start.8 = (bf16[32,128,128]{2,1,0:T(8,128)(2,1)S(1)}, bf16[32,128,128]{2,1,0:T(8,128)(2,1)S(1)}, u32[]{:S(2)}, u32[]{:S(2)}) collective-permute-start(bf16[32,128,128]{2,1,0:T(8,128)(2,1)S(1)} %collective-permute-done.7.refs_0_), channel_id=1, source_target_pairs={{0,1},{1,0},{2,3},{3,2},{4,5},{5,4},{6,7},{7,6},{8,9},{9,8},{10,11... | collective-permute-start | bytes 3145736 | tf_op jit(solution)/shard_map/ppermute | solution.py:31
  26.3 11.3 %collective-permute-start = (bf16[4,32,576]{2,1,0:T(8,128)(2,1)S(1)}, bf16[4,32,576]{2,1,0:T(8,128)(2,1)S(1)}, u32[]{:S(2)}, u32[]{:S(2)}) collective-permute-start(bf16[4,32,576]{2,1,0:T(8,128)(2,1)S(1)} %copy-done), channel_id=1, source_target_pairs={{0,8},{4,12},{8,0},{12,4},{1,9},{5,13},{9,1},{13,5},{2,10},{6,14},... | collective-permute-start | bytes 442376 | tf_op jit(solution)/shard_map/ppermute | solution.py:31
  29.2 10.8 %collective-permute-start.1 = (bf16[4,32,576]{2,1,0:T(8,128)(2,1)S(1)}, bf16[4,32,576]{2,1,0:T(8,128)(2,1)S(1)}, u32[]{:S(2)}, u32[]{:S(2)}) collective-permute-start(bf16[4,32,576]{2,1,0:T(8,128)(2,1)S(1)} %copy-done), channel_id=1, source_target_pairs={{0,4},{4,0},{8,12},{12,8},{1,5},{5,1},{9,13},{13,9},{2,6},{6,2},{1... | collective-permute-start | bytes 442376 | tf_op jit(solution)/shard_map/ppermute | solution.py:31
  37.7 7.7 %collective-permute-start.4 = (bf16[4,32,576]{2,1,0:T(8,128)(2,1)S(1)}, bf16[4,32,576]{2,1,0:T(8,128)(2,1)S(1)}, u32[]{:S(2)}, u32[]{:S(2)}) collective-permute-start(bf16[4,32,576]{2,1,0:T(8,128)(2,1)S(1)} %collective-permute-done.refs_0_), channel_id=1, source_target_pairs={{0,4},{4,0},{8,12},{12,8},{1,5},{5,1},{9,13},{13,9},{2,6},{6,2},{1... | collective-permute-start | bytes 442376 | tf_op jit(solution)/shard_map/ppermute | solution.py:31
  41.8 8.7 %collective-permute-start.2 = (bf16[136,512]{1,0:T(8,128)(2,1)S(1)}, bf16[136,512]{1,0:T(8,128)(2,1)S(1)}, u32[]{:S(2)}, u32[]{:S(2)}) collective-permute-start(bf16[136,512]{1,0:T(8,128)(2,1)S(1)} %get-tuple-element.41), channel_id=1, source_target_pairs={{0,4},{4,0},{8,12},{12,8},{1,5},{5,1},{9,13},{13,9},{2,6},{6,2},{1... | collective-permute-start | bytes 417800 | tf_op jit(solution)/shard_map/ppermute | solution.py:31
  43.3 7.2 %collective-permute-start.3 = (bf16[136,512]{1,0:T(8,128)(2,1)S(1)}, bf16[136,512]{1,0:T(8,128)(2,1)S(1)}, u32[]{:S(2)}, u32[]{:S(2)}) collective-permute-start(bf16[136,512]{1,0:T(8,128)(2,1)S(1)} %get-tuple-element.42), channel_id=1, source_target_pairs={{0,8},{4,12},{8,0},{12,4},{1,9},{5,13},{9,1},{13,5},{2,10},{6,14},... | collective-permute-start | bytes 417800 | tf_op jit(solution)/shard_map/ppermute | solution.py:31
  46.9 9.2 %collective-permute-start.5 = (bf16[136,512]{1,0:T(8,128)(2,1)S(1)}, bf16[136,512]{1,0:T(8,128)(2,1)S(1)}, u32[]{:S(2)}, u32[]{:S(2)}) collective-permute-start(bf16[136,512]{1,0:T(8,128)(2,1)S(1)} %get-tuple-element.43), channel_id=1, source_target_pairs={{0,12},{4,8},{8,4},{12,0},{1,13},{5,9},{9,5},{13,1},{2,14},{6,10},... | collective-permute-start | bytes 417800 | tf_op jit(solution)/shard_map/ppermute | solution.py:31
  57.9 6.5 %collective-permute-start.11 = (bf16[4,4096]{1,0:T(4,128)(2,1)S(1)}, bf16[4,4096]{1,0:T(4,128)(2,1)S(1)}, u32[]{:S(2)}, u32[]{:S(2)}) collective-permute-start(bf16[4,4096]{1,0:T(4,128)(2,1)S(1)} %shard_map.115.refs_0_), channel_id=1, source_target_pairs={{0,3},{1,2},{2,1},{3,0},{4,7},{5,6},{6,5},{7,4},{8,11},{9,10},{10,... | collective-permute-start | bytes 98312 | tf_op jit(solution)/shard_map/ppermute | solution.py:31
  57.9 6.5 %collective-permute-start.10 = (bf16[4,4096]{1,0:T(4,128)(2,1)S(1)}, bf16[4,4096]{1,0:T(4,128)(2,1)S(1)}, u32[]{:S(2)}, u32[]{:S(2)}) collective-permute-start(bf16[4,4096]{1,0:T(4,128)(2,1)S(1)} %shard_map.115.refs_0_), channel_id=1, source_target_pairs={{0,2},{1,3},{2,0},{3,1},{4,6},{5,7},{6,4},{7,5},{8,10},{9,11},{10,... | collective-permute-start | bytes 98312 | tf_op jit(solution)/shard_map/ppermute | solution.py:31
  59.5 4.9 %collective-permute-start.9 = (bf16[4,4096]{1,0:T(4,128)(2,1)S(1)}, bf16[4,4096]{1,0:T(4,128)(2,1)S(1)}, u32[]{:S(2)}, u32[]{:S(2)}) collective-permute-start(bf16[4,4096]{1,0:T(4,128)(2,1)S(1)} %shard_map.115.refs_0_), channel_id=1, source_target_pairs={{0,1},{1,0},{2,3},{3,2},{4,5},{5,4},{6,7},{7,6},{8,9},{9,8},{10,11... | collective-permute-start | bytes 98312 | tf_op jit(solution)/shard_map/ppermute | solution.py:31
  64.4 11.6 %slice-start = ((s8[8257536]{0:T(1024)(128)(4,1)}), s8[4194304]{0:T(1024)(128)(4,1)S(1)}, s32[]{:S(2)}) async-start(s8[8257536]{0:T(1024)(128)(4,1)} %bitcast.1), calls=%async_computation | async-start | bytes 8388608
  64.5 11.6 %slice-start.1 = ((s8[8257536]{0:T(1024)(128)(4,1)}), s8[4063232]{0:T(1024)(128)(4,1)S(1)}, s32[]{:S(2)}) async-start(s8[8257536]{0:T(1024)(128)(4,1)} %bitcast.1), calls=%async_computation.1 | async-start | bytes 8126464
  66.5 6.0 %collective-permute-start.14 = (bf16[16,1792]{1,0:T(8,128)(2,1)S(1)}, bf16[16,1792]{1,0:T(8,128)(2,1)S(1)}, u32[]{:S(2)}, u32[]{:S(2)}) collective-permute-start(bf16[16,1792]{1,0:T(8,128)(2,1)S(1)} %shard_map.118.refs_0_), channel_id=1, source_target_pairs={{0,12},{4,8},{8,4},{12,0},{1,13},{5,9},{9,5},{13,1},{2,14},{6,10},... | collective-permute-start | bytes 172040 | tf_op jit(solution)/shard_map/ppermute | solution.py:31
  69.6 6.1 %collective-permute-start.13 = (bf16[16,1792]{1,0:T(8,128)(2,1)S(1)}, bf16[16,1792]{1,0:T(8,128)(2,1)S(1)}, u32[]{:S(2)}, u32[]{:S(2)}) collective-permute-start(bf16[16,1792]{1,0:T(8,128)(2,1)S(1)} %shard_map.118.refs_0_), channel_id=1, source_target_pairs={{0,8},{4,12},{8,0},{12,4},{1,9},{5,13},{9,1},{13,5},{2,10},{6,14},... | collective-permute-start | bytes 172040 | tf_op jit(solution)/shard_map/ppermute | solution.py:31
  71.1 5.0 %collective-permute-start.12 = (bf16[16,1792]{1,0:T(8,128)(2,1)S(1)}, bf16[16,1792]{1,0:T(8,128)(2,1)S(1)}, u32[]{:S(2)}, u32[]{:S(2)}) collective-permute-start(bf16[16,1792]{1,0:T(8,128)(2,1)S(1)} %shard_map.118.refs_0_), channel_id=1, source_target_pairs={{0,4},{4,0},{8,12},{12,8},{1,5},{5,1},{9,13},{13,9},{2,6},{6,2},{1... | collective-permute-start | bytes 172040 | tf_op jit(solution)/shard_map/ppermute | solution.py:31
  77.4 1.3 %collective-permute-start.15 = (bf16[16,2432]{1,0:T(8,128)(2,1)S(1)}, bf16[16,2432]{1,0:T(8,128)(2,1)S(1)}, u32[]{:S(2)}, u32[]{:S(2)}) collective-permute-start(bf16[16,2432]{1,0:T(8,128)(2,1)S(1)} %get-tuple-element.62), channel_id=1, source_target_pairs={{0,1},{1,0},{2,3},{3,2},{4,5},{5,4},{6,7},{7,6},{8,9},{9,8},{10,11... | collective-permute-start | bytes 233480 | tf_op jit(solution)/shard_map/ppermute | solution.py:31
  77.4 6.4 %slice-start.2 = ((s8[8257536]{0:T(1024)(128)(4,1)}), s8[4194304]{0:T(1024)(128)(4,1)S(1)}, s32[]{:S(2)}) async-start(s8[8257536]{0:T(1024)(128)(4,1)} %bitcast.3), calls=%async_computation.2 | async-start | bytes 8388608
  77.4 6.4 %slice-start.3 = ((s8[8257536]{0:T(1024)(128)(4,1)}), s8[4063232]{0:T(1024)(128)(4,1)S(1)}, s32[]{:S(2)}) async-start(s8[8257536]{0:T(1024)(128)(4,1)} %bitcast.3), calls=%async_computation.3 | async-start | bytes 8126464
  78.8 4.7 %collective-permute-start.16 = (bf16[16,2432]{1,0:T(8,128)(2,1)S(1)}, bf16[16,2432]{1,0:T(8,128)(2,1)S(1)}, u32[]{:S(2)}, u32[]{:S(2)}) collective-permute-start(bf16[16,2432]{1,0:T(8,128)(2,1)S(1)} %get-tuple-element.64), channel_id=1, source_target_pairs={{0,2},{2,0},{1,3},{3,1},{4,6},{6,4},{5,7},{7,5},{8,10},{10,8},{9,1... | collective-permute-start | bytes 233480 | tf_op jit(solution)/shard_map/ppermute | solution.py:31
  83.7 1.3 %collective-permute-start.17 = (bf16[16,1152]{1,0:T(8,128)(2,1)S(1)}, bf16[16,1152]{1,0:T(8,128)(2,1)S(1)}, u32[]{:S(2)}, u32[]{:S(2)}) collective-permute-start(bf16[16,1152]{1,0:T(8,128)(2,1)S(1)} %shard_map.122.own_ref), channel_id=1, source_target_pairs={{0,1},{1,0},{2,3},{3,2},{4,5},{5,4},{6,7},{7,6},{8,9},{9,8},{10,11... | collective-permute-start | bytes 110600 | tf_op jit(solution)/shard_map/ppermute | solution.py:31
  85.7 4.5 %collective-permute-start.18 = (bf16[4,1792]{1,0:T(4,128)(2,1)S(1)}, bf16[4,1792]{1,0:T(4,128)(2,1)S(1)}, u32[]{:S(2)}, u32[]{:S(2)}) collective-permute-start(bf16[4,1792]{1,0:T(4,128)(2,1)S(1)} %get-tuple-element.66), channel_id=1, source_target_pairs={{0,4},{4,0},{8,12},{12,8},{1,5},{5,1},{9,13},{13,9},{2,6},{6,2},{1... | collective-permute-start | bytes 43016 | tf_op jit(solution)/shard_map/ppermute | solution.py:31
  86.6 4.7 %collective-permute-start.19 = (bf16[4,1792]{1,0:T(4,128)(2,1)S(1)}, bf16[4,1792]{1,0:T(4,128)(2,1)S(1)}, u32[]{:S(2)}, u32[]{:S(2)}) collective-permute-start(bf16[4,1792]{1,0:T(4,128)(2,1)S(1)} %get-tuple-element.67), channel_id=1, source_target_pairs={{0,8},{4,12},{8,0},{12,4},{1,9},{5,13},{9,1},{13,5},{2,10},{6,14},... | collective-permute-start | bytes 43016 | tf_op jit(solution)/shard_map/ppermute | solution.py:31
  89.6 5.5 %collective-permute-start.20 = (bf16[4,1792]{1,0:T(4,128)(2,1)S(1)}, bf16[4,1792]{1,0:T(4,128)(2,1)S(1)}, u32[]{:S(2)}, u32[]{:S(2)}) collective-permute-start(bf16[4,1792]{1,0:T(4,128)(2,1)S(1)} %get-tuple-element.68), channel_id=1, source_target_pairs={{0,12},{4,8},{8,4},{12,0},{1,13},{5,9},{9,5},{13,1},{2,14},{6,10},... | collective-permute-start | bytes 43016 | tf_op jit(solution)/shard_map/ppermute | solution.py:31

commit v8 on v7

--- a/solution.py
+++ b/solution.py
@@ -516,13 +516,14 @@
     product = project_out(shared, [own_part, early_part, even_part, odd_part, last_part])
     up_weight, product = lax.optimization_barrier((up_weight, product))
     terms = listed(exchange([product] * blocks, "ctx"))
-    up_fast = up_weight
+    (up_fast,) = fetch([up_weight])
 
     send, scaled, squares, base = gate_and_up_away(terms, residual, gain, gate_fast, up_fast)
     got = xor_permute(send, "seq", 1)
     keep = gate_and_up_here(scaled, gate_fast, up_fast)
     keep, send = add_core(keep, squares, got)
-    down_fast = down_weight
+    down_weight, send = lax.optimization_barrier((down_weight, send))
+    (down_fast,) = fetch([down_weight])
     pieces = listed(exchange([send] * roles, "role"))[1:]
     features = norm_gain.shape[0] * members
     hidden = activate(keep, pieces, features)

time: 96 us -> 98.9 us (1.030)
  Pallas kernels: 23.6 us -> 30.3 us
  waiting for transfers between devices: 45.6 us -> 41.7 us
    pallas_call x17 -> x19, Pallas kernels: 23.6 us -> 30.3 us  [call(): pl.pallas_call(body, out_shape=outs, in_specs=specs, out_specs=jax.tree.m...]
    ppermute x21, waiting for transfers between devices: 45.6 us -> 41.7 us  [xor_permute(): return lax.ppermute(x, axis, [(i, i ^ mask) for i in range(size)])]
  transfers between devices with their start and end apart: 21 -> 21, of which waited for: 11 -> 9; matrix products, arithmetic and copies ran while one was open for 0% -> 0% of each run, Pallas kernels for 19% -> 25%
where the time goes in v8:
time: 98.9 us; the launch traced here: 98.6 us
  waiting for transfers between devices  41.7 us (42%)
  Pallas kernels  30.3 us (31%)
  starting transfers between devices  26.4 us (27%)
    ppermute x21, waiting for transfers between devices, xor_permute(): return lax.ppermute(x, axis, [(i, i ^ mask) for i in range(size)])  41.7 us
    pallas_call x19, Pallas kernels, call(): pl.pallas_call(body, out_shape=outs, in_specs=specs, out_specs=jax.tree.m...  30.3 us
    ppermute x21, starting transfers between devices, xor_permute(): return lax.ppermute(x, axis, [(i, i ^ mask) for i in range(size)])  26.4 us
  transfers between devices with their start and end apart: 21, of which 9 were waited for; matrix products, arithmetic and copies ran while one was open for 0% of the time, Pallas kernels for 25%

profile of v8, /device:TPU:0, one launch (start us, length us, event | category | flops | bytes accessed | tf_op | source)
XLA Modules:
  0.0 98.6 jit_solution(2685677890853925080)
XLA Ops:
  0.0 0.0 copy-start
  0.0 3.0 %collective-permute-start.7 = (bf16[32,128,128]{2,1,0:T(8,128)(2,1)}, bf16[32,128,128]{2,1,0:T(8,128)(2,1)S(1)}, u32[]{:S(2)}, u32[]{:S(2)}) collective-permute-start(bf16[32,128,128]{2,1,0:T(8,128)(2,1)} %refs_1_.1), channel_id=1, source_target_pairs={{0,2},{2,0},{1,3},{3,1},{4,6},{6,4},{5,7},{7,5},{8,10},{10,8},{9,1... | collective-permute-start | bytes 3145736 | tf_op jit(solution)/shard_map/ppermute | solution.py:31
  3.0 0.0 collective-permute-start.6
  3.0 3.8 %shard_map.113 = (bf16[1792,2304]{1,0:T(8,128)(2,1)S(1)}, bf16[32,128,128]{2,1,0:T(8,128)(2,1)S(1)}, bf16[16,1792]{1,0:T(8,128)(2,1)S(1)}, f32[1792]{0:T(1024)S(1)}) custom-call(bf16[1792,2304]{1,0:T(8,128)(2,1)} %refs_0_.4, bf16[32,128,128]{2,1,0:T(8,128)(2,1)} %refs_1_.1, bf16[16,1792]{1,0:T(8,128)(2,1)} %refs_2_.3, f32[1792]{0:T(1024)} %refs_3_.7), custom_call_target="tpu_custom_call" | custom-call | bytes 18741248 | tf_op jit(solution)/shard_map/pallas_call | solution.py:47
  6.7 19.6 %collective-permute-done.7.refs_0_ = bf16[32,128,128]{2,1,0:T(8,128)(2,1)S(1)} collective-permute-done((bf16[32,128,128]{2,1,0:T(8,128)(2,1)}, bf16[32,128,128]{2,1,0:T(8,128)(2,1)S(1)}, u32[]{:S(2)}, u32[]{:S(2)}) %collective-permute-start.7) | collective-permute-done | bytes 1048608 | tf_op jit(solution)/shard_map/ppermute | solution.py:31
  26.3 0.0 collective-permute-start.8
  26.3 0.0 copy-done
  26.3 2.8 %collective-permute-start = (bf16[4,32,576]{2,1,0:T(8,128)(2,1)S(1)}, bf16[4,32,576]{2,1,0:T(8,128)(2,1)S(1)}, u32[]{:S(2)}, u32[]{:S(2)}) collective-permute-start(bf16[4,32,576]{2,1,0:T(8,128)(2,1)S(1)} %copy-done), channel_id=1, source_target_pairs={{0,8},{4,12},{8,0},{12,4},{1,9},{5,13},{9,1},{13,5},{2,10},{6,14},... | collective-permute-start | bytes 442376 | tf_op jit(solution)/shard_map/ppermute | solution.py:31
  29.2 1.6 %collective-permute-start.1 = (bf16[4,32,576]{2,1,0:T(8,128)(2,1)S(1)}, bf16[4,32,576]{2,1,0:T(8,128)(2,1)S(1)}, u32[]{:S(2)}, u32[]{:S(2)}) collective-permute-start(bf16[4,32,576]{2,1,0:T(8,128)(2,1)S(1)} %copy-done), channel_id=1, source_target_pairs={{0,4},{4,0},{8,12},{12,8},{1,5},{5,1},{9,13},{13,9},{2,6},{6,2},{1... | collective-permute-start | bytes 442376 | tf_op jit(solution)/shard_map/ppermute | solution.py:31
  30.8 6.9 %collective-permute-done.refs_0_ = bf16[4,32,576]{2,1,0:T(8,128)(2,1)S(1)} collective-permute-done((bf16[4,32,576]{2,1,0:T(8,128)(2,1)S(1)}, bf16[4,32,576]{2,1,0:T(8,128)(2,1)S(1)}, u32[]{:S(2)}, u32[]{:S(2)}) %collective-permute-start) | collective-permute-done | bytes 147488 | tf_op jit(solution)/shard_map/ppermute | solution.py:31
  37.7 0.6 collective-permute-start.4
  38.3 1.7 %shard_map.109 = (bf16[4,32,576]{2,1,0:T(8,128)(2,1)S(1)}, bf16[2,576,1024]{2,1,0:T(8,128)(2,1)S(1)}, s32[4,128]{1,0:T(4,128)S(1)}) custom-call(bf16[4,32,576]{2,1,0:T(8,128)(2,1)} %refs_0_.3, bf16[2,576,1024]{2,1,0:T(8,128)(2,1)} %bitcast.1, s32[2]{0:T(128)} %refs_2_.2, s32[4]{0:T(128)} %refs_3_.4), custom_call_target="tpu_custom_call" | custom-call | bytes 5013504 | tf_op jit(solution)/shard_map/pallas_call | solution.py:47
  40.0 0.0 collective-permute-done.1.refs_1_
  40.0 1.8 %shard_map.111 = (bf16[136,512]{1,0:T(8,128)(2,1)S(1)}, bf16[136,512]{1,0:T(8,128)(2,1)S(1)}, bf16[512,1792]{1,0:T(8,128)(2,1)S(1)}) custom-call(bf16[4,32,576]{2,1,0:T(8,128)(2,1)S(1)} %collective-permute-done.refs_0_, bf16[4,32,576]{2,1,0:T(8,128)(2,1)S(1)} %collective-permute-done.1.refs_1_, bf16[2,576,1024]{2,1,0:T(8,128)(2,1)S(1)} %get-tuple-element.40.refs_1_.refs_2_, ...), custom_call_target="tpu_custom_call" | custom-call | flops 570425344 | bytes 4194304 | tf_op jit(solution)/shard_map/pallas_call | solution.py:47
  41.8 1.4 %collective-permute-start.2 = (bf16[136,512]{1,0:T(8,128)(2,1)S(1)}, bf16[136,512]{1,0:T(8,128)(2,1)S(1)}, u32[]{:S(2)}, u32[]{:S(2)}) collective-permute-start(bf16[136,512]{1,0:T(8,128)(2,1)S(1)} %get-tuple-element.43), channel_id=1, source_target_pairs={{0,4},{4,0},{8,12},{12,8},{1,5},{5,1},{9,13},{13,9},{2,6},{6,2},{1... | collective-permute-start | bytes 417800 | tf_op jit(solution)/shard_map/ppermute | solution.py:31
  43.3 2.1 %collective-permute-start.3 = (bf16[136,512]{1,0:T(8,128)(2,1)S(1)}, bf16[136,512]{1,0:T(8,128)(2,1)S(1)}, u32[]{:S(2)}, u32[]{:S(2)}) collective-permute-start(bf16[136,512]{1,0:T(8,128)(2,1)S(1)} %get-tuple-element.44), channel_id=1, source_target_pairs={{0,8},{4,12},{8,0},{12,4},{1,9},{5,13},{9,1},{13,5},{2,10},{6,14},... | collective-permute-start | bytes 417800 | tf_op jit(solution)/shard_map/ppermute | solution.py:31
  45.3 0.0 collective-permute-done.4.refs_0_
  45.3 1.6 %shard_map.112 = (bf16[136,512]{1,0:T(8,128)(2,1)S(1)}, bf16[512,1792]{1,0:T(8,128)(2,1)S(1)}) custom-call(bf16[4,32,576]{2,1,0:T(8,128)(2,1)S(1)} %collective-permute-done.4.refs_0_, bf16[2,576,1024]{2,1,0:T(8,128)(2,1)S(1)} %get-tuple-element.40.refs_1_.refs_2_, s32[4,128]{1,0:T(4,128)S(1)} %get-tuple-element.41.refs_2_.refs_3_, bf16[4096,1792]{1,0:T(8,128)(2,1)} %refs_0_.6), custom_call_target="tpu_custom_call" | custom-call | flops 285212672 | bytes 4194304 | tf_op jit(solution)/shard_map/pallas_call | solution.py:47
  46.9 2.0 %collective-permute-start.5 = (bf16[136,512]{1,0:T(8,128)(2,1)S(1)}, bf16[136,512]{1,0:T(8,128)(2,1)S(1)}, u32[]{:S(2)}, u32[]{:S(2)}) collective-permute-start(bf16[136,512]{1,0:T(8,128)(2,1)S(1)} %get-tuple-element.45), channel_id=1, source_target_pairs={{0,12},{4,8},{8,4},{12,0},{1,13},{5,9},{9,5},{13,1},{2,14},{6,10},... | collective-permute-start | bytes 417800 | tf_op jit(solution)/shard_map/ppermute | solution.py:31
  48.9 1.6 %shard_map.110 = (bf16[136,512]{1,0:T(8,128)(2,1)S(1)}, bf16[512,1792]{1,0:T(8,128)(2,1)S(1)}) custom-call(bf16[4,32,576]{2,1,0:T(8,128)(2,1)S(1)} %get-tuple-element.39.refs_0_, bf16[2,576,1024]{2,1,0:T(8,128)(2,1)S(1)} %get-tuple-element.40.refs_1_.refs_2_, s32[4,128]{1,0:T(4,128)S(1)} %get-tuple-element.41.refs_2_.refs_3_, bf16[4096,1792]{1,0:T(8,128)(2,1)} %refs_0_.6), custom_call_target="tpu_custom_call" | custom-call | flops 285212672 | bytes 4194304 | tf_op jit(solution)/shard_map/pallas_call | solution.py:47
  50.5 0.0 collective-permute-done.2.refs_1_
  50.5 0.0 collective-permute-done.3.refs_2_
  50.5 5.6 %collective-permute-done.5.refs_3_ = bf16[136,512]{1,0:T(8,128)(2,1)S(1)} collective-permute-done((bf16[136,512]{1,0:T(8,128)(2,1)S(1)}, bf16[136,512]{1,0:T(8,128)(2,1)S(1)}, u32[]{:S(2)}, u32[]{:S(2)}) %collective-permute-start.5) | collective-permute-done | bytes 139296 | tf_op jit(solution)/shard_map/ppermute | solution.py:31
  56.1 0.0 collective-permute-done.6.refs_5_
  56.1 1.1 %shard_map.114 = (f32[4,128,128]{2,1,0:T(8,128)S(1)}, f32[4,4096]{1,0:T(4,128)S(1)}) custom-call(bf16[136,512]{1,0:T(8,128)(2,1)S(1)} %get-tuple-element.42.refs_0_, bf16[136,512]{1,0:T(8,128)(2,1)S(1)} %collective-permute-done.2.refs_1_, bf16[136,512]{1,0:T(8,128)(2,1)S(1)} %collective-permute-done.3.refs_2_, ...), custom_call_target="tpu_custom_call" | custom-call | flops 8388608 | bytes 4194304 | tf_op jit(solution)/shard_map/pallas_call | solution.py:47
  57.2 0.0 collective-permute-done.8.refs_1_
  57.2 0.7 shard_map.115.refs_0_
  57.9 0.0 collective-permute-start.11
  57.9 1.6 %collective-permute-start.10 = (bf16[4,4096]{1,0:T(4,128)(2,1)S(1)}, bf16[4,4096]{1,0:T(4,128)(2,1)S(1)}, u32[]{:S(2)}, u32[]{:S(2)}) collective-permute-start(bf16[4,4096]{1,0:T(4,128)(2,1)S(1)} %shard_map.115.refs_0_), channel_id=1, source_target_pairs={{0,2},{1,3},{2,0},{3,1},{4,6},{5,7},{6,4},{7,5},{8,10},{9,11},{10,... | collective-permute-start | bytes 98312 | tf_op jit(solution)/shard_map/ppermute | solution.py:31
  59.5 0.3 collective-permute-start.9
  59.8 2.0 %shard_map.116.refs_5_ = bf16[1024,1792]{1,0:T(8,128)(2,1)S(1)} custom-call(bf16[4096,1792]{1,0:T(8,128)(2,1)} %refs_0_.6), custom_call_target="tpu_custom_call" | custom-call | bytes 7340032 | tf_op jit(solution)/shard_map/pallas_call | solution.py:47
  61.8 2.6 %shard_map.117.refs_8_ = bf16[1536,1792]{1,0:T(8,128)(2,1)S(1)} custom-call(bf16[4096,1792]{1,0:T(8,128)(2,1)} %refs_0_.6), custom_call_target="tpu_custom_call" | custom-call | bytes 11010048 | tf_op jit(solution)/shard_map/pallas_call | solution.py:47
  64.4 0.0 collective-permute-done.11.refs_3_
  64.4 0.0 collective-permute-done.10.refs_2_
  64.4 0.0 collective-permute-done.9.refs_1_
  64.4 2.0 %shard_map.118.refs_0_ = bf16[16,1792]{1,0:T(8,128)(2,1)S(1)} custom-call(bf16[4,4096]{1,0:T(4,128)(2,1)S(1)} %shard_map.115.refs_0_, bf16[4,4096]{1,0:T(4,128)(2,1)S(1)} %collective-permute-done.9.refs_1_, bf16[4,4096]{1,0:T(4,128)(2,1)S(1)} %collective-permute-done.10.refs_2_, bf16[4,4096]{1,0:T(4,128)(2,1)S(1)} %collective-permute-done.11.refs_3_, ...), custom_call_target="tpu_custom_call" | custom-call | flops 234881024 | bytes 4194304 | tf_op jit(solution)/shard_map/pallas_call | solution.py:47
  66.5 3.1 %collective-permute-start.14 = (bf16[16,1792]{1,0:T(8,128)(2,1)S(1)}, bf16[16,1792]{1,0:T(8,128)(2,1)S(1)}, u32[]{:S(2)}, u32[]{:S(2)}) collective-permute-start(bf16[16,1792]{1,0:T(8,128)(2,1)S(1)} %shard_map.118.refs_0_), channel_id=1, source_target_pairs={{0,12},{4,8},{8,4},{12,0},{1,13},{5,9},{9,5},{13,1},{2,14},{6,10},... | collective-permute-start | bytes 172040 | tf_op jit(solution)/shard_map/ppermute | solution.py:31
  69.6 1.5 %collective-permute-start.13 = (bf16[16,1792]{1,0:T(8,128)(2,1)S(1)}, bf16[16,1792]{1,0:T(8,128)(2,1)S(1)}, u32[]{:S(2)}, u32[]{:S(2)}) collective-permute-start(bf16[16,1792]{1,0:T(8,128)(2,1)S(1)} %shard_map.118.refs_0_), channel_id=1, source_target_pairs={{0,8},{4,12},{8,0},{12,4},{1,9},{5,13},{9,1},{13,5},{2,10},{6,14},... | collective-permute-start | bytes 172040 | tf_op jit(solution)/shard_map/ppermute | solution.py:31
  71.0 0.5 collective-permute-start.12
  71.6 3.4 %shard_map.119.refs_7_.up_ref = bf16[1792,2304]{1,0:T(8,128)(2,1)S(1)} custom-call(bf16[1792,2304]{1,0:T(8,128)(2,1)} %refs_0_.7), custom_call_target="tpu_custom_call" | custom-call | bytes 16515072 | tf_op jit(solution)/shard_map/pallas_call | solution.py:47
  74.9 0.0 collective-permute-done.14.refs_3_
  74.9 0.7 collective-permute-done.13.refs_2_
  75.6 0.4 collective-permute-done.12.refs_1_
  76.0 1.3 %shard_map.120 = (bf16[16,2432]{1,0:T(8,128)(2,1)S(1)}, bf16[16,1792]{1,0:T(8,128)(2,1)S(1)}, f32[16,128]{1,0:T(8,128)S(1)}, f32[4,1792]{1,0:T(4,128)S(1)}) custom-call(bf16[16,1792]{1,0:T(8,128)(2,1)S(1)} %shard_map.118.refs_0_, bf16[16,1792]{1,0:T(8,128)(2,1)S(1)} %collective-permute-done.12.refs_1_, bf16[16,1792]{1,0:T(8,128)(2,1)S(1)} %collective-permute-done.13.refs_2_, ...), custom_call_target="tpu_custom_call" | custom-call | flops 132120576 | bytes 4194304 | tf_op jit(solution)/shard_map/pallas_call | solution.py:47
  77.3 0.0 collective-permute-start.15
  77.4 1.2 %shard_map.121.keep_ref = f32[16,2304]{1,0:T(8,128)S(1)} custom-call(bf16[16,1792]{1,0:T(8,128)(2,1)S(1)} %get-tuple-element.62.scaled_ref, bf16[1792,2304]{1,0:T(8,128)(2,1)S(1)} %get-tuple-element.59.refs_6_.gate_ref, bf16[1792,2304]{1,0:T(8,128)(2,1)S(1)} %shard_map.119.refs_7_.up_ref), custom_call_target="tpu_custom_call" | custom-call | flops 132120576 | bytes 4194304 | tf_op jit(solution)/shard_map/pallas_call | solution.py:47
  78.5 0.1 collective-permute-done.15.got_ref
  78.6 0.2 shard_map.122
  78.8 1.3 %collective-permute-start.16 = (bf16[16,2432]{1,0:T(8,128)(2,1)S(1)}, bf16[16,2432]{1,0:T(8,128)(2,1)S(1)}, u32[]{:S(2)}, u32[]{:S(2)}) collective-permute-start(bf16[16,2432]{1,0:T(8,128)(2,1)S(1)} %get-tuple-element.67), channel_id=1, source_target_pairs={{0,2},{2,0},{1,3},{3,1},{4,6},{6,4},{5,7},{7,5},{8,10},{10,8},{9,1... | collective-permute-start | bytes 233480 | tf_op jit(solution)/shard_map/ppermute | solution.py:31
  80.1 3.4 %collective-permute-done.16.refs_1_ = bf16[16,2432]{1,0:T(8,128)(2,1)S(1)} collective-permute-done((bf16[16,2432]{1,0:T(8,128)(2,1)S(1)}, bf16[16,2432]{1,0:T(8,128)(2,1)S(1)}, u32[]{:S(2)}, u32[]{:S(2)}) %collective-permute-start.16) | collective-permute-done | bytes 77856 | tf_op jit(solution)/shard_map/ppermute | solution.py:31
  83.5 0.2 shard_map.123.own_ref
  83.7 0.1 collective-permute-start.17
  83.8 3.4 %shard_map.124.weight_ref = bf16[2304,1792]{1,0:T(8,128)(2,1)S(1)} custom-call(bf16[2304,1792]{1,0:T(8,128)(2,1)} %refs_0_.8), custom_call_target="tpu_custom_call" | custom-call | bytes 16515072 | tf_op jit(solution)/shard_map/pallas_call | solution.py:47
  87.1 0.7 shard_map.125.partial_ref
  87.8 0.0 collective-permute-done.17.other_ref
  87.8 0.7 shard_map.126
  88.5 0.9 collective-permute-start.18
  89.4 3.1 %collective-permute-start.19 = (bf16[4,1792]{1,0:T(4,128)(2,1)S(1)}, bf16[4,1792]{1,0:T(4,128)(2,1)S(1)}, u32[]{:S(2)}, u32[]{:S(2)}) collective-permute-start(bf16[4,1792]{1,0:T(4,128)(2,1)S(1)} %get-tuple-element.71), channel_id=1, source_target_pairs={{0,8},{4,12},{8,0},{12,4},{1,9},{5,13},{9,1},{13,5},{2,10},{6,14},... | collective-permute-start | bytes 43016 | tf_op jit(solution)/shard_map/ppermute | solution.py:31
  92.4 0.5 collective-permute-start.20
  93.0 0.0 collective-permute-done.18.refs_2_
  93.0 1.2 %collective-permute-done.19.refs_3_ = bf16[4,1792]{1,0:T(4,128)(2,1)S(1)} collective-permute-done((bf16[4,1792]{1,0:T(4,128)(2,1)S(1)}, bf16[4,1792]{1,0:T(4,128)(2,1)S(1)}, u32[]{:S(2)}, u32[]{:S(2)}) %collective-permute-start.19) | collective-permute-done | bytes 14368 | tf_op jit(solution)/shard_map/ppermute | solution.py:31
  94.1 3.8 %collective-permute-done.20.refs_4_ = bf16[4,1792]{1,0:T(4,128)(2,1)S(1)} collective-permute-done((bf16[4,1792]{1,0:T(4,128)(2,1)S(1)}, bf16[4,1792]{1,0:T(4,128)(2,1)S(1)}, u32[]{:S(2)}, u32[]{:S(2)}) %collective-permute-start.20) | collective-permute-done | bytes 14368 | tf_op jit(solution)/shard_map/ppermute | solution.py:31
  98.0 0.6 shard_map.127
Async XLA Ops:
  0.0 26.3 %copy-start = (bf16[4,32,576]{2,1,0:T(8,128)(2,1)S(1)}, bf16[4,32,576]{2,1,0:T(8,128)(2,1)}, u32[]{:S(2)}) copy-start(bf16[4,32,576]{2,1,0:T(8,128)(2,1)} %refs_0_.3) | copy-start | bytes 442372
  0.0 26.3 %collective-permute-start.7 = (bf16[32,128,128]{2,1,0:T(8,128)(2,1)}, bf16[32,128,128]{2,1,0:T(8,128)(2,1)S(1)}, u32[]{:S(2)}, u32[]{:S(2)}) collective-permute-start(bf16[32,128,128]{2,1,0:T(8,128)(2,1)} %refs_1_.1), channel_id=1, source_target_pairs={{0,2},{2,0},{1,3},{3,1},{4,6},{6,4},{5,7},{7,5},{8,10},{10,8},{9,1... | collective-permute-start | bytes 3145736 | tf_op jit(solution)/shard_map/ppermute | solution.py:31
  3.0 53.1 %collective-permute-start.6 = (bf16[32,128,128]{2,1,0:T(8,128)(2,1)}, bf16[32,128,128]{2,1,0:T(8,128)(2,1)S(1)}, u32[]{:S(2)}, u32[]{:S(2)}) collective-permute-start(bf16[32,128,128]{2,1,0:T(8,128)(2,1)} %refs_1_.1), channel_id=1, source_target_pairs={{0,1},{1,0},{2,3},{3,2},{4,5},{5,4},{6,7},{7,6},{8,9},{9,8},{10,11... | collective-permute-start | bytes 3145736 | tf_op jit(solution)/shard_map/ppermute | solution.py:31
  26.3 30.9 %collective-permute-start.8 = (bf16[32,128,128]{2,1,0:T(8,128)(2,1)S(1)}, bf16[32,128,128]{2,1,0:T(8,128)(2,1)S(1)}, u32[]{:S(2)}, u32[]{:S(2)}) collective-permute-start(bf16[32,128,128]{2,1,0:T(8,128)(2,1)S(1)} %collective-permute-done.7.refs_0_), channel_id=1, source_target_pairs={{0,1},{1,0},{2,3},{3,2},{4,5},{5,4},{6,7},{7,6},{8,9},{9,8},{10,11... | collective-permute-start | bytes 3145736 | tf_op jit(solution)/shard_map/ppermute | solution.py:31
  26.3 11.3 %collective-permute-start = (bf16[4,32,576]{2,1,0:T(8,128)(2,1)S(1)}, bf16[4,32,576]{2,1,0:T(8,128)(2,1)S(1)}, u32[]{:S(2)}, u32[]{:S(2)}) collective-permute-start(bf16[4,32,576]{2,1,0:T(8,128)(2,1)S(1)} %copy-done), channel_id=1, source_target_pairs={{0,8},{4,12},{8,0},{12,4},{1,9},{5,13},{9,1},{13,5},{2,10},{6,14},... | collective-permute-start | bytes 442376 | tf_op jit(solution)/shard_map/ppermute | solution.py:31
  29.2 10.8 %collective-permute-start.1 = (bf16[4,32,576]{2,1,0:T(8,128)(2,1)S(1)}, bf16[4,32,576]{2,1,0:T(8,128)(2,1)S(1)}, u32[]{:S(2)}, u32[]{:S(2)}) collective-permute-start(bf16[4,32,576]{2,1,0:T(8,128)(2,1)S(1)} %copy-done), channel_id=1, source_target_pairs={{0,4},{4,0},{8,12},{12,8},{1,5},{5,1},{9,13},{13,9},{2,6},{6,2},{1... | collective-permute-start | bytes 442376 | tf_op jit(solution)/shard_map/ppermute | solution.py:31
  37.7 7.7 %collective-permute-start.4 = (bf16[4,32,576]{2,1,0:T(8,128)(2,1)S(1)}, bf16[4,32,576]{2,1,0:T(8,128)(2,1)S(1)}, u32[]{:S(2)}, u32[]{:S(2)}) collective-permute-start(bf16[4,32,576]{2,1,0:T(8,128)(2,1)S(1)} %collective-permute-done.refs_0_), channel_id=1, source_target_pairs={{0,4},{4,0},{8,12},{12,8},{1,5},{5,1},{9,13},{13,9},{2,6},{6,2},{1... | collective-permute-start | bytes 442376 | tf_op jit(solution)/shard_map/ppermute | solution.py:31
  41.8 8.7 %collective-permute-start.2 = (bf16[136,512]{1,0:T(8,128)(2,1)S(1)}, bf16[136,512]{1,0:T(8,128)(2,1)S(1)}, u32[]{:S(2)}, u32[]{:S(2)}) collective-permute-start(bf16[136,512]{1,0:T(8,128)(2,1)S(1)} %get-tuple-element.43), channel_id=1, source_target_pairs={{0,4},{4,0},{8,12},{12,8},{1,5},{5,1},{9,13},{13,9},{2,6},{6,2},{1... | collective-permute-start | bytes 417800 | tf_op jit(solution)/shard_map/ppermute | solution.py:31
  43.3 7.2 %collective-permute-start.3 = (bf16[136,512]{1,0:T(8,128)(2,1)S(1)}, bf16[136,512]{1,0:T(8,128)(2,1)S(1)}, u32[]{:S(2)}, u32[]{:S(2)}) collective-permute-start(bf16[136,512]{1,0:T(8,128)(2,1)S(1)} %get-tuple-element.44), channel_id=1, source_target_pairs={{0,8},{4,12},{8,0},{12,4},{1,9},{5,13},{9,1},{13,5},{2,10},{6,14},... | collective-permute-start | bytes 417800 | tf_op jit(solution)/shard_map/ppermute | solution.py:31
  46.9 9.2 %collective-permute-start.5 = (bf16[136,512]{1,0:T(8,128)(2,1)S(1)}, bf16[136,512]{1,0:T(8,128)(2,1)S(1)}, u32[]{:S(2)}, u32[]{:S(2)}) collective-permute-start(bf16[136,512]{1,0:T(8,128)(2,1)S(1)} %get-tuple-element.45), channel_id=1, source_target_pairs={{0,12},{4,8},{8,4},{12,0},{1,13},{5,9},{9,5},{13,1},{2,14},{6,10},... | collective-permute-start | bytes 417800 | tf_op jit(solution)/shard_map/ppermute | solution.py:31
  57.9 6.5 %collective-permute-start.11 = (bf16[4,4096]{1,0:T(4,128)(2,1)S(1)}, bf16[4,4096]{1,0:T(4,128)(2,1)S(1)}, u32[]{:S(2)}, u32[]{:S(2)}) collective-permute-start(bf16[4,4096]{1,0:T(4,128)(2,1)S(1)} %shard_map.115.refs_0_), channel_id=1, source_target_pairs={{0,3},{1,2},{2,1},{3,0},{4,7},{5,6},{6,5},{7,4},{8,11},{9,10},{10,... | collective-permute-start | bytes 98312 | tf_op jit(solution)/shard_map/ppermute | solution.py:31
  57.9 6.5 %collective-permute-start.10 = (bf16[4,4096]{1,0:T(4,128)(2,1)S(1)}, bf16[4,4096]{1,0:T(4,128)(2,1)S(1)}, u32[]{:S(2)}, u32[]{:S(2)}) collective-permute-start(bf16[4,4096]{1,0:T(4,128)(2,1)S(1)} %shard_map.115.refs_0_), channel_id=1, source_target_pairs={{0,2},{1,3},{2,0},{3,1},{4,6},{5,7},{6,4},{7,5},{8,10},{9,11},{10,... | collective-permute-start | bytes 98312 | tf_op jit(solution)/shard_map/ppermute | solution.py:31
  59.5 4.9 %collective-permute-start.9 = (bf16[4,4096]{1,0:T(4,128)(2,1)S(1)}, bf16[4,4096]{1,0:T(4,128)(2,1)S(1)}, u32[]{:S(2)}, u32[]{:S(2)}) collective-permute-start(bf16[4,4096]{1,0:T(4,128)(2,1)S(1)} %shard_map.115.refs_0_), channel_id=1, source_target_pairs={{0,1},{1,0},{2,3},{3,2},{4,5},{5,4},{6,7},{7,6},{8,9},{9,8},{10,11... | collective-permute-start | bytes 98312 | tf_op jit(solution)/shard_map/ppermute | solution.py:31
  66.5 8.5 %collective-permute-start.14 = (bf16[16,1792]{1,0:T(8,128)(2,1)S(1)}, bf16[16,1792]{1,0:T(8,128)(2,1)S(1)}, u32[]{:S(2)}, u32[]{:S(2)}) collective-permute-start(bf16[16,1792]{1,0:T(8,128)(2,1)S(1)} %shard_map.118.refs_0_), channel_id=1, source_target_pairs={{0,12},{4,8},{8,4},{12,0},{1,13},{5,9},{9,5},{13,1},{2,14},{6,10},... | collective-permute-start | bytes 172040 | tf_op jit(solution)/shard_map/ppermute | solution.py:31
  69.6 6.1 %collective-permute-start.13 = (bf16[16,1792]{1,0:T(8,128)(2,1)S(1)}, bf16[16,1792]{1,0:T(8,128)(2,1)S(1)}, u32[]{:S(2)}, u32[]{:S(2)}) collective-permute-start(bf16[16,1792]{1,0:T(8,128)(2,1)S(1)} %shard_map.118.refs_0_), channel_id=1, source_target_pairs={{0,8},{4,12},{8,0},{12,4},{1,9},{5,13},{9,1},{13,5},{2,10},{6,14},... | collective-permute-start | bytes 172040 | tf_op jit(solution)/shard_map/ppermute | solution.py:31
  71.0 5.0 %collective-permute-start.12 = (bf16[16,1792]{1,0:T(8,128)(2,1)S(1)}, bf16[16,1792]{1,0:T(8,128)(2,1)S(1)}, u32[]{:S(2)}, u32[]{:S(2)}) collective-permute-start(bf16[16,1792]{1,0:T(8,128)(2,1)S(1)} %shard_map.118.refs_0_), channel_id=1, source_target_pairs={{0,4},{4,0},{8,12},{12,8},{1,5},{5,1},{9,13},{13,9},{2,6},{6,2},{1... | collective-permute-start | bytes 172040 | tf_op jit(solution)/shard_map/ppermute | solution.py:31
  77.3 1.3 %collective-permute-start.15 = (bf16[16,2432]{1,0:T(8,128)(2,1)S(1)}, bf16[16,2432]{1,0:T(8,128)(2,1)S(1)}, u32[]{:S(2)}, u32[]{:S(2)}) collective-permute-start(bf16[16,2432]{1,0:T(8,128)(2,1)S(1)} %get-tuple-element.64), channel_id=1, source_target_pairs={{0,1},{1,0},{2,3},{3,2},{4,5},{5,4},{6,7},{7,6},{8,9},{9,8},{10,11... | collective-permute-start | bytes 233480 | tf_op jit(solution)/shard_map/ppermute | solution.py:31
  78.8 4.7 %collective-permute-start.16 = (bf16[16,2432]{1,0:T(8,128)(2,1)S(1)}, bf16[16,2432]{1,0:T(8,128)(2,1)S(1)}, u32[]{:S(2)}, u32[]{:S(2)}) collective-permute-start(bf16[16,2432]{1,0:T(8,128)(2,1)S(1)} %get-tuple-element.67), channel_id=1, source_target_pairs={{0,2},{2,0},{1,3},{3,1},{4,6},{6,4},{5,7},{7,5},{8,10},{10,8},{9,1... | collective-permute-start | bytes 233480 | tf_op jit(solution)/shard_map/ppermute | solution.py:31
  83.7 4.1 %collective-permute-start.17 = (bf16[16,1152]{1,0:T(8,128)(2,1)S(1)}, bf16[16,1152]{1,0:T(8,128)(2,1)S(1)}, u32[]{:S(2)}, u32[]{:S(2)}) collective-permute-start(bf16[16,1152]{1,0:T(8,128)(2,1)S(1)} %shard_map.123.own_ref), channel_id=1, source_target_pairs={{0,1},{1,0},{2,3},{3,2},{4,5},{5,4},{6,7},{7,6},{8,9},{9,8},{10,11... | collective-permute-start | bytes 110600 | tf_op jit(solution)/shard_map/ppermute | solution.py:31
  88.5 4.5 %collective-permute-start.18 = (bf16[4,1792]{1,0:T(4,128)(2,1)S(1)}, bf16[4,1792]{1,0:T(4,128)(2,1)S(1)}, u32[]{:S(2)}, u32[]{:S(2)}) collective-permute-start(bf16[4,1792]{1,0:T(4,128)(2,1)S(1)} %get-tuple-element.70), channel_id=1, source_target_pairs={{0,4},{4,0},{8,12},{12,8},{1,5},{5,1},{9,13},{13,9},{2,6},{6,2},{1... | collective-permute-start | bytes 43016 | tf_op jit(solution)/shard_map/ppermute | solution.py:31
  89.4 4.7 %collective-permute-start.19 = (bf16[4,1792]{1,0:T(4,128)(2,1)S(1)}, bf16[4,1792]{1,0:T(4,128)(2,1)S(1)}, u32[]{:S(2)}, u32[]{:S(2)}) collective-permute-start(bf16[4,1792]{1,0:T(4,128)(2,1)S(1)} %get-tuple-element.71), channel_id=1, source_target_pairs={{0,8},{4,12},{8,0},{12,4},{1,9},{5,13},{9,1},{13,5},{2,10},{6,14},... | collective-permute-start | bytes 43016 | tf_op jit(solution)/shard_map/ppermute | solution.py:31
  92.4 5.5 %collective-permute-start.20 = (bf16[4,1792]{1,0:T(4,128)(2,1)S(1)}, bf16[4,1792]{1,0:T(4,128)(2,1)S(1)}, u32[]{:S(2)}, u32[]{:S(2)}) collective-permute-start(bf16[4,1792]{1,0:T(4,128)(2,1)S(1)} %get-tuple-element.72), channel_id=1, source_target_pairs={{0,12},{4,8},{8,4},{12,0},{1,13},{5,9},{9,5},{13,1},{2,14},{6,10},... | collective-permute-start | bytes 43016 | tf_op jit(solution)/shard_map/ppermute | solution.py:31
